TPU v7x, 32 devices: a whole 2x2x4 slice. The times are simulated.
32 devices in a mesh: seg: 4 (over y, x), chan: 8 (over z, core).
Axes of the slice: x: 2, y: 2, z: 4, core: 2. Of those that a mesh axis runs over, the one named last changes fastest.
Arguments:
- record: bfloat16 [1280, 16384], P('chan', 'seg'), may hold values from -6 to 6
- valid: int32 [1280], P('chan'), may hold values 0 or 1
- pairs: int32 [2, 8], P(None, 'chan'), may hold values from 0 to 7
Outputs:
- cross: bfloat16 [2, 2, 200, 204800], P(None, None, 'seg', 'chan')
All inputs are finite; a program needn't handle non-finite values. No bound on the sum of `valid` on one device may be relied on, other than what follows from the above.
Results may differ from a plain program's by a relative error of at most 0.008.
Values may be sent and summed in bfloat16 or wider, within the bound.
A program may use at most 128 MiB of HBM per device.

v0:
```python
import math

import jax
import jax.numpy as jnp
from jax import lax
from jax.sharding import PartitionSpec as P

FREQS = 200
WIN = 1024
LOW_BIN = 24
STEPS = 2
BAND = 3
HOP = 512


def shifted(value, axis, steps):
    count = lax.axis_size(axis)
    initial, last = (max(0, -steps), min(count, count - steps))
    return lax.ppermute(value, axis, [(source, source + steps) for source in range(initial, last)])


def band_table():
    steps_k = jnp.arange(WIN, dtype=jnp.int32)
    bins = LOW_BIN + jnp.arange(FREQS, dtype=jnp.int32)
    phase = steps_k[:, None] * bins[None, :] % WIN
    angle = 2.0 * math.pi / WIN * phase.astype(jnp.float32)
    taper = 0.5 - 0.5 * jnp.cos(2.0 * math.pi / WIN * steps_k.astype(jnp.float32))
    factor = (8.0 / (3.0 * WIN)) ** 0.5
    cos_part = taper[:, None] * jnp.cos(angle) * factor
    sin_part = -taper[:, None] * jnp.sin(angle) * factor
    return jnp.stack([cos_part, sin_part], axis=1).astype(jnp.bfloat16)


def cross_gram(left, right, factor):

    def product(first, second):
        return jnp.einsum("wfi,wfj->fij", first, second, preferred_element_type=jnp.float32)

    real_part = product(left[:, 0], right[:, 0]) + product(left[:, 1], right[:, 1])
    imag_part = product(left[:, 1], right[:, 0]) - product(left[:, 0], right[:, 1])
    merged = jnp.stack([real_part, imag_part], axis=0) * factor
    return merged.reshape(2, merged.shape[1], merged.shape[2] * merged.shape[3]).astype(
        jnp.bfloat16
    )


def fetch_band(spectra):
    above = []
    below = []
    for reach_k in range(1, BAND + 1):
        above.append(shifted(spectra, "chan", -reach_k))
        below.append(shifted(spectra, "chan", reach_k))
    return below[::-1] + above


def per_device(record, valid, pairs):
    channels, seg_len = record.shape
    windows = seg_len // HOP
    samples = record.astype(jnp.float32)
    scale = jnp.sqrt(jnp.mean(samples * samples, axis=-1, keepdims=True) + 1e-05)
    normed = (samples / scale).astype(jnp.bfloat16)
    following = shifted(normed[:, :HOP], "seg", -1)
    extended = jnp.concatenate([normed, following], axis=1)
    frames = jnp.concatenate(
        [
            extended[:, :seg_len].reshape(channels, windows, HOP),
            extended[:, HOP:].reshape(channels, windows, HOP),
        ],
        axis=-1,
    )
    spec = jnp.einsum("cwk,kpf->wpfc", frames, band_table(), preferred_element_type=jnp.float32)
    usable = valid.astype(jnp.float32)
    spectra = (spec * usable[None, None, None, :]).astype(jnp.bfloat16)
    own = lax.all_to_all(spectra, "seg", split_axis=2, concat_axis=0, tiled=True)
    stacked = jnp.stack(fetch_band(own), axis=0)
    factor = 1.0 / math.sqrt(own.shape[0])
    block = lax.axis_index("chan")
    results = []
    for step in range(STEPS):
        offset = pairs[step, 0] - block
        position = offset + BAND - (offset > 0).astype(jnp.int32)
        partner = lax.dynamic_index_in_dim(stacked, position, 0, keepdims=False)
        results.append(cross_gram(own, partner, factor))
    return jnp.stack(results, axis=0)


def solution(mesh):
    in_specs = (P("chan", "seg"), P("chan"), P(None, "chan"))
    out_specs = P(None, None, "seg", "chan")
    return jax.shard_map(
        per_device, mesh=mesh, in_specs=in_specs, out_specs=out_specs, check_vma=False
    )
```

profile of v0, /device:TPU:1, one launch (start us, length us, event | category | flops | bytes accessed | tf_op | source)
XLA Modules:
  0.0 282.8 jit_solution(4957351050473922273)
XLA Ops:
  0.0 1.7 fusion.2
  1.7 1.6 fusion.3
  4.8 3.8 %multiply_convert_fusion.2 = (bf16[1024,1,200]{0,2,1:T(8,128)(2,1)S(1)}, bf16[1024,1,200]{0,2,1:T(8,128)(2,1)S(1)}) fusion(s32[200]{0:T(256)S(1)} %iota_add_fusion, f32[1024]{0:T(1024)S(1)} %get-tuple-element.11, f32[1024]{0:T(1024)S(1)} %get-tuple-element.12), kind=kLoop, calls=%fused_computation.47 | loop fusion | flops 4096000 | bytes 828192 | tf_op jit(solution)/shard_map/convert
  8.6 2.6 collective-permute-done
  11.4 1.6 fusion.7
  13.0 1.6 copy.16
  14.6 21.5 %all_to_all.18 = bf16[8,2,200,160]{3,0,1,2:T(8,128)(2,1)S(1)} all-to-all(bf16[8,2,200,160]{3,0,1,2:T(8,128)(2,1)S(1)} %copy.16), channel_id=1, replica_groups=mesh['seg'=4,'chan'=8] {'seg'}, dimensions={2} | all-to-all | bytes 2048000 | tf_op jit(solution)/shard_map/all_to_all | solution.py:74
  36.3 8.5 %collective-permute-start.1 = (bf16[32,2,50,160]{3,0,2,1:T(8,128)(2,1)S(1)}, bf16[32,2,50,160]{3,0,2,1:T(8,128)(2,1)}, u32[]{:S(2)}, u32[]{:S(2)}) collective-permute-start(bf16[32,2,50,160]{3,0,2,1:T(8,128)(2,1)S(1)} %bitcast.74), channel_id=1, source_target_pairs={{0,3},{1,4},{2,5},{3,6},{4,7},{8,11},{9,12},{10,13},{11,14},{12,15... | collective-permute-start | bytes 3072008 | tf_op jit(solution)/shard_map/ppermute | solution.py:19
  44.8 3.2 %collective-permute-start.2 = (bf16[32,2,50,160]{3,0,2,1:T(8,128)(2,1)S(1)}, bf16[32,2,50,160]{3,0,2,1:T(8,128)(2,1)}, u32[]{:S(2)}, u32[]{:S(2)}) collective-permute-start(bf16[32,2,50,160]{3,0,2,1:T(8,128)(2,1)S(1)} %bitcast.75), channel_id=1, source_target_pairs={{0,2},{1,3},{2,4},{3,5},{4,6},{5,7},{8,10},{9,11},{10,12},{11,13},... | collective-permute-start | bytes 3072008 | tf_op jit(solution)/shard_map/ppermute | solution.py:19
  48.0 1.9 collective-permute-start.3
  49.9 2.5 collective-permute-start.4
  55.7 23.6 %collective-permute-done.1 = bf16[32,2,50,160]{3,0,2,1:T(8,128)(2,1)} collective-permute-done((bf16[32,2,50,160]{3,0,2,1:T(8,128)(2,1)S(1)}, bf16[32,2,50,160]{3,0,2,1:T(8,128)(2,1)}, u32[]{:S(2)}, u32[]{:S(2)}) %collective-permute-start.1) | collective-permute-done | bytes 1024032 | tf_op jit(solution)/shard_map/ppermute | solution.py:19
  80.8 1.6 bitcast_dynamic-update-slice_fusion.5
  82.3 29.4 %collective-permute-done.2 = bf16[32,2,50,160]{3,0,2,1:T(8,128)(2,1)} collective-permute-done((bf16[32,2,50,160]{3,0,2,1:T(8,128)(2,1)S(1)}, bf16[32,2,50,160]{3,0,2,1:T(8,128)(2,1)}, u32[]{:S(2)}, u32[]{:S(2)}) %collective-permute-start.2) | collective-permute-done | bytes 1024032 | tf_op jit(solution)/shard_map/ppermute | solution.py:19
  113.3 16.0 %collective-permute-done.3 = bf16[32,2,50,160]{3,0,2,1:T(8,128)(2,1)S(1)} collective-permute-done((bf16[32,2,50,160]{3,0,2,1:T(8,128)(2,1)S(1)}, bf16[32,2,50,160]{3,0,2,1:T(8,128)(2,1)S(1)}, u32[]{:S(2)}, u32[]{:S(2)}) %collective-permute-start.3) | collective-permute-done | bytes 1024032 | tf_op jit(solution)/shard_map/ppermute | solution.py:19
  129.4 1.6 bitcast_dynamic-update-slice_fusion.2
  131.1 27.6 %collective-permute-done.6 = bf16[32,2,50,160]{3,0,2,1:T(8,128)(2,1)S(1)} collective-permute-done((bf16[32,2,50,160]{3,0,2,1:T(8,128)(2,1)S(1)}, bf16[32,2,50,160]{3,0,2,1:T(8,128)(2,1)S(1)}, u32[]{:S(2)}, u32[]{:S(2)}) %collective-permute-start.6) | collective-permute-done | bytes 1024032 | tf_op jit(solution)/shard_map/ppermute | solution.py:19
  160.5 4.5 %fusion.16 = f32[50,160,160]{2,1,0:T(8,128)} fusion(bf16[32,2,50,160]{3,0,2,1:T(8,128)(2,1)S(1)} %get-tuple-element.5, bf16[32,2,50,160]{3,0,2,1:T(8,128)(2,1)S(1)} %bitcast.81), kind=kOutput, calls=%fused_computation.51 | convolution fusion | flops 81920000 | bytes 6758400 | tf_op jit(solution)/shard_map/wfi,wfj->fij/dot_general | solution.py:37
  165.0 4.6 %fusion.19 = f32[50,160,160]{2,1,0:T(8,128)} fusion(bf16[32,2,50,160]{3,0,2,1:T(8,128)(2,1)S(1)} %get-tuple-element.6, bf16[32,2,50,160]{3,0,2,1:T(8,128)(2,1)S(1)} %bitcast.82), kind=kOutput, calls=%fused_computation.54 | convolution fusion | flops 81920000 | bytes 6758400 | tf_op jit(solution)/shard_map/wfi,wfj->fij/dot_general | solution.py:37
  169.5 4.6 %fusion.18 = f32[50,160,160]{2,1,0:T(8,128)} fusion(bf16[32,2,50,160]{3,0,2,1:T(8,128)(2,1)S(1)} %get-tuple-element.6, bf16[32,2,50,160]{3,0,2,1:T(8,128)(2,1)S(1)} %bitcast.83), kind=kOutput, calls=%fused_computation.53 | convolution fusion | flops 81920000 | bytes 6758400 | tf_op jit(solution)/shard_map/wfi,wfj->fij/dot_general | solution.py:37
  174.2 4.6 %convolution_add_fusion.1 = f32[50,160,160]{2,1,0:T(8,128)} fusion(f32[50,160,160]{2,1,0:T(8,128)S(1)} %fusion.17, bf16[32,2,50,160]{3,0,2,1:T(8,128)(2,1)S(1)} %get-tuple-element.5, bf16[32,2,50,160]{3,0,2,1:T(8,128)(2,1)S(1)} %bitcast.84), kind=kOutput, calls=%fused_computation.10 | convolution fusion | flops 83200000 | bytes 14950400 | tf_op jit(solution)/shard_map/wfi,wfj->fij/dot_general | solution.py:37
  178.7 10.4 %stack.58 = f32[1,1,50,25600]{3,2,1,0:T(8,128)} reshape(f32[50,160,160]{2,1,0:T(8,128)} %convolution_add_fusion.1) | data formatting | bytes 10240000 | tf_op jit(solution)/shard_map/stack | solution.py:41
  189.1 8.1 %convolution_subtract_fusion.1 = f32[50,160,160]{2,1,0:T(8,128)} fusion(f32[50,160,160]{2,1,0:T(8,128)} %fusion.16, bf16[32,2,50,160]{3,0,2,1:T(8,128)(2,1)} %copy-done, bf16[32,2,50,160]{3,0,2,1:T(8,128)(2,1)S(1)} %bitcast.85), kind=kOutput, calls=%fused_computation.9 | convolution fusion | flops 83200000 | bytes 14950400 | tf_op jit(solution)/shard_map/wfi,wfj->fij/dot_general | solution.py:37
  197.2 10.4 %stack.59 = f32[1,1,50,25600]{3,2,1,0:T(8,128)} reshape(f32[50,160,160]{2,1,0:T(8,128)} %convolution_subtract_fusion.1) | data formatting | bytes 10240000 | tf_op jit(solution)/shard_map/stack | solution.py:41
  207.6 7.9 %convolution_add_fusion = f32[50,160,160]{2,1,0:T(8,128)} fusion(f32[50,160,160]{2,1,0:T(8,128)} %fusion.19, bf16[32,2,50,160]{3,0,2,1:T(8,128)(2,1)S(1)} %get-tuple-element.6, bf16[32,2,50,160]{3,0,2,1:T(8,128)(2,1)S(1)} %bitcast.86), kind=kOutput, calls=%fused_computation.8 | convolution fusion | flops 83200000 | bytes 11878400 | tf_op jit(solution)/shard_map/wfi,wfj->fij/dot_general | solution.py:37
  215.5 10.4 %stack.61 = f32[1,1,50,25600]{3,2,1,0:T(8,128)} reshape(f32[50,160,160]{2,1,0:T(8,128)} %convolution_add_fusion) | data formatting | bytes 10240000 | tf_op jit(solution)/shard_map/stack | solution.py:41
  225.9 7.9 %convolution_subtract_fusion = f32[50,160,160]{2,1,0:T(8,128)} fusion(f32[50,160,160]{2,1,0:T(8,128)} %fusion.18, bf16[32,2,50,160]{3,0,2,1:T(8,128)(2,1)S(1)} %get-tuple-element.6, bf16[32,2,50,160]{3,0,2,1:T(8,128)(2,1)S(1)} %bitcast.87), kind=kOutput, calls=%fused_computation.7 | convolution fusion | flops 83200000 | bytes 11878400 | tf_op jit(solution)/shard_map/wfi,wfj->fij/dot_general | solution.py:37
  233.8 10.5 %stack.62 = f32[1,1,50,25600]{3,2,1,0:T(8,128)} reshape(f32[50,160,160]{2,1,0:T(8,128)} %convolution_subtract_fusion) | data formatting | bytes 10240000 | tf_op jit(solution)/shard_map/stack | solution.py:41
  244.3 7.9 %fusion = bf16[1,2,50,25600]{3,2,1,0:T(8,128)(2,1)} fusion(f32[1,1,50,25600]{3,2,1,0:T(8,128)} %stack.59, f32[1,1,50,25600]{3,2,1,0:T(8,128)} %stack.58), kind=kLoop, calls=%fused_computation.1 | loop fusion | flops 7680000 | bytes 15360000 | tf_op jit(solution)/shard_map/convert_element_type | solution.py:42
  252.2 6.1 %fusion.1 = bf16[1,2,50,25600]{3,2,1,0:T(8,128)(2,1)} fusion(f32[1,1,50,25600]{3,2,1,0:T(8,128)} %stack.62, f32[1,1,50,25600]{3,2,1,0:T(8,128)S(1)} %bitcast.89), kind=kLoop, calls=%fused_computation.3 | loop fusion | flops 7680000 | bytes 15360000 | tf_op jit(solution)/shard_map/convert_element_type | solution.py:42
  258.3 6.1 %pad_maximum_fusion = bf16[2,2,50,25600]{3,2,1,0:T(8,128)(2,1)S(1)} fusion(bf16[1,2,50,25600]{3,2,1,0:T(8,128)(2,1)} %fusion.1, bf16[1,2,50,25600]{3,2,1,0:T(8,128)(2,1)} %fusion), kind=kLoop, calls=%fused_computation.4 | loop fusion | flops 5120000 | bytes 20480000 | tf_op jit(solution)/shard_map/stack | solution.py:84
  264.4 18.4 %copy.19 = bf16[2,2,50,25600]{3,1,2,0:T(2,128)(2,1)} copy(bf16[2,2,50,25600]{3,2,1,0:T(8,128)(2,1)S(1)} %pad_maximum_fusion) | data formatting | bytes 20480000 | tf_op jit(solution)/shard_map/stack | solution.py:84
  (32 shorter events, 8.8 us)
Async XLA Ops:
  1.7 3.2 %copy-start.2 = (s32[160]{0:T(256)S(1)}, s32[160]{0:T(256)}, u32[]{:S(2)}) copy-start(s32[160]{0:T(256)} %param.4) | copy-start | bytes 1924
  3.4 7.9 %collective-permute-start = (bf16[160,512]{1,0:T(8,128)(2,1)S(1)}, bf16[160,512]{1,0:T(8,128)(2,1)S(1)}, u32[]{:S(2)}, u32[]{:S(2)}) collective-permute-start(bf16[160,512]{1,0:T(8,128)(2,1)S(1)} %slice.50), channel_id=1, source_target_pairs={{8,0},{16,8},{24,16},{9,1},{17,9},{25,17},{10,2},{18,10},{26,18},{... | collective-permute-start | bytes 491528 | tf_op jit(solution)/shard_map/ppermute | solution.py:19
  14.6 37.8 %copy-start.1 = (s32[2,1]{0,1:T(1,128)S(1)}, s32[2,1]{0,1:T(1,128)}, u32[]{:S(2)}) copy-start(s32[2,1]{0,1:T(1,128)} %param.5) | copy-start | bytes 28
  36.3 43.0 %collective-permute-start.1 = (bf16[32,2,50,160]{3,0,2,1:T(8,128)(2,1)S(1)}, bf16[32,2,50,160]{3,0,2,1:T(8,128)(2,1)}, u32[]{:S(2)}, u32[]{:S(2)}) collective-permute-start(bf16[32,2,50,160]{3,0,2,1:T(8,128)(2,1)S(1)} %bitcast.74), channel_id=1, source_target_pairs={{0,3},{1,4},{2,5},{3,6},{4,7},{8,11},{9,12},{10,13},{11,14},{12,15... | collective-permute-start | bytes 3072008 | tf_op jit(solution)/shard_map/ppermute | solution.py:19
  44.8 66.9 %collective-permute-start.2 = (bf16[32,2,50,160]{3,0,2,1:T(8,128)(2,1)S(1)}, bf16[32,2,50,160]{3,0,2,1:T(8,128)(2,1)}, u32[]{:S(2)}, u32[]{:S(2)}) collective-permute-start(bf16[32,2,50,160]{3,0,2,1:T(8,128)(2,1)S(1)} %bitcast.75), channel_id=1, source_target_pairs={{0,2},{1,3},{2,4},{3,5},{4,6},{5,7},{8,10},{9,11},{10,12},{11,13},... | collective-permute-start | bytes 3072008 | tf_op jit(solution)/shard_map/ppermute | solution.py:19
  48.0 81.3 %collective-permute-start.3 = (bf16[32,2,50,160]{3,0,2,1:T(8,128)(2,1)S(1)}, bf16[32,2,50,160]{3,0,2,1:T(8,128)(2,1)S(1)}, u32[]{:S(2)}, u32[]{:S(2)}) collective-permute-start(bf16[32,2,50,160]{3,0,2,1:T(8,128)(2,1)S(1)} %bitcast.76), channel_id=1, source_target_pairs={{0,1},{1,2},{2,3},{3,4},{4,5},{5,6},{6,7},{8,9},{9,10},{10,11},{11... | collective-permute-start | bytes 3072008 | tf_op jit(solution)/shard_map/ppermute | solution.py:19
  49.9 79.5 %collective-permute-start.4 = (bf16[32,2,50,160]{3,0,2,1:T(8,128)(2,1)S(1)}, bf16[32,2,50,160]{3,0,2,1:T(8,128)(2,1)}, u32[]{:S(2)}, u32[]{:S(2)}) collective-permute-start(bf16[32,2,50,160]{3,0,2,1:T(8,128)(2,1)S(1)} %bitcast.77), channel_id=1, source_target_pairs={{1,0},{2,1},{3,2},{4,3},{5,4},{6,5},{7,6},{9,8},{10,9},{11,10},{12... | collective-permute-start | bytes 3072008 | tf_op jit(solution)/shard_map/ppermute | solution.py:19
  54.4 76.6 %collective-permute-start.5 = (bf16[32,2,50,160]{3,0,2,1:T(8,128)(2,1)S(1)}, bf16[32,2,50,160]{3,0,2,1:T(8,128)(2,1)S(1)}, u32[]{:S(2)}, u32[]{:S(2)}) collective-permute-start(bf16[32,2,50,160]{3,0,2,1:T(8,128)(2,1)S(1)} %bitcast.78), channel_id=1, source_target_pairs={{2,0},{3,1},{4,2},{5,3},{6,4},{7,5},{10,8},{11,9},{12,10},{13,11},... | collective-permute-start | bytes 3072008 | tf_op jit(solution)/shard_map/ppermute | solution.py:19
  79.3 79.4 %collective-permute-start.6 = (bf16[32,2,50,160]{3,0,2,1:T(8,128)(2,1)S(1)}, bf16[32,2,50,160]{3,0,2,1:T(8,128)(2,1)S(1)}, u32[]{:S(2)}, u32[]{:S(2)}) collective-permute-start(bf16[32,2,50,160]{3,0,2,1:T(8,128)(2,1)S(1)} %bitcast.79), channel_id=1, source_target_pairs={{3,0},{4,1},{5,2},{6,3},{7,4},{11,8},{12,9},{13,10},{14,11},{15,12... | collective-permute-start | bytes 3072008 | tf_op jit(solution)/shard_map/ppermute | solution.py:19
  159.2 14.9 %copy-start = (bf16[32,2,50,160]{3,0,2,1:T(8,128)(2,1)}, bf16[32,2,50,160]{3,0,2,1:T(8,128)(2,1)S(1)}, u32[]{:S(2)}) copy-start(bf16[32,2,50,160]{3,0,2,1:T(8,128)(2,1)S(1)} %get-tuple-element.5) | copy-start | bytes 3072004
  233.8 18.4 %slice-start = ((s8[5734400]{0:T(1024)(128)(4,1)}), s8[1540096]{0:T(1024)(128)(4,1)S(1)}, s32[]{:S(2)}) async-start(s8[5734400]{0:T(1024)(128)(4,1)} %bitcast.88), calls=%async_computation.1 | async-start | bytes 3080192
  244.3 7.9 %slice-start.1 = ((s8[5734400]{0:T(1024)(128)(4,1)}), s8[4194304]{0:T(1024)(128)(4,1)S(1)}, s32[]{:S(2)}) async-start(s8[5734400]{0:T(1024)(128)(4,1)} %bitcast.88), calls=%async_computation.2 | async-start | bytes 8388608
where the time goes:
time: 284 us; the launch traced here: 283 us
  waiting for transfers between devices  99.2 us (35%)
  local copies, waits for them, and re-layouts  68.2 us (24%)
  matrix products  44.9 us (16%)
  other arithmetic  27.3 us (10%)
  blocking collectives  21.5 us (8%)
  starting transfers between devices  20.2 us (7%)
    ppermute x7, waiting for transfers between devices, shifted(): lax.ppermute(value, axis, [(source, source + steps) for source in range(i...  99.2 us
    dot_general x8, matrix products, product(): jnp.einsum('wfi,wfj->fij', first, second, preferred_element_type=jnp.floa...  43.4 us
    another operation x4, local copies, waits for them, and re-layouts, cross_gram(): merged = jnp.stack([real_part, imag_part], axis=0) * factor  41.7 us
    all_to_all x1, blocking collectives, per_device(): lax.all_to_all(spectra, 'seg', split_axis=2, concat_axis=0, tiled=True)  21.5 us
    ppermute x7, starting transfers between devices, shifted(): lax.ppermute(value, axis, [(source, source + steps) for source in range(i...  20.2 us
    another operation x1, local copies, waits for them, and re-layouts, per_device(): return jnp.stack(results, axis=0)  18.4 us
    convert_element_type x2, other arithmetic, cross_gram(): merged.reshape(2, merged.shape[1], merged.shape[2] * merged.shape[3])  14 us
    another operation x1, other arithmetic, per_device(): return jnp.stack(results, axis=0)  6.07 us
  transfers between devices with their start and end apart: 7, of which 5 were waited for; matrix products, arithmetic and copies ran while one was open for 3% of the time, Pallas kernels for 0%

commit v1 on v0

--- a/solution.py
+++ b/solution.py
@@ -1,8 +1,11 @@
+import functools
 import math
 
 import jax
 import jax.numpy as jnp
 from jax import lax
+from jax.experimental import pallas as pl
+from jax.experimental.pallas import tpu as pltpu
 from jax.sharding import PartitionSpec as P
 
 FREQS = 200
@@ -11,6 +14,8 @@
 STEPS = 2
 BAND = 3
 HOP = 512
+GROUP = 8
+LANES = 128
 
 
 def shifted(value, axis, steps):
@@ -31,17 +36,77 @@
     return jnp.stack([cos_part, sin_part], axis=1).astype(jnp.bfloat16)
 
 
-def cross_gram(left, right, factor):
+def gram_kernel(count, factor, sel_ref, own_ref, first_ref, second_ref, out_ref, low, high):
+    del sel_ref
+    group = pl.program_id(0)
+    rows, chans = own_ref.shape[1:]
+    half = rows // 2
+    tail = chans - LANES
 
-    def product(first, second):
-        return jnp.einsum("wfi,wfj->fij", first, second, preferred_element_type=jnp.float32)
+    def one_freq(f, carry):
+        left = own_ref[f]
+        for step, ref in enumerate((first_ref, second_ref)):
+            right = ref[0, f]
+            turned = jnp.concatenate([-right[half:], right[:half]], axis=0)
+            for part, operand in enumerate((right, turned)):
+                gram = lax.dot_general(
+                    left, operand, (((0,), (0,)), ((), ())), preferred_element_type=jnp.float32
+                )
+                gram = gram * factor
+                spot = 2 * step + part
+                low[spot, pl.ds(f, chans, stride=GROUP), :] = gram[:, :LANES]
+                rest = jnp.concatenate(
+                    [gram[:, LANES:], jnp.zeros((chans, LANES - tail), jnp.float32)], axis=1
+                )
+                high[spot, pl.ds(f, chans, stride=GROUP), :] = rest
+        return carry
 
-    real_part = product(left[:, 0], right[:, 0]) + product(left[:, 1], right[:, 1])
-    imag_part = product(left[:, 1], right[:, 0]) - product(left[:, 0], right[:, 1])
-    merged = jnp.stack([real_part, imag_part], axis=0) * factor
-    return merged.reshape(2, merged.shape[1], merged.shape[2] * merged.shape[3]).astype(
-        jnp.bfloat16
+    lax.fori_loop(0, jnp.minimum(GROUP, count - group * GROUP), one_freq, 0)
+    batch = LANES // math.gcd(chans, LANES)
+
+    def one_batch(a, carry):
+        for spot in range(2 * STEPS):
+            pieces = []
+            for r in range(batch):
+                at = pl.ds(pl.multiple_of((a * batch + r) * GROUP, GROUP), GROUP)
+                pieces.append(low[spot, at, :])
+                pieces.append(high[spot, at, :][:, :tail])
+            merged = jnp.concatenate(pieces, axis=1).astype(jnp.bfloat16)
+            width = batch * chans
+            out_ref[spot // 2, spot % 2, :, pl.ds(pl.multiple_of(a * width, LANES), width)] = merged
+        return carry
+
+    lax.fori_loop(0, chans // batch, one_batch, 0)
+
+
+def cross_stacks(own, stacked, chosen, factor):
+    freqs, rows, chans = own.shape
+    block = (1, GROUP, rows, chans)
+    grid_spec = pltpu.PrefetchScalarGridSpec(
+        num_scalar_prefetch=1,
+        grid=(pl.cdiv(freqs, GROUP),),
+        in_specs=[
+            pl.BlockSpec((GROUP, rows, chans), lambda g, sel: (g, 0, 0)),
+            pl.BlockSpec(block, lambda g, sel: (sel[0], g, 0, 0)),
+            pl.BlockSpec(block, lambda g, sel: (sel[1], g, 0, 0)),
+        ],
+        out_specs=pl.BlockSpec((STEPS, 2, GROUP, chans * chans), lambda g, sel: (0, 0, g, 0)),
+        scratch_shapes=[
+            pltpu.VMEM((2 * STEPS, chans * GROUP, LANES), jnp.float32),
+            pltpu.VMEM((2 * STEPS, chans * GROUP, LANES), jnp.float32),
+        ],
     )
+    return pl.pallas_call(
+        functools.partial(gram_kernel, freqs, factor),
+        grid_spec=grid_spec,
+        out_shape=jax.ShapeDtypeStruct((STEPS, 2, freqs, chans * chans), jnp.bfloat16),
+        compiler_params=pltpu.CompilerParams(vmem_limit_bytes=40 * 2**20),
+        cost_estimate=pl.CostEstimate(
+            flops=8 * STEPS * freqs * rows * chans * chans,
+            bytes_accessed=4 * STEPS * freqs * chans * chans,
+            transcendentals=0,
+        ),
+    )(chosen, own, stacked, stacked)
 
 
 def fetch_band(spectra):
@@ -71,17 +136,13 @@
     spec = jnp.einsum("cwk,kpf->wpfc", frames, band_table(), preferred_element_type=jnp.float32)
     usable = valid.astype(jnp.float32)
     spectra = (spec * usable[None, None, None, :]).astype(jnp.bfloat16)
-    own = lax.all_to_all(spectra, "seg", split_axis=2, concat_axis=0, tiled=True)
+    got = lax.all_to_all(spectra, "seg", split_axis=2, concat_axis=0, tiled=True)
+    total, _, freqs, _ = got.shape
+    own = got.transpose(2, 1, 0, 3).reshape(freqs, 2 * total, channels)
     stacked = jnp.stack(fetch_band(own), axis=0)
-    factor = 1.0 / math.sqrt(own.shape[0])
-    block = lax.axis_index("chan")
-    results = []
-    for step in range(STEPS):
-        offset = pairs[step, 0] - block
-        position = offset + BAND - (offset > 0).astype(jnp.int32)
-        partner = lax.dynamic_index_in_dim(stacked, position, 0, keepdims=False)
-        results.append(cross_gram(own, partner, factor))
-    return jnp.stack(results, axis=0)
+    offset = pairs[:, 0] - lax.axis_index("chan")
+    chosen = offset + BAND - (offset > 0).astype(jnp.int32)
+    return cross_stacks(own, stacked, chosen, 1.0 / math.sqrt(total))
 
 
 def solution(mesh):

time: 284 us -> 218 us (0.77)
  local copies, waits for them, and re-layouts: 68.2 us -> 21.7 us
  matrix products: 44.9 us -> 1.55 us
  Pallas kernels: 0 us -> 43.3 us
  other arithmetic: 27.3 us -> 7.23 us
  waiting for transfers between devices: 99.2 us -> 103 us
    another operation x5 -> x0, local copies, waits for them, and re-layouts: 60.1 us -> none  [the longest x4 41.7 us: cross_gram(): merged = jnp.stack([real_part, imag_part], axis=0) * factor]
    dot_general x8 -> x0, matrix products: 43.4 us -> none  [product(): jnp.einsum('wfi,wfj->fij', first, second, preferred_element_type=jnp.floa...]
    pallas_call x0 -> x1, Pallas kernels: none -> 43.3 us  [cross_stacks(): pl.pallas_call(functools.partial(gram_kernel, freqs, factor), grid_spec=g...]
    pallas_call x0 -> x1, local copies, waits for them, and re-layouts: none -> 15.6 us  [cross_stacks(): pl.pallas_call(functools.partial(gram_kernel, freqs, factor), grid_spec=g...]
    convert_element_type x2 -> x0, other arithmetic: 14 us -> none  [cross_gram(): merged.reshape(2, merged.shape[1], merged.shape[2] * merged.shape[3])]
    another operation x2 -> x1, other arithmetic: 9.84 us -> 3.78 us  [the longest x1 6.07 us: per_device(): return jnp.stack(results, axis=0)]
    ppermute x7, waiting for transfers between devices: 99.2 us -> 103 us  [shifted(): lax.ppermute(value, axis, [(source, source + steps) for source in range(i...]
where the time goes in v1:
time: 218 us
  waiting for transfers between devices  103 us (47%)
  Pallas kernels  43.3 us (20%)
  local copies, waits for them, and re-layouts  21.7 us (10%)
  blocking collectives  21.5 us (10%)
  starting transfers between devices  20 us (9%)
  other arithmetic  7.23 us (3%)
    ppermute x7, waiting for transfers between devices, shifted(): lax.ppermute(value, axis, [(source, source + steps) for source in range(i...  103 us
    pallas_call x1, Pallas kernels, cross_stacks(): pl.pallas_call(functools.partial(gram_kernel, freqs, factor), grid_spec=g...  43.3 us
    all_to_all x1, blocking collectives, per_device(): lax.all_to_all(spectra, 'seg', split_axis=2, concat_axis=0, tiled=True)  21.5 us
    ppermute x7, starting transfers between devices, shifted(): lax.ppermute(value, axis, [(source, source + steps) for source in range(i...  20 us
    pallas_call x1, local copies, waits for them, and re-layouts, cross_stacks(): pl.pallas_call(functools.partial(gram_kernel, freqs, factor), grid_spec=g...  15.6 us
  transfers between devices with their start and end apart: 7, of which 5 were waited for; matrix products, arithmetic and copies ran while one was open for 3% of the time, Pallas kernels for 0%

profile of v1, /device:TPU:1, one launch (start us, length us, event | category | flops | bytes accessed | tf_op | source)
XLA Modules:
  0.0 218.0 jit_solution(10739796748870681140)
XLA Ops:
  0.0 1.7 fusion
  1.7 1.6 fusion.1
  3.4 1.3 collective-permute-start
  4.7 0.1 copy.32
  4.9 3.8 %multiply_convert_fusion.2 = (bf16[1024,1,200]{0,2,1:T(8,128)(2,1)S(1)}, bf16[1024,1,200]{0,2,1:T(8,128)(2,1)S(1)}) fusion(s32[200]{0:T(256)S(1)} %iota_add_fusion, f32[1024]{0:T(1024)S(1)} %get-tuple-element.7, f32[1024]{0:T(1024)S(1)} %get-tuple-element.8), kind=kLoop, calls=%fused_computation.30 | loop fusion | flops 4096000 | bytes 828192 | tf_op jit(solution)/shard_map/convert
  8.6 2.6 %collective-permute-done = bf16[160,512]{1,0:T(8,128)(2,1)S(1)} collective-permute-done((bf16[160,512]{1,0:T(8,128)(2,1)S(1)}, bf16[160,512]{1,0:T(8,128)(2,1)S(1)}, u32[]{:S(2)}, u32[]{:S(2)}) %collective-permute-start) | collective-permute-done | bytes 163872 | tf_op jit(solution)/shard_map/ppermute | solution.py:24
  11.2 0.1 pad_maximum_fusion
  11.3 0.1 copy.31
  11.4 1.6 fusion.5
  13.0 1.6 copy.18
  14.6 21.5 %all_to_all.18 = bf16[8,2,200,160]{3,0,1,2:T(8,128)(2,1)S(1)} all-to-all(bf16[8,2,200,160]{3,0,1,2:T(8,128)(2,1)S(1)} %copy.18), channel_id=1, replica_groups=mesh['seg'=4,'chan'=8] {'seg'}, dimensions={2} | all-to-all | bytes 2048000 | tf_op jit(solution)/shard_map/all_to_all | solution.py:139
  36.1 0.2 copy.30
  36.3 0.2 copy.21
  36.5 8.5 %collective-permute-start.1 = (bf16[50,64,160]{2,1,0:T(8,128)(2,1)S(1)}, bf16[50,64,160]{2,1,0:T(8,128)(2,1)}, u32[]{:S(2)}, u32[]{:S(2)}) collective-permute-start(bf16[50,64,160]{2,1,0:T(8,128)(2,1)S(1)} %bitcast.45), channel_id=1, source_target_pairs={{0,3},{1,4},{2,5},{3,6},{4,7},{8,11},{9,12},{10,13},{11,14},{12,15... | collective-permute-start | bytes 3072008 | tf_op jit(solution)/shard_map/ppermute | solution.py:24
  45.0 3.2 %collective-permute-start.2 = (bf16[50,64,160]{2,1,0:T(8,128)(2,1)S(1)}, bf16[50,64,160]{2,1,0:T(8,128)(2,1)}, u32[]{:S(2)}, u32[]{:S(2)}) collective-permute-start(bf16[50,64,160]{2,1,0:T(8,128)(2,1)S(1)} %bitcast.46), channel_id=1, source_target_pairs={{0,2},{1,3},{2,4},{3,5},{4,6},{5,7},{8,10},{9,11},{10,12},{11,13},... | collective-permute-start | bytes 3072008 | tf_op jit(solution)/shard_map/ppermute | solution.py:24
  48.2 1.9 collective-permute-start.3
  50.1 2.5 %collective-permute-start.4 = (bf16[50,64,160]{2,1,0:T(8,128)(2,1)S(1)}, bf16[50,64,160]{2,1,0:T(8,128)(2,1)S(1)}, u32[]{:S(2)}, u32[]{:S(2)}) collective-permute-start(bf16[50,64,160]{2,1,0:T(8,128)(2,1)S(1)} %bitcast.48), channel_id=1, source_target_pairs={{1,0},{2,1},{3,2},{4,3},{5,4},{6,5},{7,6},{9,8},{10,9},{11,10},{12... | collective-permute-start | bytes 3072008 | tf_op jit(solution)/shard_map/ppermute | solution.py:24
  52.6 1.3 collective-permute-start.5
  53.9 25.5 %collective-permute-done.1 = bf16[50,64,160]{2,1,0:T(8,128)(2,1)} collective-permute-done((bf16[50,64,160]{2,1,0:T(8,128)(2,1)S(1)}, bf16[50,64,160]{2,1,0:T(8,128)(2,1)}, u32[]{:S(2)}, u32[]{:S(2)}) %collective-permute-start.1) | collective-permute-done | bytes 1024032 | tf_op jit(solution)/shard_map/ppermute | solution.py:24
  79.4 1.3 collective-permute-start.6
  80.7 1.6 bitcast_dynamic-update-slice_fusion.5
  82.3 29.5 %collective-permute-done.2 = bf16[50,64,160]{2,1,0:T(8,128)(2,1)} collective-permute-done((bf16[50,64,160]{2,1,0:T(8,128)(2,1)S(1)}, bf16[50,64,160]{2,1,0:T(8,128)(2,1)}, u32[]{:S(2)}, u32[]{:S(2)}) %collective-permute-start.2) | collective-permute-done | bytes 1024032 | tf_op jit(solution)/shard_map/ppermute | solution.py:24
  111.9 1.6 bitcast_dynamic-update-slice_fusion.4
  113.5 15.9 %collective-permute-done.3 = bf16[50,64,160]{2,1,0:T(8,128)(2,1)S(1)} collective-permute-done((bf16[50,64,160]{2,1,0:T(8,128)(2,1)S(1)}, bf16[50,64,160]{2,1,0:T(8,128)(2,1)S(1)}, u32[]{:S(2)}, u32[]{:S(2)}) %collective-permute-start.3) | collective-permute-done | bytes 1024032 | tf_op jit(solution)/shard_map/ppermute | solution.py:24
  129.4 0.1 bitcast_dynamic-update-slice_fusion.3
  129.5 0.0 collective-permute-done.4
  129.5 0.2 bitcast_dynamic-update-slice_fusion.2
  129.7 0.2 bitcast_dynamic-update-slice_fusion.1
  129.9 28.9 %collective-permute-done.6 = bf16[50,64,160]{2,1,0:T(8,128)(2,1)S(1)} collective-permute-done((bf16[50,64,160]{2,1,0:T(8,128)(2,1)S(1)}, bf16[50,64,160]{2,1,0:T(8,128)(2,1)S(1)}, u32[]{:S(2)}, u32[]{:S(2)}) %collective-permute-start.6) | collective-permute-done | bytes 1024032 | tf_op jit(solution)/shard_map/ppermute | solution.py:24
  158.9 0.2 bitcast_dynamic-update-slice_fusion.first_ref.second_ref
  159.1 43.3 %shard_map.37 = bf16[2,2,50,25600]{3,2,1,0:T(8,128)(2,1)} custom-call(s32[2]{0:T(128)S(1)} %fusion.16.sel_ref, bf16[50,64,160]{2,1,0:T(8,128)(2,1)S(1)} %bitcast.51, bf16[6,50,64,160]{3,2,1,0:T(8,128)(2,1)S(1)} %bitcast_dynamic-update-slice_fusion.first_ref.second_ref, bf16[6,50,64,160]{3,2,1,0:T(8,128)(2,1)S(1)} %bitcast_dynamic-update-slice_fusion.first_ref.second_ref), custom_call_target="tpu_custom_call" | custom-call | flops 1310720000 | bytes 10240000 | tf_op jit(solution)/shard_map/pallas_call | solution.py:99
  202.4 15.6 %copy.22 = bf16[2,2,50,25600]{3,1,2,0:T(2,128)(2,1)} copy(bf16[2,2,50,25600]{3,2,1,0:T(8,128)(2,1)} %shard_map.37) | data formatting | bytes 20480000 | tf_op jit(solution)/shard_map/pallas_call | solution.py:99
  (11 shorter events, 0.1 us)
Async XLA Ops:
  1.7 3.2 %copy-start = (s32[160]{0:T(256)S(1)}, s32[160]{0:T(256)}, u32[]{:S(2)}) copy-start(s32[160]{0:T(256)} %param.4) | copy-start | bytes 1924
  3.4 7.9 %collective-permute-start = (bf16[160,512]{1,0:T(8,128)(2,1)S(1)}, bf16[160,512]{1,0:T(8,128)(2,1)S(1)}, u32[]{:S(2)}, u32[]{:S(2)}) collective-permute-start(bf16[160,512]{1,0:T(8,128)(2,1)S(1)} %slice.8), channel_id=1, source_target_pairs={{8,0},{16,8},{24,16},{9,1},{17,9},{25,17},{10,2},{18,10},{26,18},{... | collective-permute-start | bytes 491528 | tf_op jit(solution)/shard_map/ppermute | solution.py:24
  36.1 16.5 %copy-start.1 = (s32[2,1]{0,1:T(1,128)S(1)}, s32[2,1]{0,1:T(1,128)}, u32[]{:S(2)}) copy-start(s32[2,1]{0,1:T(1,128)} %param.5) | copy-start | bytes 28
  36.5 43.0 %collective-permute-start.1 = (bf16[50,64,160]{2,1,0:T(8,128)(2,1)S(1)}, bf16[50,64,160]{2,1,0:T(8,128)(2,1)}, u32[]{:S(2)}, u32[]{:S(2)}) collective-permute-start(bf16[50,64,160]{2,1,0:T(8,128)(2,1)S(1)} %bitcast.45), channel_id=1, source_target_pairs={{0,3},{1,4},{2,5},{3,6},{4,7},{8,11},{9,12},{10,13},{11,14},{12,15... | collective-permute-start | bytes 3072008 | tf_op jit(solution)/shard_map/ppermute | solution.py:24
  45.0 66.9 %collective-permute-start.2 = (bf16[50,64,160]{2,1,0:T(8,128)(2,1)S(1)}, bf16[50,64,160]{2,1,0:T(8,128)(2,1)}, u32[]{:S(2)}, u32[]{:S(2)}) collective-permute-start(bf16[50,64,160]{2,1,0:T(8,128)(2,1)S(1)} %bitcast.46), channel_id=1, source_target_pairs={{0,2},{1,3},{2,4},{3,5},{4,6},{5,7},{8,10},{9,11},{10,12},{11,13},... | collective-permute-start | bytes 3072008 | tf_op jit(solution)/shard_map/ppermute | solution.py:24
  48.2 81.3 %collective-permute-start.3 = (bf16[50,64,160]{2,1,0:T(8,128)(2,1)S(1)}, bf16[50,64,160]{2,1,0:T(8,128)(2,1)S(1)}, u32[]{:S(2)}, u32[]{:S(2)}) collective-permute-start(bf16[50,64,160]{2,1,0:T(8,128)(2,1)S(1)} %bitcast.47), channel_id=1, source_target_pairs={{0,1},{1,2},{2,3},{3,4},{4,5},{5,6},{6,7},{8,9},{9,10},{10,11},{11... | collective-permute-start | bytes 3072008 | tf_op jit(solution)/shard_map/ppermute | solution.py:24
  50.1 79.5 %collective-permute-start.4 = (bf16[50,64,160]{2,1,0:T(8,128)(2,1)S(1)}, bf16[50,64,160]{2,1,0:T(8,128)(2,1)S(1)}, u32[]{:S(2)}, u32[]{:S(2)}) collective-permute-start(bf16[50,64,160]{2,1,0:T(8,128)(2,1)S(1)} %bitcast.48), channel_id=1, source_target_pairs={{1,0},{2,1},{3,2},{4,3},{5,4},{6,5},{7,6},{9,8},{10,9},{11,10},{12... | collective-permute-start | bytes 3072008 | tf_op jit(solution)/shard_map/ppermute | solution.py:24
  52.6 77.1 %collective-permute-start.5 = (bf16[50,64,160]{2,1,0:T(8,128)(2,1)S(1)}, bf16[50,64,160]{2,1,0:T(8,128)(2,1)S(1)}, u32[]{:S(2)}, u32[]{:S(2)}) collective-permute-start(bf16[50,64,160]{2,1,0:T(8,128)(2,1)S(1)} %bitcast.49), channel_id=1, source_target_pairs={{2,0},{3,1},{4,2},{5,3},{6,4},{7,5},{10,8},{11,9},{12,10},{13,11},... | collective-permute-start | bytes 3072008 | tf_op jit(solution)/shard_map/ppermute | solution.py:24
  79.4 79.4 %collective-permute-start.6 = (bf16[50,64,160]{2,1,0:T(8,128)(2,1)S(1)}, bf16[50,64,160]{2,1,0:T(8,128)(2,1)S(1)}, u32[]{:S(2)}, u32[]{:S(2)}) collective-permute-start(bf16[50,64,160]{2,1,0:T(8,128)(2,1)S(1)} %bitcast.50), channel_id=1, source_target_pairs={{3,0},{4,1},{5,2},{6,3},{7,4},{11,8},{12,9},{13,10},{14,11},{15,12... | collective-permute-start | bytes 3072008 | tf_op jit(solution)/shard_map/ppermute | solution.py:24

commit v2 on v1

--- a/solution.py
+++ b/solution.py
@@ -14,7 +14,6 @@
 STEPS = 2
 BAND = 3
 HOP = 512
-GROUP = 8
 LANES = 128
 
 
@@ -36,77 +35,76 @@
     return jnp.stack([cos_part, sin_part], axis=1).astype(jnp.bfloat16)
 
 
-def gram_kernel(count, factor, sel_ref, own_ref, first_ref, second_ref, out_ref, low, high):
+def gram_kernel(factor, sel_ref, own_ref, first_ref, second_ref, out_ref, *held):
     del sel_ref
-    group = pl.program_id(0)
-    rows, chans = own_ref.shape[1:]
-    half = rows // 2
-    tail = chans - LANES
+    group, rows, _ = own_ref.shape
+    chans = first_ref.shape[-1]
+    batch = LANES // math.gcd(chans, LANES)
+    reach = chans // batch
+    width = batch * chans // LANES
 
     def one_freq(f, carry):
         left = own_ref[f]
         for step, ref in enumerate((first_ref, second_ref)):
-            right = ref[0, f]
-            turned = jnp.concatenate([-right[half:], right[:half]], axis=0)
-            for part, operand in enumerate((right, turned)):
-                gram = lax.dot_general(
-                    left, operand, (((0,), (0,)), ((), ())), preferred_element_type=jnp.float32
-                )
-                gram = gram * factor
-                spot = 2 * step + part
-                low[spot, pl.ds(f, chans, stride=GROUP), :] = gram[:, :LANES]
-                rest = jnp.concatenate(
-                    [gram[:, LANES:], jnp.zeros((chans, LANES - tail), jnp.float32)], axis=1
-                )
-                high[spot, pl.ds(f, chans, stride=GROUP), :] = rest
+            grams = jnp.dot(left, ref[0, f], preferred_element_type=jnp.float32)
+            for part in range(2):
+                pieces = []
+                for r in range(batch):
+                    at = (part * batch + r) * reach
+                    pieces.append(grams[at : at + reach])
+                for m in range(width):
+                    parts = []
+                    for r in range(batch):
+                        low = max(m * LANES - r * chans, 0)
+                        high = min((m + 1) * LANES - r * chans, chans)
+                        if low < high:
+                            parts.append(pieces[r][:, low:high])
+                    line = parts[0] if len(parts) == 1 else jnp.concatenate(parts, axis=1)
+                    held[step][pl.ds(2 * m + part, reach, stride=2 * width), :] = line
+            out_ref[step, f] = (held[step][...] * factor).astype(jnp.bfloat16)
         return carry
 
-    lax.fori_loop(0, jnp.minimum(GROUP, count - group * GROUP), one_freq, 0)
+    lax.fori_loop(0, group, one_freq, 0)
+
+
+def gram_operand(own):
+    freqs, rows, chans = own.shape
+    half = rows // 2
     batch = LANES // math.gcd(chans, LANES)
-
-    def one_batch(a, carry):
-        for spot in range(2 * STEPS):
-            pieces = []
-            for r in range(batch):
-                at = pl.ds(pl.multiple_of((a * batch + r) * GROUP, GROUP), GROUP)
-                pieces.append(low[spot, at, :])
-                pieces.append(high[spot, at, :][:, :tail])
-            merged = jnp.concatenate(pieces, axis=1).astype(jnp.bfloat16)
-            width = batch * chans
-            out_ref[spot // 2, spot % 2, :, pl.ds(pl.multiple_of(a * width, LANES), width)] = merged
-        return carry
-
-    lax.fori_loop(0, chans // batch, one_batch, 0)
+    turned = jnp.concatenate([own[:, half:], -own[:, :half]], axis=1)
+    both = jnp.stack([own, turned], axis=1).reshape(freqs, 2, rows, chans // batch, batch)
+    return both.transpose(0, 1, 4, 3, 2).reshape(freqs, 2 * chans, rows)
 
 
 def cross_stacks(own, stacked, chosen, factor):
     freqs, rows, chans = own.shape
-    block = (1, GROUP, rows, chans)
+    lines = 2 * chans * chans // LANES
+    group = max(n for n in range(1, 9) if freqs % n == 0)
+    block = (1, group, rows, chans)
     grid_spec = pltpu.PrefetchScalarGridSpec(
         num_scalar_prefetch=1,
-        grid=(pl.cdiv(freqs, GROUP),),
+        grid=(freqs // group,),
         in_specs=[
-            pl.BlockSpec((GROUP, rows, chans), lambda g, sel: (g, 0, 0)),
+            pl.BlockSpec((group, 2 * chans, rows), lambda g, sel: (g, 0, 0)),
             pl.BlockSpec(block, lambda g, sel: (sel[0], g, 0, 0)),
             pl.BlockSpec(block, lambda g, sel: (sel[1], g, 0, 0)),
         ],
-        out_specs=pl.BlockSpec((STEPS, 2, GROUP, chans * chans), lambda g, sel: (0, 0, g, 0)),
-        scratch_shapes=[
-            pltpu.VMEM((2 * STEPS, chans * GROUP, LANES), jnp.float32),
-            pltpu.VMEM((2 * STEPS, chans * GROUP, LANES), jnp.float32),
-        ],
+        out_specs=pl.BlockSpec((STEPS, group, lines, LANES), lambda g, sel: (0, g, 0, 0)),
+        scratch_shapes=[pltpu.VMEM((lines, LANES), jnp.float32)] * STEPS,
     )
-    return pl.pallas_call(
-        functools.partial(gram_kernel, freqs, factor),
+    merged = pl.pallas_call(
+        functools.partial(gram_kernel, factor),
         grid_spec=grid_spec,
-        out_shape=jax.ShapeDtypeStruct((STEPS, 2, freqs, chans * chans), jnp.bfloat16),
-        compiler_params=pltpu.CompilerParams(vmem_limit_bytes=40 * 2**20),
+        out_shape=jax.ShapeDtypeStruct((STEPS, freqs, lines, LANES), jnp.bfloat16),
+        compiler_params=pltpu.CompilerParams(vmem_limit_bytes=24 * 2**20),
         cost_estimate=pl.CostEstimate(
             flops=8 * STEPS * freqs * rows * chans * chans,
             bytes_accessed=4 * STEPS * freqs * chans * chans,
             transcendentals=0,
         ),
-    )(chosen, own, stacked, stacked)
+    )(chosen, gram_operand(own), stacked, stacked)
+    merged = merged.reshape(STEPS, freqs, lines // 2, 2, LANES).transpose(0, 3, 1, 2, 4)
+    return merged.reshape(STEPS, 2, freqs, chans * chans)
 
 
 def fetch_band(spectra):

time: 218 us -> 181 us (0.83)
  waiting for transfers between devices: 103 us -> 70.3 us
  Pallas kernels: 43.3 us -> 19.9 us
  local copies, waits for them, and re-layouts: 21.7 us -> 31.3 us
  other arithmetic: 7.23 us -> 14.4 us
    ppermute x7, waiting for transfers between devices: 103 us -> 70.3 us  [shifted(): lax.ppermute(value, axis, [(source, source + steps) for source in range(i...]
    pallas_call x1, Pallas kernels: 43.3 us -> 19.9 us  [cross_stacks(): pl.pallas_call(functools.partial(gram_kernel, factor), grid_spec=grid_spe...]
    pallas_call x1 -> x0, local copies, waits for them, and re-layouts: 15.6 us -> none  [cross_stacks(): pl.pallas_call(functools.partial(gram_kernel, freqs, factor), grid_spec=g...]
    transpose x0 -> x1, local copies, waits for them, and re-layouts: none -> 8.02 us  [gram_operand(): return both.transpose(0, 1, 4, 3, 2).reshape(freqs, 2 * chans, rows)]
    transpose x1 -> x2, local copies, waits for them, and re-layouts: 0.17 us -> 5.78 us  [per_device(): own = got.transpose(2, 1, 0, 3).reshape(freqs, 2 * total, channels)]
    transpose x0 -> x1, other arithmetic: none -> 5.32 us  [gram_operand(): return both.transpose(0, 1, 4, 3, 2).reshape(freqs, 2 * chans, rows)]
    another operation x0 -> x1, local copies, waits for them, and re-layouts: none -> 4.65 us  [gram_operand(): jnp.stack([own, turned], axis=1)]
    unnamed x9 -> x11, local copies, waits for them, and re-layouts: 3.68 us -> 8.2 us
  transfers between devices with their start and end apart: 7 -> 7, of which waited for: 5 -> 4; matrix products, arithmetic and copies ran while one was open for 3% -> 22% of each run, Pallas kernels for 0% -> 0%
where the time goes in v2:
time: 181 us; the launch traced here: 180 us
  waiting for transfers between devices  70.3 us (39%)
  local copies, waits for them, and re-layouts  31.3 us (17%)
  blocking collectives  21.5 us (12%)
  starting transfers between devices  21.1 us (12%)
  Pallas kernels  19.9 us (11%)
  other arithmetic  14.4 us (8%)
    ppermute x7, waiting for transfers between devices, shifted(): lax.ppermute(value, axis, [(source, source + steps) for source in range(i...  70.3 us
    all_to_all x1, blocking collectives, per_device(): lax.all_to_all(spectra, 'seg', split_axis=2, concat_axis=0, tiled=True)  21.5 us
    ppermute x7, starting transfers between devices, shifted(): lax.ppermute(value, axis, [(source, source + steps) for source in range(i...  21.1 us
    pallas_call x1, Pallas kernels, cross_stacks(): pl.pallas_call(functools.partial(gram_kernel, factor), grid_spec=grid_spe...  19.9 us
    unnamed x11, local copies, waits for them, and re-layouts  8.2 us
    transpose x1, local copies, waits for them, and re-layouts, gram_operand(): return both.transpose(0, 1, 4, 3, 2).reshape(freqs, 2 * chans, rows)  8.02 us
    transpose x2, local copies, waits for them, and re-layouts, per_device(): own = got.transpose(2, 1, 0, 3).reshape(freqs, 2 * total, channels)  5.78 us
    transpose x1, other arithmetic, gram_operand(): return both.transpose(0, 1, 4, 3, 2).reshape(freqs, 2 * chans, rows)  5.32 us
  transfers between devices with their start and end apart: 7, of which 4 were waited for; matrix products, arithmetic and copies ran while one was open for 22% of the time, Pallas kernels for 0%

profile of v2, /device:TPU:1, one launch (start us, length us, event | category | flops | bytes accessed | tf_op | source)
XLA Modules:
  0.0 180.3 jit_solution(14409580603879895361)
XLA Ops:
  0.0 1.7 fusion
  1.7 1.6 fusion.1
  3.4 1.3 collective-permute-start
  4.8 3.8 %multiply_convert_fusion.2 = (bf16[1024,1,200]{0,2,1:T(8,128)(2,1)S(1)}, bf16[1024,1,200]{0,2,1:T(8,128)(2,1)S(1)}) fusion(s32[200]{0:T(256)S(1)} %iota_add_fusion, f32[1024]{0:T(1024)S(1)} %get-tuple-element.9, f32[1024]{0:T(1024)S(1)} %get-tuple-element.10), kind=kLoop, calls=%fused_computation.33 | loop fusion | flops 4096000 | bytes 828192 | tf_op jit(solution)/shard_map/convert
  8.6 2.6 %collective-permute-done = bf16[160,512]{1,0:T(8,128)(2,1)S(1)} collective-permute-done((bf16[160,512]{1,0:T(8,128)(2,1)S(1)}, bf16[160,512]{1,0:T(8,128)(2,1)S(1)}, u32[]{:S(2)}, u32[]{:S(2)}) %collective-permute-start) | collective-permute-done | bytes 163872 | tf_op jit(solution)/shard_map/ppermute | solution.py:23
  11.4 1.6 fusion.5
  13.0 1.6 copy.27
  14.6 21.5 %all_to_all.18 = bf16[8,2,200,160]{3,0,1,2:T(8,128)(2,1)S(1)} all-to-all(bf16[8,2,200,160]{3,0,1,2:T(8,128)(2,1)S(1)} %copy.27), channel_id=1, replica_groups=mesh['seg'=4,'chan'=8] {'seg'}, dimensions={2} | all-to-all | bytes 2048000 | tf_op jit(solution)/shard_map/all_to_all | solution.py:137
  36.1 0.2 copy.43
  36.3 1.4 copy.31
  37.7 8.5 %collective-permute-start.1 = (bf16[50,64,160]{2,1,0:T(8,128)(2,1)}, bf16[50,64,160]{2,1,0:T(8,128)(2,1)}, u32[]{:S(2)}, u32[]{:S(2)}) collective-permute-start(bf16[50,64,160]{2,1,0:T(8,128)(2,1)} %bitcast.12), channel_id=1, source_target_pairs={{0,3},{1,4},{2,5},{3,6},{4,7},{8,11},{9,12},{10,13},{11,14},{12,15... | collective-permute-start | bytes 3072008 | tf_op jit(solution)/shard_map/ppermute | solution.py:23
  46.2 3.3 %collective-permute-start.2 = (bf16[50,64,160]{2,1,0:T(8,128)(2,1)}, bf16[50,64,160]{2,1,0:T(8,128)(2,1)}, u32[]{:S(2)}, u32[]{:S(2)}) collective-permute-start(bf16[50,64,160]{2,1,0:T(8,128)(2,1)} %bitcast.12), channel_id=1, source_target_pairs={{0,2},{1,3},{2,4},{3,5},{4,6},{5,7},{8,10},{9,11},{10,12},{11,13},... | collective-permute-start | bytes 3072008 | tf_op jit(solution)/shard_map/ppermute | solution.py:23
  49.5 1.9 %collective-permute-start.3 = (bf16[50,64,160]{2,1,0:T(8,128)(2,1)}, bf16[50,64,160]{2,1,0:T(8,128)(2,1)}, u32[]{:S(2)}, u32[]{:S(2)}) collective-permute-start(bf16[50,64,160]{2,1,0:T(8,128)(2,1)} %bitcast.12), channel_id=1, source_target_pairs={{0,1},{1,2},{2,3},{3,4},{4,5},{5,6},{6,7},{8,9},{9,10},{10,11},{11... | collective-permute-start | bytes 3072008 | tf_op jit(solution)/shard_map/ppermute | solution.py:23
  51.4 3.6 %collective-permute-start.4 = (bf16[50,64,160]{2,1,0:T(8,128)(2,1)}, bf16[50,64,160]{2,1,0:T(8,128)(2,1)}, u32[]{:S(2)}, u32[]{:S(2)}) collective-permute-start(bf16[50,64,160]{2,1,0:T(8,128)(2,1)} %bitcast.12), channel_id=1, source_target_pairs={{1,0},{2,1},{3,2},{4,3},{5,4},{6,5},{7,6},{9,8},{10,9},{11,10},{12... | collective-permute-start | bytes 3072008 | tf_op jit(solution)/shard_map/ppermute | solution.py:23
  54.9 1.3 collective-permute-start.5
  56.2 1.5 fusion.18
  57.8 4.4 %copy.30 = bf16[50,2,32,160]{0,2,1,3:T(8,128)(2,1)} copy(bf16[50,2,32,160]{3,2,0,1:T(8,128)(2,1)S(1)} %bitcast.57) | data formatting | bytes 2048000 | tf_op jit(solution)/shard_map/transpose | solution.py:139
  62.2 0.4 pad_maximum_fusion
  62.6 2.5 %copy.32 = bf16[50,64,160]{1,2,0:T(8,128)(2,1)} copy(bf16[50,64,160]{2,1,0:T(8,128)(2,1)S(1)} %pad_maximum_fusion) | data formatting | bytes 2048000 | tf_op jit(solution)/shard_map/concatenate | solution.py:74
  65.1 4.7 %copy.33 = bf16[50,1,64,40,4]{0,2,4,3,1:T(8,128)(2,1)S(1)} copy(bf16[50,1,64,40,4]{2,4,3,0,1:T(4,128)(2,1)} %bitcast.60) | data formatting | bytes 2048000 | tf_op jit(solution)/shard_map/stack | solution.py:75
  69.7 5.3 %maximum_bitcast_fusion = bf16[50,2,4,40,64]{0,4,2,3,1:T(8,128)(2,1)} fusion(bf16[50,1,64,40,4]{0,2,4,3,1:T(8,128)(2,1)S(1)} %copy.33, bf16[50,1,64,40,4]{0,2,4,3,1:T(8,128)(2,1)} %bitcast.59), kind=kLoop, calls=%fused_computation | loop fusion | flops 1024000 | bytes 4096000 | tf_op jit(solution)/shard_map/transpose | solution.py:76
  75.0 8.0 %copy.34 = bf16[50,2,4,40,64]{4,3,2,1,0:T(8,128)(2,1)} copy(bf16[50,2,4,40,64]{0,4,2,3,1:T(8,128)(2,1)} %maximum_bitcast_fusion) | data formatting | bytes 4096000 | tf_op jit(solution)/shard_map/transpose | solution.py:76
  83.1 1.3 collective-permute-start.6
  84.4 1.6 bitcast_dynamic-update-slice_fusion.5
  86.0 27.4 %collective-permute-done.2 = bf16[50,64,160]{2,1,0:T(8,128)(2,1)} collective-permute-done((bf16[50,64,160]{2,1,0:T(8,128)(2,1)}, bf16[50,64,160]{2,1,0:T(8,128)(2,1)}, u32[]{:S(2)}, u32[]{:S(2)}) %collective-permute-start.2) | collective-permute-done | bytes 1024032 | tf_op jit(solution)/shard_map/ppermute | solution.py:23
  113.4 1.6 bitcast_dynamic-update-slice_fusion.4
  115.0 15.9 %collective-permute-done.3 = bf16[50,64,160]{2,1,0:T(8,128)(2,1)} collective-permute-done((bf16[50,64,160]{2,1,0:T(8,128)(2,1)}, bf16[50,64,160]{2,1,0:T(8,128)(2,1)}, u32[]{:S(2)}, u32[]{:S(2)}) %collective-permute-start.3) | collective-permute-done | bytes 1024032 | tf_op jit(solution)/shard_map/ppermute | solution.py:23
  130.9 1.6 bitcast_dynamic-update-slice_fusion.3
  132.6 1.6 bitcast_dynamic-update-slice_fusion.2
  134.2 1.8 bitcast_dynamic-update-slice_fusion.1
  136.0 24.3 %collective-permute-done.6 = bf16[50,64,160]{2,1,0:T(8,128)(2,1)S(1)} collective-permute-done((bf16[50,64,160]{2,1,0:T(8,128)(2,1)}, bf16[50,64,160]{2,1,0:T(8,128)(2,1)S(1)}, u32[]{:S(2)}, u32[]{:S(2)}) %collective-permute-start.6) | collective-permute-done | bytes 1024032 | tf_op jit(solution)/shard_map/ppermute | solution.py:23
  160.4 19.9 %shard_map.37 = bf16[2,50,400,128]{3,2,1,0:T(8,128)(2,1)} custom-call(s32[2]{0:T(128)S(1)} %fusion.16.sel_ref, bf16[50,320,64]{2,1,0:T(8,128)(2,1)S(1)} %bitcast.55, bf16[6,50,64,160]{3,2,1,0:T(8,128)(2,1)S(1)} %bitcast_dynamic-update-slice_fusion.first_ref.second_ref, bf16[6,50,64,160]{3,2,1,0:T(8,128)(2,1)S(1)} %bitcast_dynamic-update-slice_fusion.first_ref.second_ref), custom_call_target="tpu_custom_call" | custom-call | flops 1310720000 | bytes 10240000 | tf_op jit(solution)/shard_map/pallas_call | solution.py:95
  (19 shorter events, 0.5 us)
Async XLA Ops:
  1.7 3.2 %copy-start.1 = (s32[160]{0:T(256)S(1)}, s32[160]{0:T(256)}, u32[]{:S(2)}) copy-start(s32[160]{0:T(256)} %param.4) | copy-start | bytes 1924
  3.4 7.9 %collective-permute-start = (bf16[160,512]{1,0:T(8,128)(2,1)S(1)}, bf16[160,512]{1,0:T(8,128)(2,1)S(1)}, u32[]{:S(2)}, u32[]{:S(2)}) collective-permute-start(bf16[160,512]{1,0:T(8,128)(2,1)S(1)} %slice.16), channel_id=1, source_target_pairs={{8,0},{16,8},{24,16},{9,1},{17,9},{25,17},{10,2},{18,10},{26,18},{... | collective-permute-start | bytes 491528 | tf_op jit(solution)/shard_map/ppermute | solution.py:23
  36.1 13.4 %copy-start.2 = (s32[2,1]{0,1:T(1,128)S(1)}, s32[2,1]{0,1:T(1,128)}, u32[]{:S(2)}) copy-start(s32[2,1]{0,1:T(1,128)} %param.5) | copy-start | bytes 28
  37.7 45.4 %collective-permute-start.1 = (bf16[50,64,160]{2,1,0:T(8,128)(2,1)}, bf16[50,64,160]{2,1,0:T(8,128)(2,1)}, u32[]{:S(2)}, u32[]{:S(2)}) collective-permute-start(bf16[50,64,160]{2,1,0:T(8,128)(2,1)} %bitcast.12), channel_id=1, source_target_pairs={{0,3},{1,4},{2,5},{3,6},{4,7},{8,11},{9,12},{10,13},{11,14},{12,15... | collective-permute-start | bytes 3072008 | tf_op jit(solution)/shard_map/ppermute | solution.py:23
  46.2 67.2 %collective-permute-start.2 = (bf16[50,64,160]{2,1,0:T(8,128)(2,1)}, bf16[50,64,160]{2,1,0:T(8,128)(2,1)}, u32[]{:S(2)}, u32[]{:S(2)}) collective-permute-start(bf16[50,64,160]{2,1,0:T(8,128)(2,1)} %bitcast.12), channel_id=1, source_target_pairs={{0,2},{1,3},{2,4},{3,5},{4,6},{5,7},{8,10},{9,11},{10,12},{11,13},... | collective-permute-start | bytes 3072008 | tf_op jit(solution)/shard_map/ppermute | solution.py:23
  49.5 81.5 %collective-permute-start.3 = (bf16[50,64,160]{2,1,0:T(8,128)(2,1)}, bf16[50,64,160]{2,1,0:T(8,128)(2,1)}, u32[]{:S(2)}, u32[]{:S(2)}) collective-permute-start(bf16[50,64,160]{2,1,0:T(8,128)(2,1)} %bitcast.12), channel_id=1, source_target_pairs={{0,1},{1,2},{2,3},{3,4},{4,5},{5,6},{6,7},{8,9},{9,10},{10,11},{11... | collective-permute-start | bytes 3072008 | tf_op jit(solution)/shard_map/ppermute | solution.py:23
  51.4 81.2 %collective-permute-start.4 = (bf16[50,64,160]{2,1,0:T(8,128)(2,1)}, bf16[50,64,160]{2,1,0:T(8,128)(2,1)}, u32[]{:S(2)}, u32[]{:S(2)}) collective-permute-start(bf16[50,64,160]{2,1,0:T(8,128)(2,1)} %bitcast.12), channel_id=1, source_target_pairs={{1,0},{2,1},{3,2},{4,3},{5,4},{6,5},{7,6},{9,8},{10,9},{11,10},{12... | collective-permute-start | bytes 3072008 | tf_op jit(solution)/shard_map/ppermute | solution.py:23
  54.9 79.2 %collective-permute-start.5 = (bf16[50,64,160]{2,1,0:T(8,128)(2,1)}, bf16[50,64,160]{2,1,0:T(8,128)(2,1)}, u32[]{:S(2)}, u32[]{:S(2)}) collective-permute-start(bf16[50,64,160]{2,1,0:T(8,128)(2,1)} %bitcast.12), channel_id=1, source_target_pairs={{2,0},{3,1},{4,2},{5,3},{6,4},{7,5},{10,8},{11,9},{12,10},{13,11},... | collective-permute-start | bytes 3072008 | tf_op jit(solution)/shard_map/ppermute | solution.py:23
  83.1 77.2 %collective-permute-start.6 = (bf16[50,64,160]{2,1,0:T(8,128)(2,1)}, bf16[50,64,160]{2,1,0:T(8,128)(2,1)S(1)}, u32[]{:S(2)}, u32[]{:S(2)}) collective-permute-start(bf16[50,64,160]{2,1,0:T(8,128)(2,1)} %bitcast.12), channel_id=1, source_target_pairs={{3,0},{4,1},{5,2},{6,3},{7,4},{11,8},{12,9},{13,10},{14,11},{15,12... | collective-permute-start | bytes 3072008 | tf_op jit(solution)/shard_map/ppermute | solution.py:23
  134.2 26.2 %copy-start = (bf16[50,2,4,40,64]{4,3,2,1,0:T(8,128)(2,1)S(1)}, bf16[50,2,4,40,64]{4,3,2,1,0:T(8,128)(2,1)}, u32[]{:S(2)}) copy-start(bf16[50,2,4,40,64]{4,3,2,1,0:T(8,128)(2,1)} %copy.34) | copy-start | bytes 6144004

commit v3 on v2

v3 whole, which is shorter than its diff:
```python
import functools
import math

import jax
import jax.numpy as jnp
from jax import lax
from jax.experimental import pallas as pl
from jax.experimental.pallas import tpu as pltpu
from jax.sharding import PartitionSpec as P

FREQS = 200
WIN = 1024
LOW_BIN = 24
STEPS = 2
BAND = 3
HOP = 512
LANES = 128


def shifted(value, axis, steps):
    count = lax.axis_size(axis)
    initial, last = (max(0, -steps), min(count, count - steps))
    return lax.ppermute(value, axis, [(source, source + steps) for source in range(initial, last)])


def band_table():
    steps_k = jnp.arange(WIN, dtype=jnp.int32)
    bins = LOW_BIN + jnp.arange(FREQS, dtype=jnp.int32)
    phase = steps_k[:, None] * bins[None, :] % WIN
    angle = 2.0 * math.pi / WIN * phase.astype(jnp.float32)
    taper = 0.5 - 0.5 * jnp.cos(2.0 * math.pi / WIN * steps_k.astype(jnp.float32))
    factor = (8.0 / (3.0 * WIN)) ** 0.5
    cos_part = taper[:, None] * jnp.cos(angle) * factor
    sin_part = -taper[:, None] * jnp.sin(angle) * factor
    return jnp.stack([cos_part, sin_part], axis=1).astype(jnp.bfloat16)


def gram_kernel(factor, sel_ref, own_ref, *refs):
    found, (out_ref, turn, held_a, held_b, partners, sems) = refs[:-6], refs[-6:]
    group, rows, wide = own_ref.shape
    chans = math.isqrt(out_ref.shape[2] * LANES // 2)
    batch = wide // chans
    half = rows // 2
    reach = chans // batch
    width = batch * chans // LANES
    start = pl.program_id(0) * group

    @pl.when(pl.program_id(0) == 0)
    def _():
        for step in range(STEPS):
            for place, ref in enumerate(found):

                @pl.when(sel_ref[step] == place)
                def _():
                    pltpu.make_async_copy(ref, partners.at[step], sems.at[step]).start()

        for step in range(STEPS):
            pltpu.make_async_copy(found[0], partners.at[step], sems.at[step]).wait()

    def one_freq(f, carry):
        own = own_ref[f].astype(jnp.float32)
        plain, turned = [], []
        for r in range(batch):
            piece = own[:, r * chans : (r + 1) * chans]
            plain.append(piece)
            turned += [piece[half:], -piece[:half]]
        upright = jnp.concatenate(plain + turned, axis=0).T
        columns = []
        for k in range(turn.shape[0]):
            turn[k] = upright[:, k * LANES : (k + 1) * LANES]
            columns.append(
                jnp.concatenate(
                    [turn[k, pl.ds(r, reach, stride=batch), :] for r in range(batch)], axis=0
                )
            )
        left = jnp.concatenate(columns, axis=1).astype(jnp.bfloat16)
        for step, held in enumerate((held_a, held_b)):
            packed = partners[step, start + f]
            right = jnp.concatenate(
                [packed[:, r * chans : (r + 1) * chans] for r in range(batch)], axis=0
            )
            empty = jnp.zeros_like(right)
            for part in range(2):
                operand = jnp.concatenate([empty, right] if part else [right, empty], axis=0)
                gram = jnp.dot(left, operand, preferred_element_type=jnp.float32)
                pieces = [gram[r * reach : (r + 1) * reach] for r in range(batch)]
                for m in range(width):
                    parts = []
                    for r in range(batch):
                        low = max(m * LANES - r * chans, 0)
                        high = min((m + 1) * LANES - r * chans, chans)
                        if low < high:
                            parts.append(pieces[r][:, low:high])
                    line = parts[0] if len(parts) == 1 else jnp.concatenate(parts, axis=1)
                    held[pl.ds(2 * m + part, reach, stride=2 * width), :] = line
            out_ref[step, f] = (held[...] * factor).astype(jnp.bfloat16)
        return carry

    lax.fori_loop(0, group, one_freq, 0)


def packed_windows(got, batch):
    total, _, freqs, chans = got.shape
    split = got.reshape(total // batch, batch, 2, freqs, chans)
    return split.transpose(3, 2, 0, 1, 4).reshape(freqs, 2 * total // batch, batch * chans)


def cross_stacks(own, found, chosen, chans, factor):
    freqs, rows, wide = own.shape
    double = 2 * rows * wide // chans
    lines = 2 * chans * chans // LANES
    group = max(n for n in range(1, 9) if freqs % n == 0)
    grid_spec = pltpu.PrefetchScalarGridSpec(
        num_scalar_prefetch=1,
        grid=(freqs // group,),
        in_specs=[pl.BlockSpec((group, rows, wide), lambda g, sel: (g, 0, 0))]
        + [pl.BlockSpec(memory_space=pl.ANY)] * len(found),
        out_specs=pl.BlockSpec((STEPS, group, lines, LANES), lambda g, sel: (0, g, 0, 0)),
        scratch_shapes=[pltpu.VMEM((double // LANES, chans, LANES), jnp.float32)]
        + [pltpu.VMEM((lines, LANES), jnp.float32)] * STEPS
        + [
            pltpu.VMEM((STEPS,) + found[0].shape, jnp.bfloat16),
            pltpu.SemaphoreType.DMA((STEPS,)),
        ],
    )
    merged = pl.pallas_call(
        functools.partial(gram_kernel, factor),
        grid_spec=grid_spec,
        out_shape=jax.ShapeDtypeStruct((STEPS, freqs, lines, LANES), jnp.bfloat16),
        compiler_params=pltpu.CompilerParams(vmem_limit_bytes=24 * 2**20),
        cost_estimate=pl.CostEstimate(
            flops=4 * STEPS * freqs * double * chans * chans,
            bytes_accessed=4 * STEPS * freqs * chans * chans,
            transcendentals=0,
        ),
    )(chosen, own, *found)
    merged = merged.reshape(STEPS, freqs, lines // 2, 2, LANES).transpose(0, 3, 1, 2, 4)
    return merged.reshape(STEPS, 2, freqs, chans * chans)


def fetch_band(own):
    count = lax.axis_size("chan")
    swap = [(b, b ^ 1) for b in range(count)]
    above = shifted(own, "chan", -2)
    below = shifted(own, "chan", 2)
    twin = lax.ppermute(own, "chan", swap)
    on_down = lax.ppermute(above, "chan", [(b, b - 1) for b in range(2, count, 2)])
    on_up = lax.ppermute(below, "chan", [(b, b + 1) for b in range(1, count - 1, 2)])
    twin_above = lax.ppermute(above, "chan", swap)
    twin_below = lax.ppermute(below, "chan", swap)
    return [twin, above, below, twin_above, twin_below, on_down, on_up]


PLACES = ((6, 2, 4, 0, 0, 1, 3), (4, 2, 0, 0, 3, 1, 5))


def per_device(record, valid, pairs):
    channels, seg_len = record.shape
    windows = seg_len // HOP
    samples = record.astype(jnp.float32)
    scale = jnp.sqrt(jnp.mean(samples * samples, axis=-1, keepdims=True) + 1e-05)
    normed = (samples / scale).astype(jnp.bfloat16)
    following = shifted(normed[:, :HOP], "seg", -1)
    extended = jnp.concatenate([normed, following], axis=1)
    frames = jnp.concatenate(
        [
            extended[:, :seg_len].reshape(channels, windows, HOP),
            extended[:, HOP:].reshape(channels, windows, HOP),
        ],
        axis=-1,
    )
    spec = jnp.einsum("cwk,kpf->wpfc", frames, band_table(), preferred_element_type=jnp.float32)
    usable = valid.astype(jnp.float32)
    spectra = (spec * usable[None, None, None, :]).astype(jnp.bfloat16)
    got = lax.all_to_all(spectra, "seg", split_axis=2, concat_axis=0, tiled=True)
    batch = LANES // math.gcd(channels, LANES)
    own = packed_windows(got, batch)
    found = fetch_band(own)
    block = lax.axis_index("chan")
    row = jnp.where(block % 2 == 1, jnp.array(PLACES[1]), jnp.array(PLACES[0]))
    chosen = row[pairs[:, 0] - block + BAND].astype(jnp.int32)
    return cross_stacks(own, found, chosen, channels, 1.0 / math.sqrt(got.shape[0]))


def solution(mesh):
    in_specs = (P("chan", "seg"), P("chan"), P(None, "chan"))
    out_specs = P(None, None, "seg", "chan")
    return jax.shard_map(
        per_device, mesh=mesh, in_specs=in_specs, out_specs=out_specs, check_vma=False
    )
```

time: 181 us -> 116 us (0.64)
  waiting for transfers between devices: 70.3 us -> 29.5 us
  local copies, waits for them, and re-layouts: 31.3 us -> 5.7 us
  Pallas kernels: 19.9 us -> 30.2 us
  other arithmetic: 14.4 us -> 6.02 us
    ppermute x7 -> x3, waiting for transfers between devices: 70.3 us -> 16.4 us  [shifted(): lax.ppermute(value, axis, [(source, source + steps) for source in range(i...]
    ppermute x7 -> x3, starting transfers between devices: 21.1 us -> 5.86 us  [shifted(): lax.ppermute(value, axis, [(source, source + steps) for source in range(i...]
    ppermute x0 -> x5, starting transfers between devices: none -> 14.8 us  [the longest x1 9.09 us: fetch_band(): lax.ppermute(below, 'chan', [(b, b + 1) for b in range(1, count - 1, 2)])]
    ppermute x0 -> x5, waiting for transfers between devices: none -> 13.1 us  [the longest x1 7.66 us: fetch_band(): lax.ppermute(below, 'chan', [(b, b + 1) for b in range(1, count - 1, 2)])]
    transpose x3 -> x1, local copies, waits for them, and re-layouts: 13.8 us -> 0.92 us  [packed_windows(): split.transpose(3, 2, 0, 1, 4)]
    pallas_call x1, Pallas kernels: 19.9 us -> 30.2 us  [cross_stacks(): pl.pallas_call(functools.partial(gram_kernel, factor), grid_spec=grid_spe...]
    unnamed x11 -> x10, local copies, waits for them, and re-layouts: 8.2 us -> 0.03 us
    transpose x1 -> x0, other arithmetic: 5.32 us -> none  [gram_operand(): return both.transpose(0, 1, 4, 3, 2).reshape(freqs, 2 * chans, rows)]
  transfers between devices with their start and end apart: 7 -> 8, of which waited for: 4 -> 4; matrix products, arithmetic and copies ran while one was open for 22% -> 4% of each run, Pallas kernels for 0% -> 0%
where the time goes in v3:
time: 116 us; the launch traced here: 115 us
  Pallas kernels  30.2 us (26%)
  waiting for transfers between devices  29.5 us (25%)
  blocking collectives  21.5 us (19%)
  starting transfers between devices  20.6 us (18%)
  other arithmetic  6.02 us (5%)
  local copies, waits for them, and re-layouts  5.7 us (5%)
  matrix products  1.58 us (1%)
    pallas_call x1, Pallas kernels, cross_stacks(): pl.pallas_call(functools.partial(gram_kernel, factor), grid_spec=grid_spe...  30.2 us
    all_to_all x1, blocking collectives, per_device(): lax.all_to_all(spectra, 'seg', split_axis=2, concat_axis=0, tiled=True)  21.5 us
    ppermute x3, waiting for transfers between devices, shifted(): lax.ppermute(value, axis, [(source, source + steps) for source in range(i...  16.4 us
    ppermute x1, starting transfers between devices, fetch_band(): lax.ppermute(below, 'chan', [(b, b + 1) for b in range(1, count - 1, 2)])  9.09 us
    ppermute x1, waiting for transfers between devices, fetch_band(): lax.ppermute(below, 'chan', [(b, b + 1) for b in range(1, count - 1, 2)])  7.66 us
    ppermute x3, starting transfers between devices, shifted(): lax.ppermute(value, axis, [(source, source + steps) for source in range(i...  5.86 us
    ppermute x1, waiting for transfers between devices, fetch_band(): lax.ppermute(above, 'chan', [(b, b - 1) for b in range(2, count, 2)])  5.45 us
    another operation x1, other arithmetic  3.78 us
  transfers between devices with their start and end apart: 8, of which 4 were waited for; matrix products, arithmetic and copies ran while one was open for 4% of the time, Pallas kernels for 0%

profile of v3, /device:TPU:1, one launch (start us, length us, event | category | flops | bytes accessed | tf_op | source)
XLA Modules:
  0.0 115.3 jit_solution(4723348295970986797)
XLA Ops:
  0.0 1.8 %fusion = f32[160]{0:T(256)S(1)} fusion(bf16[160,4096]{1,0:T(8,128)(2,1)} %param.5), kind=kLoop, calls=%fused_computation.3 | loop fusion | flops 1965920 | bytes 1311360 | tf_op jit(solution)/shard_map/reduce_sum | solution.py:161
  1.8 0.3 fusion.1
  2.1 1.3 %collective-permute-start = (bf16[160,512]{1,0:T(8,128)(2,1)S(1)}, bf16[160,512]{1,0:T(8,128)(2,1)S(1)}, u32[]{:S(2)}, u32[]{:S(2)}) collective-permute-start(bf16[160,512]{1,0:T(8,128)(2,1)S(1)} %slice.10), channel_id=1, source_target_pairs={{8,0},{16,8},{24,16},{9,1},{17,9},{25,17},{10,2},{18,10},{26,18},{... | collective-permute-start | bytes 491528 | tf_op jit(solution)/shard_map/ppermute | solution.py:23
  3.5 0.1 copy.32
  3.6 3.8 %multiply_convert_fusion.2 = (bf16[1024,1,200]{0,2,1:T(8,128)(2,1)S(1)}, bf16[1024,1,200]{0,2,1:T(8,128)(2,1)S(1)}) fusion(s32[200]{0:T(256)S(1)} %iota_add_fusion, f32[1024]{0:T(1024)S(1)} %get-tuple-element.7, f32[1024]{0:T(1024)S(1)} %get-tuple-element.8), kind=kLoop, calls=%fused_computation.24 | loop fusion | flops 4096000 | bytes 828192 | tf_op jit(solution)/shard_map/convert
  7.4 2.6 %collective-permute-done = bf16[160,512]{1,0:T(8,128)(2,1)S(1)} collective-permute-done((bf16[160,512]{1,0:T(8,128)(2,1)S(1)}, bf16[160,512]{1,0:T(8,128)(2,1)S(1)}, u32[]{:S(2)}, u32[]{:S(2)}) %collective-permute-start) | collective-permute-done | bytes 163872 | tf_op jit(solution)/shard_map/ppermute | solution.py:23
  10.0 0.1 pad_maximum_fusion
  10.1 0.1 copy.31
  10.2 1.6 %fusion.5 = bf16[8,2,200,160]{2,3,0,1:T(8,128)(2,1)S(1)} fusion(bf16[160,8,512]{2,0,1:T(8,128)(2,1)S(1)} %bitcast.40, bf16[160,8,512]{2,0,1:T(8,128)(2,1)S(1)} %bitcast.39, f32[160]{0:T(256)S(1)} %convert_element_type.48, bf16[1024,1,200]{0,2,1:T(8,128)(2,1)S(1)} %get-tuple-element.6, bf16[1024,1,200]{0,2,1:T(8,128)(2,1)S(1)} %get-tuple-element.5), kind=kOutput, calls=%fused_computation.10 | convolution fusion | flops 1056481280 | bytes 4465280 | tf_op jit(solution)/shard_map/cwk,kpf->wpfc/dot_general | solution.py:172
  11.8 1.6 %copy.20 = bf16[8,2,200,160]{3,0,1,2:T(8,128)(2,1)S(1)} copy(bf16[8,2,200,160]{2,3,0,1:T(8,128)(2,1)S(1)} %fusion.5) | data formatting | bytes 2048000 | tf_op jit(solution)/shard_map/convert_element_type | solution.py:174
  13.4 21.5 %all_to_all.15 = bf16[8,2,200,160]{3,0,1,2:T(8,128)(2,1)S(1)} all-to-all(bf16[8,2,200,160]{3,0,1,2:T(8,128)(2,1)S(1)} %copy.20), channel_id=1, replica_groups=mesh['seg'=4,'chan'=8] {'seg'}, dimensions={2} | all-to-all | bytes 2048000 | tf_op jit(solution)/shard_map/all_to_all | solution.py:175
  34.9 1.3 %copy.22 = bf16[4,8,2,50,160]{4,2,3,1,0:T(2,128)(2,1)S(1)} copy(bf16[4,8,2,50,160]{4,1,2,3,0:T(8,128)(2,1)S(1)} %bitcast.36) | data formatting | bytes 2048000 | tf_op jit(solution)/shard_map/all_to_all | solution.py:175
  36.1 0.9 copy.23
  37.1 0.0 copy-start.4
  37.1 0.0 copy-start.2
  37.1 0.0 copy-start.3
  37.1 1.0 reshape.188.own_ref
  38.2 3.3 %collective-permute-start.3 = (bf16[50,16,640]{2,1,0:T(8,128)(2,1)S(1)}, bf16[50,16,640]{2,1,0:T(8,128)(2,1)S(1)}, u32[]{:S(2)}, u32[]{:S(2)}) collective-permute-start(bf16[50,16,640]{2,1,0:T(8,128)(2,1)S(1)} %reshape.188.own_ref), channel_id=1, source_target_pairs={{0,2},{1,3},{2,4},{3,5},{4,6},{5,7},{8,10},{9,11},{10,12},{11,13},... | collective-permute-start | bytes 3072008 | tf_op jit(solution)/shard_map/ppermute | solution.py:23
  41.4 1.3 %collective-permute-start.2 = (bf16[50,16,640]{2,1,0:T(8,128)(2,1)S(1)}, bf16[50,16,640]{2,1,0:T(8,128)(2,1)S(1)}, u32[]{:S(2)}, u32[]{:S(2)}) collective-permute-start(bf16[50,16,640]{2,1,0:T(8,128)(2,1)S(1)} %reshape.188.own_ref), channel_id=1, source_target_pairs={{2,0},{3,1},{4,2},{5,3},{6,4},{7,5},{10,8},{11,9},{12,10},{13,11},... | collective-permute-start | bytes 3072008 | tf_op jit(solution)/shard_map/ppermute | solution.py:23
  42.7 3.6 %collective-permute-start.1 = (bf16[50,16,640]{2,1,0:T(8,128)(2,1)S(1)}, bf16[50,16,640]{2,1,0:T(8,128)(2,1)}, u32[]{:S(2)}, u32[]{:S(2)}) collective-permute-start(bf16[50,16,640]{2,1,0:T(8,128)(2,1)S(1)} %reshape.188.own_ref), channel_id=1, source_target_pairs={{0,1},{1,0},{2,3},{3,2},{4,5},{5,4},{6,7},{7,6},{8,9},{9,8},{10,11... | collective-permute-start | bytes 3072008 | tf_op jit(solution)/shard_map/ppermute | solution.py:146
  46.3 13.8 %collective-permute-done.3.refs_2_ = bf16[50,16,640]{2,1,0:T(8,128)(2,1)S(1)} collective-permute-done((bf16[50,16,640]{2,1,0:T(8,128)(2,1)S(1)}, bf16[50,16,640]{2,1,0:T(8,128)(2,1)S(1)}, u32[]{:S(2)}, u32[]{:S(2)}) %collective-permute-start.3) | collective-permute-done | bytes 1024032 | tf_op jit(solution)/shard_map/ppermute | solution.py:23
  60.1 9.1 %collective-permute-start.7 = (bf16[50,16,640]{2,1,0:T(8,128)(2,1)S(1)}, bf16[50,16,640]{2,1,0:T(8,128)(2,1)}, u32[]{:S(2)}, u32[]{:S(2)}) collective-permute-start(bf16[50,16,640]{2,1,0:T(8,128)(2,1)S(1)} %collective-permute-done.3.refs_2_), channel_id=1, source_target_pairs={{1,2},{3,4},{5,6},{9,10},{11,12},{13,14},{17,18},{19,20},{21,22},{... | collective-permute-start | bytes 3072008 | tf_op jit(solution)/shard_map/ppermute | solution.py:148
  69.1 0.0 collective-permute-start.5
  69.1 0.0 collective-permute-done.2.refs_1_
  69.2 1.3 %collective-permute-start.6 = (bf16[50,16,640]{2,1,0:T(8,128)(2,1)S(1)}, bf16[50,16,640]{2,1,0:T(8,128)(2,1)}, u32[]{:S(2)}, u32[]{:S(2)}) collective-permute-start(bf16[50,16,640]{2,1,0:T(8,128)(2,1)S(1)} %collective-permute-done.2.refs_1_), channel_id=1, source_target_pairs={{2,1},{4,3},{6,5},{10,9},{12,11},{14,13},{18,17},{20,19},{22,21},{... | collective-permute-start | bytes 3072008 | tf_op jit(solution)/shard_map/ppermute | solution.py:147
  70.4 0.9 collective-permute-start.4
  71.3 0.6 gather_fusion
  72.0 0.0 collective-permute-done.1.refs_0_
  72.0 7.7 %collective-permute-done.7.refs_6_ = bf16[50,16,640]{2,1,0:T(8,128)(2,1)} collective-permute-done((bf16[50,16,640]{2,1,0:T(8,128)(2,1)S(1)}, bf16[50,16,640]{2,1,0:T(8,128)(2,1)}, u32[]{:S(2)}, u32[]{:S(2)}) %collective-permute-start.7) | collective-permute-done | bytes 1024032 | tf_op jit(solution)/shard_map/ppermute | solution.py:148
  79.6 5.5 %collective-permute-done.6.refs_5_ = bf16[50,16,640]{2,1,0:T(8,128)(2,1)} collective-permute-done((bf16[50,16,640]{2,1,0:T(8,128)(2,1)S(1)}, bf16[50,16,640]{2,1,0:T(8,128)(2,1)}, u32[]{:S(2)}, u32[]{:S(2)}) %collective-permute-start.6) | collective-permute-done | bytes 1024032 | tf_op jit(solution)/shard_map/ppermute | solution.py:147
  85.1 0.0 collective-permute-done.4.refs_3_
  85.1 30.2 %shard_map.55 = bf16[2,50,400,128]{3,2,1,0:T(8,128)(2,1)} custom-call(s32[2]{0:T(128)S(1)} %gather_fusion, bf16[50,16,640]{2,1,0:T(8,128)(2,1)S(1)} %reshape.188.own_ref, bf16[50,16,640]{2,1,0:T(8,128)(2,1)} %collective-permute-done.1.refs_0_, bf16[50,16,640]{2,1,0:T(8,128)(2,1)S(1)} %collective-permute-done.2.refs_1_, ...), custom_call_target="tpu_custom_call" | custom-call | flops 1310720000 | bytes 10240000 | tf_op jit(solution)/shard_map/pallas_call | solution.py:126
  (16 shorter events, 0.1 us)
Async XLA Ops:
  0.0 1.8 %copy-start = (bf16[160,4096]{1,0:T(8,128)(2,1)S(1)}, bf16[160,4096]{1,0:T(8,128)(2,1)}, u32[]{:S(2)}) copy-start(bf16[160,4096]{1,0:T(8,128)(2,1)} %param.5) | copy-start | bytes 3932164
  1.8 1.7 %copy-start.1 = (s32[160]{0:T(256)S(1)}, s32[160]{0:T(256)}, u32[]{:S(2)}) copy-start(s32[160]{0:T(256)} %param.6) | copy-start | bytes 1924
  2.1 7.9 %collective-permute-start = (bf16[160,512]{1,0:T(8,128)(2,1)S(1)}, bf16[160,512]{1,0:T(8,128)(2,1)S(1)}, u32[]{:S(2)}, u32[]{:S(2)}) collective-permute-start(bf16[160,512]{1,0:T(8,128)(2,1)S(1)} %slice.10), channel_id=1, source_target_pairs={{8,0},{16,8},{24,16},{9,1},{17,9},{25,17},{10,2},{18,10},{26,18},{... | collective-permute-start | bytes 491528 | tf_op jit(solution)/shard_map/ppermute | solution.py:23
  37.1 34.2 %copy-start.4 = (s32[2,1]{0,1:T(1,128)S(1)}, s32[2,1]{0,1:T(1,128)}, u32[]{:S(2)}) copy-start(s32[2,1]{0,1:T(1,128)} %param.7) | copy-start | bytes 28
  37.1 34.2 %copy-start.2 = (s32[7]{0:T(128)S(1)}, s32[7]{0:T(128)}, u32[]{:S(2)}) copy-start(s32[7]{0:T(128)} %constant.59.clone) | copy-start | bytes 88
  37.1 34.2 %copy-start.3 = (s32[7]{0:T(128)S(1)}, s32[7]{0:T(128)}, u32[]{:S(2)}) copy-start(s32[7]{0:T(128)} %constant.58.clone) | copy-start | bytes 88
  38.2 21.9 %collective-permute-start.3 = (bf16[50,16,640]{2,1,0:T(8,128)(2,1)S(1)}, bf16[50,16,640]{2,1,0:T(8,128)(2,1)S(1)}, u32[]{:S(2)}, u32[]{:S(2)}) collective-permute-start(bf16[50,16,640]{2,1,0:T(8,128)(2,1)S(1)} %reshape.188.own_ref), channel_id=1, source_target_pairs={{0,2},{1,3},{2,4},{3,5},{4,6},{5,7},{8,10},{9,11},{10,12},{11,13},... | collective-permute-start | bytes 3072008 | tf_op jit(solution)/shard_map/ppermute | solution.py:23
  41.4 27.7 %collective-permute-start.2 = (bf16[50,16,640]{2,1,0:T(8,128)(2,1)S(1)}, bf16[50,16,640]{2,1,0:T(8,128)(2,1)S(1)}, u32[]{:S(2)}, u32[]{:S(2)}) collective-permute-start(bf16[50,16,640]{2,1,0:T(8,128)(2,1)S(1)} %reshape.188.own_ref), channel_id=1, source_target_pairs={{2,0},{3,1},{4,2},{5,3},{6,4},{7,5},{10,8},{11,9},{12,10},{13,11},... | collective-permute-start | bytes 3072008 | tf_op jit(solution)/shard_map/ppermute | solution.py:23
  42.7 29.3 %collective-permute-start.1 = (bf16[50,16,640]{2,1,0:T(8,128)(2,1)S(1)}, bf16[50,16,640]{2,1,0:T(8,128)(2,1)}, u32[]{:S(2)}, u32[]{:S(2)}) collective-permute-start(bf16[50,16,640]{2,1,0:T(8,128)(2,1)S(1)} %reshape.188.own_ref), channel_id=1, source_target_pairs={{0,1},{1,0},{2,3},{3,2},{4,5},{5,4},{6,7},{7,6},{8,9},{9,8},{10,11... | collective-permute-start | bytes 3072008 | tf_op jit(solution)/shard_map/ppermute | solution.py:146
  60.1 19.6 %collective-permute-start.7 = (bf16[50,16,640]{2,1,0:T(8,128)(2,1)S(1)}, bf16[50,16,640]{2,1,0:T(8,128)(2,1)}, u32[]{:S(2)}, u32[]{:S(2)}) collective-permute-start(bf16[50,16,640]{2,1,0:T(8,128)(2,1)S(1)} %collective-permute-done.3.refs_2_), channel_id=1, source_target_pairs={{1,2},{3,4},{5,6},{9,10},{11,12},{13,14},{17,18},{19,20},{21,22},{... | collective-permute-start | bytes 3072008 | tf_op jit(solution)/shard_map/ppermute | solution.py:148
  69.1 10.5 %collective-permute-start.5 = (bf16[50,16,640]{2,1,0:T(8,128)(2,1)S(1)}, bf16[50,16,640]{2,1,0:T(8,128)(2,1)}, u32[]{:S(2)}, u32[]{:S(2)}) collective-permute-start(bf16[50,16,640]{2,1,0:T(8,128)(2,1)S(1)} %collective-permute-done.3.refs_2_), channel_id=1, source_target_pairs={{0,1},{1,0},{2,3},{3,2},{4,5},{5,4},{6,7},{7,6},{8,9},{9,8},{10,11... | collective-permute-start | bytes 3072008 | tf_op jit(solution)/shard_map/ppermute | solution.py:150
  69.2 15.9 %collective-permute-start.6 = (bf16[50,16,640]{2,1,0:T(8,128)(2,1)S(1)}, bf16[50,16,640]{2,1,0:T(8,128)(2,1)}, u32[]{:S(2)}, u32[]{:S(2)}) collective-permute-start(bf16[50,16,640]{2,1,0:T(8,128)(2,1)S(1)} %collective-permute-done.2.refs_1_), channel_id=1, source_target_pairs={{2,1},{4,3},{6,5},{10,9},{12,11},{14,13},{18,17},{20,19},{22,21},{... | collective-permute-start | bytes 3072008 | tf_op jit(solution)/shard_map/ppermute | solution.py:147
  70.4 14.7 %collective-permute-start.4 = (bf16[50,16,640]{2,1,0:T(8,128)(2,1)S(1)}, bf16[50,16,640]{2,1,0:T(8,128)(2,1)}, u32[]{:S(2)}, u32[]{:S(2)}) collective-permute-start(bf16[50,16,640]{2,1,0:T(8,128)(2,1)S(1)} %collective-permute-done.2.refs_1_), channel_id=1, source_target_pairs={{0,1},{1,0},{2,3},{3,2},{4,5},{5,4},{6,7},{7,6},{8,9},{9,8},{10,11... | collective-permute-start | bytes 3072008 | tf_op jit(solution)/shard_map/ppermute | solution.py:149

commit v4 on v3

v4 whole, which is shorter than its diff:
```python
import functools
import math

import jax
import jax.numpy as jnp
from jax import lax
from jax.experimental import pallas as pl
from jax.experimental.pallas import tpu as pltpu
from jax.sharding import PartitionSpec as P

FREQS = 200
WIN = 1024
LOW_BIN = 24
STEPS = 2
BAND = 3
HOP = 512
LANES = 128


def shifted(value, axis, steps):
    count = lax.axis_size(axis)
    initial, last = (max(0, -steps), min(count, count - steps))
    return lax.ppermute(value, axis, [(source, source + steps) for source in range(initial, last)])


def band_table():
    steps_k = jnp.arange(WIN, dtype=jnp.int32)
    bins = LOW_BIN + jnp.arange(FREQS, dtype=jnp.int32)
    phase = steps_k[:, None] * bins[None, :] % WIN
    angle = 2.0 * math.pi / WIN * phase.astype(jnp.float32)
    taper = 0.5 - 0.5 * jnp.cos(2.0 * math.pi / WIN * steps_k.astype(jnp.float32))
    factor = (8.0 / (3.0 * WIN)) ** 0.5
    cos_part = taper[:, None] * jnp.cos(angle) * factor
    sin_part = -taper[:, None] * jnp.sin(angle) * factor
    return jnp.stack([cos_part, sin_part], axis=1).astype(jnp.bfloat16)


def turn_kernel(half, own_ref, left_ref, *turns):
    group, rows, wide = own_ref.shape
    chans = left_ref.shape[1]
    batch = wide // chans
    reach = chans // batch
    row = lax.broadcasted_iota(jnp.int32, (rows, chans), 0)
    real = row % (2 * half) < half
    for f in range(group):
        turn = turns[f]
        own = own_ref[f].astype(jnp.float32)
        plain = [own[:, r * chans : (r + 1) * chans] for r in range(batch)]
        turned = [
            jnp.where(real, pltpu.roll(p, rows - half, 0), -pltpu.roll(p, half, 0)) for p in plain
        ]
        upright = jnp.concatenate(plain + turned, axis=0).T
        for k in range(turn.shape[0]):
            turn[k] = upright[:, k * LANES : (k + 1) * LANES]
            for r in range(batch):
                left_ref[f, pl.ds(r * reach, reach), pl.ds(k * LANES, LANES)] = turn[
                    k, pl.ds(r, reach, stride=batch), :
                ].astype(jnp.bfloat16)


def turned_own(own, chans, half):
    freqs, rows, wide = own.shape
    double = 2 * rows * wide // chans
    group = freq_group(freqs)
    return pl.pallas_call(
        functools.partial(turn_kernel, half),
        grid=(freqs // group,),
        in_specs=[pl.BlockSpec((group, rows, wide), lambda g: (g, 0, 0))],
        out_specs=pl.BlockSpec((group, chans, double), lambda g: (g, 0, 0)),
        out_shape=jax.ShapeDtypeStruct((freqs, chans, double), jnp.bfloat16),
        scratch_shapes=[pltpu.VMEM((double // LANES, chans, LANES), jnp.float32)] * group,
        compiler_params=pltpu.CompilerParams(vmem_limit_bytes=16 * 2**20),
        cost_estimate=pl.CostEstimate(
            flops=0, bytes_accessed=24 * freqs * chans * double, transcendentals=0
        ),
    )(own)


def freq_group(freqs):
    return max(n for n in range(1, 6) if freqs % n == 0)


def gram_kernel(factor, places, aliased, sel_ref, left_ref, *refs):
    group, chans, _ = left_ref.shape
    found, refs = refs[:places], refs[places + aliased :]
    out_ref, refs = refs[0], refs[1:]
    held, (partners, sems) = refs[:-2], refs[-2:]
    batch = found[0].shape[2] // chans
    reach = chans // batch
    width = batch * chans // LANES
    start = pl.program_id(0) * group

    @pl.when(pl.program_id(0) == 0)
    def _():
        for step in range(STEPS):
            for place, ref in enumerate(found):

                @pl.when(sel_ref[step] == place)
                def _():
                    pltpu.make_async_copy(ref, partners.at[step], sems.at[step]).start()

        for step in range(STEPS):
            pltpu.make_async_copy(found[0], partners.at[step], sems.at[step]).wait()

    for f in range(group):
        left = left_ref[f]
        for step in range(STEPS):
            lines = held[f * STEPS + step]
            packed = partners[step, start + f]
            right = jnp.concatenate(
                [packed[:, r * chans : (r + 1) * chans] for r in range(batch)], axis=0
            )
            empty = jnp.zeros_like(right)
            for part in range(2):
                operand = jnp.concatenate([empty, right] if part else [right, empty], axis=0)
                gram = jnp.dot(left, operand, preferred_element_type=jnp.float32)
                pieces = [gram[r * reach : (r + 1) * reach] for r in range(batch)]
                for m in range(width):
                    parts = []
                    for r in range(batch):
                        low = max(m * LANES - r * chans, 0)
                        high = min((m + 1) * LANES - r * chans, chans)
                        if low < high:
                            parts.append(pieces[r][:, low:high])
                    line = parts[0] if len(parts) == 1 else jnp.concatenate(parts, axis=1)
                    lines[pl.ds(2 * m + part, reach, stride=2 * width), :] = line
            out_ref[step, f] = (lines[...] * factor).astype(jnp.bfloat16)


def cross_stacks(left, found, chosen, factor, total, first, so_far):
    freqs, chans, double = left.shape
    lines = 2 * chans * chans // LANES
    group = freq_group(freqs)
    skip = first // group
    extra = [] if so_far is None else [so_far]
    anywhere = pl.BlockSpec(memory_space=pl.ANY)
    grid_spec = pltpu.PrefetchScalarGridSpec(
        num_scalar_prefetch=1,
        grid=(freqs // group,),
        in_specs=[pl.BlockSpec((group, chans, double), lambda g, sel: (g, 0, 0))]
        + [anywhere] * (len(found) + len(extra)),
        out_specs=pl.BlockSpec((STEPS, group, lines, LANES), lambda g, sel: (0, g + skip, 0, 0)),
        scratch_shapes=[pltpu.VMEM((lines, LANES), jnp.float32)] * (STEPS * group)
        + [
            pltpu.VMEM((STEPS,) + found[0].shape, jnp.bfloat16),
            pltpu.SemaphoreType.DMA((STEPS,)),
        ],
    )
    return pl.pallas_call(
        functools.partial(gram_kernel, factor, len(found), len(extra)),
        grid_spec=grid_spec,
        out_shape=jax.ShapeDtypeStruct((STEPS, total, lines, LANES), jnp.bfloat16),
        input_output_aliases={2 + len(found): 0} if extra else {},
        compiler_params=pltpu.CompilerParams(vmem_limit_bytes=24 * 2**20),
        cost_estimate=pl.CostEstimate(
            flops=4 * STEPS * freqs * double * chans * chans,
            bytes_accessed=12 * STEPS * freqs * chans * chans,
            transcendentals=0,
        ),
    )(chosen, left, *found, *extra)


def fetch_band(own, make_left):
    count = lax.axis_size("chan")
    swap = [(b, b ^ 1) for b in range(count)]
    above = shifted(own, "chan", -2)
    below = shifted(own, "chan", 2)
    twin = lax.ppermute(own, "chan", swap)
    above, below, left = lax.optimization_barrier((above, below, make_left(own)))
    on_down = lax.ppermute(above, "chan", [(b, b - 1) for b in range(2, count, 2)])
    on_up = lax.ppermute(below, "chan", [(b, b + 1) for b in range(1, count - 1, 2)])
    twin_above = lax.ppermute(above, "chan", swap)
    twin_below = lax.ppermute(below, "chan", swap)
    return left, [twin, above, below, twin_above, twin_below, on_down, on_up]


PLACES = ((6, 2, 4, 0, 0, 1, 3), (4, 2, 0, 0, 3, 1, 5))


def per_device(record, valid, pairs):
    channels, seg_len = record.shape
    windows = seg_len // HOP
    samples = record.astype(jnp.float32)
    scale = jnp.sqrt(jnp.mean(samples * samples, axis=-1, keepdims=True) + 1e-05)
    normed = (samples / scale).astype(jnp.bfloat16)
    following = shifted(normed[:, :HOP], "seg", -1)
    extended = jnp.concatenate([normed, following], axis=1)
    frames = jnp.concatenate(
        [
            extended[:, :seg_len].reshape(channels, windows, HOP),
            extended[:, HOP:].reshape(channels, windows, HOP),
        ],
        axis=-1,
    )
    spec = jnp.einsum("cwk,kpf->wpfc", frames, band_table(), preferred_element_type=jnp.float32)
    usable = valid.astype(jnp.float32)
    spectra = (spec * usable[None, None, None, :]).astype(jnp.bfloat16)
    batch = LANES // math.gcd(channels, LANES)
    segs = lax.axis_size("seg")
    freqs = FREQS // segs
    half = windows // batch
    split = spectra.reshape(half, batch, 2, segs, freqs, channels)
    packed = split.transpose(3, 4, 2, 0, 1, 5).reshape(segs, freqs, 2 * half, batch * channels)
    block = lax.axis_index("chan")
    row = jnp.where(block % 2 == 1, jnp.array(PLACES[1]), jnp.array(PLACES[0]))
    chosen = row[pairs[:, 0] - block + BAND].astype(jnp.int32)
    factor = 1.0 / math.sqrt(segs * windows)
    group = freq_group(freqs)
    cut = pl.cdiv(freqs // group, 2) * group
    chunks = []
    for first, last in ((0, cut), (cut, freqs)):
        got = lax.all_to_all(packed[:, first:last], "seg", split_axis=0, concat_axis=0, tiled=True)
        own = got.transpose(1, 0, 2, 3).reshape(last - first, segs * 2 * half, batch * channels)
        chunks.append((first,) + fetch_band(own, lambda x: turned_own(x, channels, half)))
    merged = None
    for first, left, found in chunks:
        merged = cross_stacks(left, found, chosen, factor, freqs, first, merged)
    lines = merged.shape[2]
    merged = merged.reshape(STEPS, freqs, lines // 2, 2, LANES).transpose(0, 3, 1, 2, 4)
    return merged.reshape(STEPS, 2, freqs, channels * channels)


def solution(mesh):
    in_specs = (P("chan", "seg"), P("chan"), P(None, "chan"))
    out_specs = P(None, None, "seg", "chan")
    return jax.shard_map(
        per_device, mesh=mesh, in_specs=in_specs, out_specs=out_specs, check_vma=False
    )
```

time: 116 us -> 91.3 us (0.79)
  waiting for transfers between devices: 29.5 us -> 4.92 us
  starting transfers between devices: 20.6 us -> 40.9 us
  blocking collectives: 21.5 us -> 9.4 us
  Pallas kernels: 30.2 us -> 19.7 us
  local copies, waits for them, and re-layouts: 5.7 us -> 7.59 us
    ppermute x3 -> x5, waiting for transfers between devices: 16.4 us -> 2.6 us  [shifted(): lax.ppermute(value, axis, [(source, source + steps) for source in range(i...]
    all_to_all x1, blocking collectives: 21.5 us -> 9.4 us  [per_device(): lax.all_to_all(packed[:, first:last], 'seg', split_axis=0, concat_axis=0,...]
    pallas_call x1 -> x4, Pallas kernels: 30.2 us -> 19.7 us  [the longest x2 16.2 us: cross_stacks(): pl.pallas_call(functools.partial(gram_kernel, factor, len(found), len(ext...]
    ppermute x1 -> x2, waiting for transfers between devices: 7.66 us -> 0.01 us  [fetch_band(): lax.ppermute(below, 'chan', [(b, b + 1) for b in range(1, count - 1, 2)])]
    ppermute x1 -> x2, starting transfers between devices: 0.85 us -> 7.34 us  [fetch_band(): twin_above = lax.ppermute(above, 'chan', swap)]
    ppermute x3 -> x5, starting transfers between devices: 5.86 us -> 12 us  [shifted(): lax.ppermute(value, axis, [(source, source + steps) for source in range(i...]
    all_to_all x0 -> x1, starting transfers between devices: none -> 3.47 us  [per_device(): lax.all_to_all(packed[:, first:last], 'seg', split_axis=0, concat_axis=0,...]
    ppermute x1 -> x2, waiting for transfers between devices: 5.45 us -> 2.29 us  [fetch_band(): lax.ppermute(above, 'chan', [(b, b - 1) for b in range(2, count, 2)])]
  transfers between devices with their start and end apart: 8 -> 16, of which waited for: 4 -> 2; matrix products, arithmetic and copies ran while one was open for 4% -> 6% of each run, Pallas kernels for 0% -> 13%
where the time goes in v4:
time: 91.3 us; the launch traced here: 90.5 us
  starting transfers between devices  40.9 us (45%)
  Pallas kernels  19.7 us (22%)
  blocking collectives  9.4 us (10%)
  local copies, waits for them, and re-layouts  7.59 us (8%)
  other arithmetic  6.02 us (7%)
  waiting for transfers between devices  4.92 us (5%)
  matrix products  1.58 us (2%)
    pallas_call x2, Pallas kernels, cross_stacks(): pl.pallas_call(functools.partial(gram_kernel, factor, len(found), len(ext...  16.2 us
    ppermute x5, starting transfers between devices, shifted(): lax.ppermute(value, axis, [(source, source + steps) for source in range(i...  12 us
    ppermute x2, starting transfers between devices, fetch_band(): lax.ppermute(below, 'chan', [(b, b + 1) for b in range(1, count - 1, 2)])  11.2 us
    all_to_all x1, blocking collectives, per_device(): lax.all_to_all(packed[:, first:last], 'seg', split_axis=0, concat_axis=0,...  9.4 us
    ppermute x2, starting transfers between devices, fetch_band(): twin_above = lax.ppermute(above, 'chan', swap)  7.34 us
    ppermute x2, starting transfers between devices, fetch_band(): twin = lax.ppermute(own, 'chan', swap)  4.14 us
    another operation x1, other arithmetic  3.78 us
    all_to_all x1, starting transfers between devices, per_device(): lax.all_to_all(packed[:, first:last], 'seg', split_axis=0, concat_axis=0,...  3.47 us
  transfers between devices with their start and end apart: 16, of which 2 were waited for; matrix products, arithmetic and copies ran while one was open for 6% of the time, Pallas kernels for 13%

profile of v4, /device:TPU:1, one launch (start us, length us, event | category | flops | bytes accessed | tf_op | source)
XLA Modules:
  0.0 90.5 jit_solution(1339961645674715275)
XLA Ops:
  0.0 1.8 %fusion = f32[160]{0:T(256)S(1)} fusion(bf16[160,4096]{1,0:T(8,128)(2,1)} %param.5), kind=kLoop, calls=%fused_computation.3 | loop fusion | flops 1965920 | bytes 1311360 | tf_op jit(solution)/shard_map/reduce_sum | solution.py:184
  1.8 0.3 fusion.1
  2.1 1.3 %collective-permute-start = (bf16[160,512]{1,0:T(8,128)(2,1)S(1)}, bf16[160,512]{1,0:T(8,128)(2,1)S(1)}, u32[]{:S(2)}, u32[]{:S(2)}) collective-permute-start(bf16[160,512]{1,0:T(8,128)(2,1)S(1)} %slice.18), channel_id=1, source_target_pairs={{8,0},{16,8},{24,16},{9,1},{17,9},{25,17},{10,2},{18,10},{26,18},{... | collective-permute-start | bytes 491528 | tf_op jit(solution)/shard_map/ppermute | solution.py:23
  3.6 3.8 %multiply_convert_fusion.2 = (bf16[1024,1,200]{0,2,1:T(8,128)(2,1)S(1)}, bf16[1024,1,200]{0,2,1:T(8,128)(2,1)S(1)}) fusion(s32[200]{0:T(256)S(1)} %iota_add_fusion, f32[1024]{0:T(1024)S(1)} %get-tuple-element.21, f32[1024]{0:T(1024)S(1)} %get-tuple-element.22), kind=kLoop, calls=%fused_computation.24 | loop fusion | flops 4096000 | bytes 828192 | tf_op jit(solution)/shard_map/convert
  7.4 2.6 %collective-permute-done = bf16[160,512]{1,0:T(8,128)(2,1)S(1)} collective-permute-done((bf16[160,512]{1,0:T(8,128)(2,1)S(1)}, bf16[160,512]{1,0:T(8,128)(2,1)S(1)}, u32[]{:S(2)}, u32[]{:S(2)}) %collective-permute-start) | collective-permute-done | bytes 163872 | tf_op jit(solution)/shard_map/ppermute | solution.py:23
  10.2 1.6 %fusion.5 = bf16[8,2,200,160]{2,3,0,1:T(8,128)(2,1)S(1)} fusion(bf16[160,8,512]{2,0,1:T(8,128)(2,1)S(1)} %bitcast.40, bf16[160,8,512]{2,0,1:T(8,128)(2,1)S(1)} %bitcast.39, f32[160]{0:T(256)S(1)} %convert_element_type.48, bf16[1024,1,200]{0,2,1:T(8,128)(2,1)S(1)} %get-tuple-element.20, bf16[1024,1,200]{0,2,1:T(8,128)(2,1)S(1)} %get-tuple-element.19), kind=kOutput, calls=%fused_computation.10 | convolution fusion | flops 1056481280 | bytes 4465280 | tf_op jit(solution)/shard_map/cwk,kpf->wpfc/dot_general | solution.py:195
  11.8 1.6 %copy.15 = bf16[8,2,200,160]{3,1,2,0:T(2,128)(2,1)S(1)} copy(bf16[8,2,200,160]{2,3,0,1:T(8,128)(2,1)S(1)} %fusion.5) | data formatting | bytes 2048000 | tf_op jit(solution)/shard_map/convert_element_type | solution.py:197
  13.4 1.3 %copy.16 = bf16[4,50,2,2,4,160]{5,4,3,2,1,0:T(4,128)(2,1)S(1)} copy(bf16[4,50,2,2,4,160]{5,2,1,0,4,3:T(2,128)(2,1)S(1)} %bitcast.35) | data formatting | bytes 2048000 | tf_op jit(solution)/shard_map/transpose | solution.py:203
  14.6 1.4 %reshape.193 = bf16[4,50,4,640]{3,2,1,0:T(4,128)(2,1)S(1)} reshape(bf16[4,50,2,2,4,160]{5,4,3,2,1,0:T(4,128)(2,1)S(1)} %copy.16) | data formatting | bytes 2048000 | tf_op jit(solution)/shard_map/reshape | solution.py:203
  16.1 1.1 %fusion.17 = (bf16[4,25,4,640]{3,2,1,0:T(4,128)(2,1)S(1)}, bf16[4,25,4,640]{3,2,1,0:T(4,128)(2,1)}) fusion(bf16[4,50,4,640]{3,2,1,0:T(4,128)(2,1)S(1)} %reshape.193), kind=kLoop, calls=%fused_computation.37 | loop fusion | bytes 2048000 | tf_op jit(solution)/shard_map/slice | solution.py:212
  17.2 9.4 %all_to_all.10 = bf16[4,25,4,640]{3,2,1,0:T(4,128)(2,1)S(1)} all-to-all(bf16[4,25,4,640]{3,2,1,0:T(4,128)(2,1)S(1)} %get-tuple-element.17), channel_id=1, replica_groups=mesh['seg'=4,'chan'=8] {'seg'}, dimensions={0} | all-to-all | bytes 1024000 | tf_op jit(solution)/shard_map/all_to_all | solution.py:212
  26.6 3.5 %all-to-all-start = ((bf16[4,25,4,640]{3,2,1,0:T(4,128)(2,1)}), bf16[4,25,4,640]{3,2,1,0:T(4,128)(2,1)S(1)}, u32[]{:S(2)}, u32[]{:S(2)}) async-start(bf16[4,25,4,640]{3,2,1,0:T(4,128)(2,1)} %get-tuple-element.18), calls=%async_computation | async-start | bytes 1024000 | tf_op jit(solution)/shard_map/all_to_all | solution.py:212
  30.1 0.2 copy.18
  30.4 4.0 %collective-permute-start.9 = (bf16[25,16,640]{2,1,0:T(8,128)(2,1)S(1)}, bf16[25,16,640]{2,1,0:T(8,128)(2,1)}, u32[]{:S(2)}, u32[]{:S(2)}) collective-permute-start(bf16[25,16,640]{2,1,0:T(8,128)(2,1)S(1)} %reshape.195.own_ref), channel_id=1, source_target_pairs={{0,2},{1,3},{2,4},{3,5},{4,6},{5,7},{8,10},{9,11},{10,12},{11,13},... | collective-permute-start | bytes 1536008 | tf_op jit(solution)/shard_map/ppermute | solution.py:23
  34.4 1.3 %collective-permute-start.8 = (bf16[25,16,640]{2,1,0:T(8,128)(2,1)S(1)}, bf16[25,16,640]{2,1,0:T(8,128)(2,1)}, u32[]{:S(2)}, u32[]{:S(2)}) collective-permute-start(bf16[25,16,640]{2,1,0:T(8,128)(2,1)S(1)} %reshape.195.own_ref), channel_id=1, source_target_pairs={{2,0},{3,1},{4,2},{5,3},{6,4},{7,5},{10,8},{11,9},{12,10},{13,11},... | collective-permute-start | bytes 1536008 | tf_op jit(solution)/shard_map/ppermute | solution.py:23
  35.7 0.2 copy.17
  36.1 4.2 %collective-permute-start.2 = (bf16[25,16,640]{2,1,0:T(8,128)(2,1)S(1)}, bf16[25,16,640]{2,1,0:T(8,128)(2,1)S(1)}, u32[]{:S(2)}, u32[]{:S(2)}) collective-permute-start(bf16[25,16,640]{2,1,0:T(8,128)(2,1)S(1)} %reshape.194.own_ref), channel_id=1, source_target_pairs={{0,2},{1,3},{2,4},{3,5},{4,6},{5,7},{8,10},{9,11},{10,12},{11,13},... | collective-permute-start | bytes 1536008 | tf_op jit(solution)/shard_map/ppermute | solution.py:23
  40.2 1.3 %collective-permute-start.1 = (bf16[25,16,640]{2,1,0:T(8,128)(2,1)S(1)}, bf16[25,16,640]{2,1,0:T(8,128)(2,1)S(1)}, u32[]{:S(2)}, u32[]{:S(2)}) collective-permute-start(bf16[25,16,640]{2,1,0:T(8,128)(2,1)S(1)} %reshape.194.own_ref), channel_id=1, source_target_pairs={{2,0},{3,1},{4,2},{5,3},{6,4},{7,5},{10,8},{11,9},{12,10},{13,11},... | collective-permute-start | bytes 1536008 | tf_op jit(solution)/shard_map/ppermute | solution.py:23
  41.5 4.0 %collective-permute-start.10 = (bf16[25,16,640]{2,1,0:T(8,128)(2,1)S(1)}, bf16[25,16,640]{2,1,0:T(8,128)(2,1)}, u32[]{:S(2)}, u32[]{:S(2)}) collective-permute-start(bf16[25,16,640]{2,1,0:T(8,128)(2,1)S(1)} %reshape.195.own_ref), channel_id=1, source_target_pairs={{0,1},{1,0},{2,3},{3,2},{4,5},{5,4},{6,7},{7,6},{8,9},{9,8},{10,11... | collective-permute-start | bytes 1536008 | tf_op jit(solution)/shard_map/ppermute | solution.py:168
  45.5 1.7 %shard_map.56.left_ref = bf16[25,160,128]{2,1,0:T(8,128)(2,1)S(1)} custom-call(bf16[25,16,640]{2,1,0:T(8,128)(2,1)S(1)} %reshape.195.own_ref), custom_call_target="tpu_custom_call" | custom-call | bytes 12288000 | tf_op jit(solution)/shard_map/pallas_call | solution.py:65
  47.2 1.3 %collective-permute-start.13 = (bf16[25,16,640]{2,1,0:T(8,128)(2,1)}, bf16[25,16,640]{2,1,0:T(8,128)(2,1)}, u32[]{:S(2)}, u32[]{:S(2)}) collective-permute-start(bf16[25,16,640]{2,1,0:T(8,128)(2,1)} %collective-permute-done.8.refs_1_), channel_id=1, source_target_pairs={{2,1},{4,3},{6,5},{10,9},{12,11},{14,13},{18,17},{20,19},{22,21},{... | collective-permute-start | bytes 1536008 | tf_op jit(solution)/shard_map/ppermute | solution.py:170
  48.5 7.3 %collective-permute-start.11 = (bf16[25,16,640]{2,1,0:T(8,128)(2,1)}, bf16[25,16,640]{2,1,0:T(8,128)(2,1)}, u32[]{:S(2)}, u32[]{:S(2)}) collective-permute-start(bf16[25,16,640]{2,1,0:T(8,128)(2,1)} %collective-permute-done.8.refs_1_), channel_id=1, source_target_pairs={{0,1},{1,0},{2,3},{3,2},{4,5},{5,4},{6,7},{7,6},{8,9},{9,8},{10,11... | collective-permute-start | bytes 1536008 | tf_op jit(solution)/shard_map/ppermute | solution.py:172
  55.8 5.4 %collective-permute-start.14 = (bf16[25,16,640]{2,1,0:T(8,128)(2,1)}, bf16[25,16,640]{2,1,0:T(8,128)(2,1)}, u32[]{:S(2)}, u32[]{:S(2)}) collective-permute-start(bf16[25,16,640]{2,1,0:T(8,128)(2,1)} %collective-permute-done.9.refs_2_), channel_id=1, source_target_pairs={{1,2},{3,4},{5,6},{9,10},{11,12},{13,14},{17,18},{19,20},{21,22},{... | collective-permute-start | bytes 1536008 | tf_op jit(solution)/shard_map/ppermute | solution.py:171
  61.4 0.7 copy-done.2
  62.1 1.7 %shard_map.55.left_ref = bf16[25,160,128]{2,1,0:T(8,128)(2,1)S(1)} custom-call(bf16[25,16,640]{2,1,0:T(8,128)(2,1)S(1)} %reshape.194.own_ref), custom_call_target="tpu_custom_call" | custom-call | bytes 12288000 | tf_op jit(solution)/shard_map/pallas_call | solution.py:65
  63.8 0.2 collective-permute-start.3
  64.0 2.3 %collective-permute-done.13.refs_5_ = bf16[25,16,640]{2,1,0:T(8,128)(2,1)} collective-permute-done((bf16[25,16,640]{2,1,0:T(8,128)(2,1)}, bf16[25,16,640]{2,1,0:T(8,128)(2,1)}, u32[]{:S(2)}, u32[]{:S(2)}) %collective-permute-start.13) | collective-permute-done | bytes 512032 | tf_op jit(solution)/shard_map/ppermute | solution.py:170
  66.3 1.3 %collective-permute-start.6 = (bf16[25,16,640]{2,1,0:T(8,128)(2,1)}, bf16[25,16,640]{2,1,0:T(8,128)(2,1)}, u32[]{:S(2)}, u32[]{:S(2)}) collective-permute-start(bf16[25,16,640]{2,1,0:T(8,128)(2,1)} %copy-done.2), channel_id=1, source_target_pairs={{2,1},{4,3},{6,5},{10,9},{12,11},{14,13},{18,17},{20,19},{22,21},{... | collective-permute-start | bytes 1536008 | tf_op jit(solution)/shard_map/ppermute | solution.py:170
  67.7 5.8 %collective-permute-start.7 = (bf16[25,16,640]{2,1,0:T(8,128)(2,1)}, bf16[25,16,640]{2,1,0:T(8,128)(2,1)}, u32[]{:S(2)}, u32[]{:S(2)}) collective-permute-start(bf16[25,16,640]{2,1,0:T(8,128)(2,1)} %copy-done), channel_id=1, source_target_pairs={{1,2},{3,4},{5,6},{9,10},{11,12},{13,14},{17,18},{19,20},{21,22},{... | collective-permute-start | bytes 1536008 | tf_op jit(solution)/shard_map/ppermute | solution.py:171
  73.5 0.6 gather_fusion
  74.1 8.0 %shard_map.57.refs_7_ = bf16[2,50,400,128]{3,2,1,0:T(8,128)(2,1)} custom-call(s32[2]{0:T(128)S(1)} %gather_fusion, bf16[25,160,128]{2,1,0:T(8,128)(2,1)S(1)} %shard_map.56.left_ref, bf16[25,16,640]{2,1,0:T(8,128)(2,1)} %collective-permute-done.10.refs_0_, bf16[25,16,640]{2,1,0:T(8,128)(2,1)} %collective-permute-done.8.refs_1_, ...), custom_call_target="tpu_custom_call" | custom-call | flops 655360000 | bytes 15360000 | tf_op jit(solution)/shard_map/pallas_call | solution.py:149
  82.2 8.2 %shard_map.58 = bf16[2,50,400,128]{3,2,1,0:T(8,128)(2,1)} custom-call(s32[2]{0:T(128)S(1)} %gather_fusion, bf16[25,160,128]{2,1,0:T(8,128)(2,1)S(1)} %shard_map.55.left_ref, bf16[25,16,640]{2,1,0:T(8,128)(2,1)} %collective-permute-done.3.refs_0_, bf16[25,16,640]{2,1,0:T(8,128)(2,1)S(1)} %copy-done.3, ...), custom_call_target="tpu_custom_call", output_to_operand_aliasing={{}: (9, {})} | custom-call | flops 655360000 | bytes 15360000 | tf_op jit(solution)/shard_map/pallas_call | solution.py:149
  (47 shorter events, 0.9 us)
Async XLA Ops:
  0.0 1.8 %copy-start.4 = (bf16[160,4096]{1,0:T(8,128)(2,1)S(1)}, bf16[160,4096]{1,0:T(8,128)(2,1)}, u32[]{:S(2)}) copy-start(bf16[160,4096]{1,0:T(8,128)(2,1)} %param.5) | copy-start | bytes 3932164
  1.8 1.7 %copy-start.5 = (s32[160]{0:T(256)S(1)}, s32[160]{0:T(256)}, u32[]{:S(2)}) copy-start(s32[160]{0:T(256)} %param.6) | copy-start | bytes 1924
  2.1 7.9 %collective-permute-start = (bf16[160,512]{1,0:T(8,128)(2,1)S(1)}, bf16[160,512]{1,0:T(8,128)(2,1)S(1)}, u32[]{:S(2)}, u32[]{:S(2)}) collective-permute-start(bf16[160,512]{1,0:T(8,128)(2,1)S(1)} %slice.18), channel_id=1, source_target_pairs={{8,0},{16,8},{24,16},{9,1},{17,9},{25,17},{10,2},{18,10},{26,18},{... | collective-permute-start | bytes 491528 | tf_op jit(solution)/shard_map/ppermute | solution.py:23
  26.6 9.1 %all-to-all-start = ((bf16[4,25,4,640]{3,2,1,0:T(4,128)(2,1)}), bf16[4,25,4,640]{3,2,1,0:T(4,128)(2,1)S(1)}, u32[]{:S(2)}, u32[]{:S(2)}) async-start(bf16[4,25,4,640]{3,2,1,0:T(4,128)(2,1)} %get-tuple-element.18), calls=%async_computation | async-start | bytes 1024000 | tf_op jit(solution)/shard_map/all_to_all | solution.py:212
  30.4 16.8 %collective-permute-start.9 = (bf16[25,16,640]{2,1,0:T(8,128)(2,1)S(1)}, bf16[25,16,640]{2,1,0:T(8,128)(2,1)}, u32[]{:S(2)}, u32[]{:S(2)}) collective-permute-start(bf16[25,16,640]{2,1,0:T(8,128)(2,1)S(1)} %reshape.195.own_ref), channel_id=1, source_target_pairs={{0,2},{1,3},{2,4},{3,5},{4,6},{5,7},{8,10},{9,11},{10,12},{11,13},... | collective-permute-start | bytes 1536008 | tf_op jit(solution)/shard_map/ppermute | solution.py:23
  34.4 12.8 %collective-permute-start.8 = (bf16[25,16,640]{2,1,0:T(8,128)(2,1)S(1)}, bf16[25,16,640]{2,1,0:T(8,128)(2,1)}, u32[]{:S(2)}, u32[]{:S(2)}) collective-permute-start(bf16[25,16,640]{2,1,0:T(8,128)(2,1)S(1)} %reshape.195.own_ref), channel_id=1, source_target_pairs={{2,0},{3,1},{4,2},{5,3},{6,4},{7,5},{10,8},{11,9},{12,10},{13,11},... | collective-permute-start | bytes 1536008 | tf_op jit(solution)/shard_map/ppermute | solution.py:23
  36.0 37.4 %copy-start.8 = (s32[2,1]{0,1:T(1,128)S(1)}, s32[2,1]{0,1:T(1,128)}, u32[]{:S(2)}) copy-start(s32[2,1]{0,1:T(1,128)} %param.7) | copy-start | bytes 28
  36.0 37.4 %copy-start.6 = (s32[7]{0:T(128)S(1)}, s32[7]{0:T(128)}, u32[]{:S(2)}) copy-start(s32[7]{0:T(128)} %constant.59.clone) | copy-start | bytes 88
  36.1 37.4 %copy-start.7 = (s32[7]{0:T(128)S(1)}, s32[7]{0:T(128)}, u32[]{:S(2)}) copy-start(s32[7]{0:T(128)} %constant.58.clone) | copy-start | bytes 88
  36.1 19.7 %collective-permute-start.2 = (bf16[25,16,640]{2,1,0:T(8,128)(2,1)S(1)}, bf16[25,16,640]{2,1,0:T(8,128)(2,1)S(1)}, u32[]{:S(2)}, u32[]{:S(2)}) collective-permute-start(bf16[25,16,640]{2,1,0:T(8,128)(2,1)S(1)} %reshape.194.own_ref), channel_id=1, source_target_pairs={{0,2},{1,3},{2,4},{3,5},{4,6},{5,7},{8,10},{9,11},{10,12},{11,13},... | collective-permute-start | bytes 1536008 | tf_op jit(solution)/shard_map/ppermute | solution.py:23
  40.2 21.0 %collective-permute-start.1 = (bf16[25,16,640]{2,1,0:T(8,128)(2,1)S(1)}, bf16[25,16,640]{2,1,0:T(8,128)(2,1)S(1)}, u32[]{:S(2)}, u32[]{:S(2)}) collective-permute-start(bf16[25,16,640]{2,1,0:T(8,128)(2,1)S(1)} %reshape.194.own_ref), channel_id=1, source_target_pairs={{2,0},{3,1},{4,2},{5,3},{6,4},{7,5},{10,8},{11,9},{12,10},{13,11},... | collective-permute-start | bytes 1536008 | tf_op jit(solution)/shard_map/ppermute | solution.py:23
  41.5 22.3 %collective-permute-start.10 = (bf16[25,16,640]{2,1,0:T(8,128)(2,1)S(1)}, bf16[25,16,640]{2,1,0:T(8,128)(2,1)}, u32[]{:S(2)}, u32[]{:S(2)}) collective-permute-start(bf16[25,16,640]{2,1,0:T(8,128)(2,1)S(1)} %reshape.195.own_ref), channel_id=1, source_target_pairs={{0,1},{1,0},{2,3},{3,2},{4,5},{5,4},{6,7},{7,6},{8,9},{9,8},{10,11... | collective-permute-start | bytes 1536008 | tf_op jit(solution)/shard_map/ppermute | solution.py:168
  47.2 19.0 %collective-permute-start.13 = (bf16[25,16,640]{2,1,0:T(8,128)(2,1)}, bf16[25,16,640]{2,1,0:T(8,128)(2,1)}, u32[]{:S(2)}, u32[]{:S(2)}) collective-permute-start(bf16[25,16,640]{2,1,0:T(8,128)(2,1)} %collective-permute-done.8.refs_1_), channel_id=1, source_target_pairs={{2,1},{4,3},{6,5},{10,9},{12,11},{14,13},{18,17},{20,19},{22,21},{... | collective-permute-start | bytes 1536008 | tf_op jit(solution)/shard_map/ppermute | solution.py:170
  48.5 19.0 %collective-permute-start.11 = (bf16[25,16,640]{2,1,0:T(8,128)(2,1)}, bf16[25,16,640]{2,1,0:T(8,128)(2,1)}, u32[]{:S(2)}, u32[]{:S(2)}) collective-permute-start(bf16[25,16,640]{2,1,0:T(8,128)(2,1)} %collective-permute-done.8.refs_1_), channel_id=1, source_target_pairs={{0,1},{1,0},{2,3},{3,2},{4,5},{5,4},{6,7},{7,6},{8,9},{9,8},{10,11... | collective-permute-start | bytes 1536008 | tf_op jit(solution)/shard_map/ppermute | solution.py:172
  55.8 5.4 %copy-start = (bf16[25,16,640]{2,1,0:T(8,128)(2,1)}, bf16[25,16,640]{2,1,0:T(8,128)(2,1)S(1)}, u32[]{:S(2)}) copy-start(bf16[25,16,640]{2,1,0:T(8,128)(2,1)S(1)} %collective-permute-done.2.refs_2_) | copy-start | bytes 1536004
  55.8 11.8 %collective-permute-start.14 = (bf16[25,16,640]{2,1,0:T(8,128)(2,1)}, bf16[25,16,640]{2,1,0:T(8,128)(2,1)}, u32[]{:S(2)}, u32[]{:S(2)}) collective-permute-start(bf16[25,16,640]{2,1,0:T(8,128)(2,1)} %collective-permute-done.9.refs_2_), channel_id=1, source_target_pairs={{1,2},{3,4},{5,6},{9,10},{11,12},{13,14},{17,18},{19,20},{21,22},{... | collective-permute-start | bytes 1536008 | tf_op jit(solution)/shard_map/ppermute | solution.py:171
  61.3 0.8 copy-start.2
  61.3 12.2 %collective-permute-start.12 = (bf16[25,16,640]{2,1,0:T(8,128)(2,1)}, bf16[25,16,640]{2,1,0:T(8,128)(2,1)}, u32[]{:S(2)}, u32[]{:S(2)}) collective-permute-start(bf16[25,16,640]{2,1,0:T(8,128)(2,1)} %collective-permute-done.9.refs_2_), channel_id=1, source_target_pairs={{0,1},{1,0},{2,3},{3,2},{4,5},{5,4},{6,7},{7,6},{8,9},{9,8},{10,11... | collective-permute-start | bytes 1536008 | tf_op jit(solution)/shard_map/ppermute | solution.py:173
  63.8 18.4 %collective-permute-start.3 = (bf16[25,16,640]{2,1,0:T(8,128)(2,1)S(1)}, bf16[25,16,640]{2,1,0:T(8,128)(2,1)}, u32[]{:S(2)}, u32[]{:S(2)}) collective-permute-start(bf16[25,16,640]{2,1,0:T(8,128)(2,1)S(1)} %reshape.194.own_ref), channel_id=1, source_target_pairs={{0,1},{1,0},{2,3},{3,2},{4,5},{5,4},{6,7},{7,6},{8,9},{9,8},{10,11... | collective-permute-start | bytes 1536008 | tf_op jit(solution)/shard_map/ppermute | solution.py:168
  66.3 15.9 %collective-permute-start.6 = (bf16[25,16,640]{2,1,0:T(8,128)(2,1)}, bf16[25,16,640]{2,1,0:T(8,128)(2,1)}, u32[]{:S(2)}, u32[]{:S(2)}) collective-permute-start(bf16[25,16,640]{2,1,0:T(8,128)(2,1)} %copy-done.2), channel_id=1, source_target_pairs={{2,1},{4,3},{6,5},{10,9},{12,11},{14,13},{18,17},{20,19},{22,21},{... | collective-permute-start | bytes 1536008 | tf_op jit(solution)/shard_map/ppermute | solution.py:170
  67.6 14.6 %collective-permute-start.4 = (bf16[25,16,640]{2,1,0:T(8,128)(2,1)}, bf16[25,16,640]{2,1,0:T(8,128)(2,1)}, u32[]{:S(2)}, u32[]{:S(2)}) collective-permute-start(bf16[25,16,640]{2,1,0:T(8,128)(2,1)} %copy-done.2), channel_id=1, source_target_pairs={{0,1},{1,0},{2,3},{3,2},{4,5},{5,4},{6,7},{7,6},{8,9},{9,8},{10,11... | collective-permute-start | bytes 1536008 | tf_op jit(solution)/shard_map/ppermute | solution.py:172
  67.7 14.6 %collective-permute-start.7 = (bf16[25,16,640]{2,1,0:T(8,128)(2,1)}, bf16[25,16,640]{2,1,0:T(8,128)(2,1)}, u32[]{:S(2)}, u32[]{:S(2)}) collective-permute-start(bf16[25,16,640]{2,1,0:T(8,128)(2,1)} %copy-done), channel_id=1, source_target_pairs={{1,2},{3,4},{5,6},{9,10},{11,12},{13,14},{17,18},{19,20},{21,22},{... | collective-permute-start | bytes 1536008 | tf_op jit(solution)/shard_map/ppermute | solution.py:171
  73.4 8.8 %collective-permute-start.5 = (bf16[25,16,640]{2,1,0:T(8,128)(2,1)}, bf16[25,16,640]{2,1,0:T(8,128)(2,1)}, u32[]{:S(2)}, u32[]{:S(2)}) collective-permute-start(bf16[25,16,640]{2,1,0:T(8,128)(2,1)} %copy-done), channel_id=1, source_target_pairs={{0,1},{1,0},{2,3},{3,2},{4,5},{5,4},{6,7},{7,6},{8,9},{9,8},{10,11... | collective-permute-start | bytes 1536008 | tf_op jit(solution)/shard_map/ppermute | solution.py:173
  74.1 8.1 %copy-start.1 = (bf16[25,16,640]{2,1,0:T(8,128)(2,1)S(1)}, bf16[25,16,640]{2,1,0:T(8,128)(2,1)}, u32[]{:S(2)}) copy-start(bf16[25,16,640]{2,1,0:T(8,128)(2,1)} %copy-done) | copy-start | bytes 1536004
  74.1 8.1 %copy-start.3 = (bf16[25,16,640]{2,1,0:T(8,128)(2,1)S(1)}, bf16[25,16,640]{2,1,0:T(8,128)(2,1)}, u32[]{:S(2)}) copy-start(bf16[25,16,640]{2,1,0:T(8,128)(2,1)} %copy-done.2) | copy-start | bytes 1536004

commit v5 on v4

--- a/solution.py
+++ b/solution.py
@@ -85,7 +85,9 @@
     found, refs = refs[:places], refs[places + aliased :]
     out_ref, refs = refs[0], refs[1:]
     held, (partners, sems) = refs[:-2], refs[-2:]
-    batch = found[0].shape[2] // chans
+    twin, above, below, theirs, passed = found
+    found = [twin, above, below, theirs.at[0], theirs.at[1], passed]
+    batch = twin.shape[2] // chans
     reach = chans // batch
     width = batch * chans // LANES
     start = pl.program_id(0) * group
@@ -167,14 +169,14 @@
     below = shifted(own, "chan", 2)
     twin = lax.ppermute(own, "chan", swap)
     above, below, left = lax.optimization_barrier((above, below, make_left(own)))
-    on_down = lax.ppermute(above, "chan", [(b, b - 1) for b in range(2, count, 2)])
-    on_up = lax.ppermute(below, "chan", [(b, b + 1) for b in range(1, count - 1, 2)])
-    twin_above = lax.ppermute(above, "chan", swap)
-    twin_below = lax.ppermute(below, "chan", swap)
-    return left, [twin, above, below, twin_above, twin_below, on_down, on_up]
-
-
-PLACES = ((6, 2, 4, 0, 0, 1, 3), (4, 2, 0, 0, 3, 1, 5))
+    odd = lax.axis_index("chan") % 2 == 1
+    forward = [(b, b + 1 if b % 2 else b - 1) for b in range(1, count - 1)]
+    passed = lax.ppermute(jnp.where(odd, below, above), "chan", forward)
+    theirs = lax.ppermute(jnp.stack([above, below], axis=0), "chan", swap)
+    return left, [twin, above, below, theirs, passed]
+
+
+PLACES = ((5, 2, 4, 0, 0, 1, 3), (4, 2, 0, 0, 3, 1, 5))
 
 
 def per_device(record, valid, pairs):

time: 91.3 us -> 98.7 us (1.081)
  starting transfers between devices: 40.9 us -> 28.4 us
  waiting for transfers between devices: 4.92 us -> 14.4 us
  other arithmetic: 6.02 us -> 9.91 us
  Pallas kernels: 19.7 us -> 23.4 us
  local copies, waits for them, and re-layouts: 7.59 us -> 10.3 us
    ppermute x8 -> x4, starting transfers between devices: 21.2 us -> 9.81 us  [the longest x2 5.54 us: fetch_band(): passed = lax.ppermute(jnp.where(odd, below, above), 'chan', forward)]
    ppermute x8 -> x4, waiting for transfers between devices: 2.31 us -> 8.24 us  [the longest x2 8.23 us: fetch_band(): passed = lax.ppermute(jnp.where(odd, below, above), 'chan', forward)]
    pallas_call x2, Pallas kernels: 3.43 us -> 7.54 us  [turned_own(): pl.pallas_call(functools.partial(turn_kernel, half), grid=(freqs // group...]
    ppermute x5, waiting for transfers between devices: 2.6 us -> 6.11 us  [shifted(): lax.ppermute(value, axis, [(source, source + steps) for source in range(i...]
    another operation x1 -> x3, other arithmetic: 3.78 us -> 5.91 us
    select_n x0 -> x2, other arithmetic: none -> 1.76 us  [fetch_band(): passed = lax.ppermute(jnp.where(odd, below, above), 'chan', forward)]
    reshape x2, local copies, waits for them, and re-layouts: 0.24 us -> 1.84 us  [per_device(): got.transpose(1, 0, 2, 3)]
    unnamed x18, local copies, waits for them, and re-layouts: 0.73 us -> 1.85 us
  transfers between devices with their start and end apart: 16 -> 12, of which waited for: 2 -> 3; matrix products, arithmetic and copies ran while one was open for 6% -> 11% of each run, Pallas kernels for 13% -> 16%
where the time goes in v5:
time: 98.7 us; the launch traced here: 97.8 us
  starting transfers between devices  28.4 us (29%)
  Pallas kernels  23.4 us (24%)
  waiting for transfers between devices  14.4 us (15%)
  local copies, waits for them, and re-layouts  10.3 us (10%)
  other arithmetic  9.91 us (10%)
  blocking collectives  9.4 us (10%)
  matrix products  1.58 us (2%)
    pallas_call x2, Pallas kernels, cross_stacks(): pl.pallas_call(functools.partial(gram_kernel, factor, len(found), len(ext...  15.9 us
    ppermute x5, starting transfers between devices, shifted(): lax.ppermute(value, axis, [(source, source + steps) for source in range(i...  11.1 us
    all_to_all x1, blocking collectives, per_device(): lax.all_to_all(packed[:, first:last], 'seg', split_axis=0, concat_axis=0,...  9.4 us
    ppermute x2, waiting for transfers between devices, fetch_band(): passed = lax.ppermute(jnp.where(odd, below, above), 'chan', forward)  8.23 us
    pallas_call x2, Pallas kernels, turned_own(): pl.pallas_call(functools.partial(turn_kernel, half), grid=(freqs // group...  7.54 us
    ppermute x5, waiting for transfers between devices, shifted(): lax.ppermute(value, axis, [(source, source + steps) for source in range(i...  6.11 us
    ppermute x2, starting transfers between devices, fetch_band(): passed = lax.ppermute(jnp.where(odd, below, above), 'chan', forward)  5.54 us
    ppermute x2, starting transfers between devices, fetch_band(): theirs = lax.ppermute(jnp.stack([above, below], axis=0), 'chan', swap)  4.27 us
  transfers between devices with their start and end apart: 12, of which 3 were waited for; matrix products, arithmetic and copies ran while one was open for 11% of the time, Pallas kernels for 16%

profile of v5, /device:TPU:1, one launch (start us, length us, event | category | flops | bytes accessed | tf_op | source)
XLA Modules:
  0.0 97.8 jit_solution(2785428487019917224)
XLA Ops:
  0.0 1.8 %fusion = f32[160]{0:T(256)S(1)} fusion(bf16[160,4096]{1,0:T(8,128)(2,1)} %param.5), kind=kLoop, calls=%fused_computation.3 | loop fusion | flops 1965920 | bytes 1311360 | tf_op jit(solution)/shard_map/reduce_sum | solution.py:186
  2.1 1.3 %collective-permute-start = (bf16[160,512]{1,0:T(8,128)(2,1)S(1)}, bf16[160,512]{1,0:T(8,128)(2,1)S(1)}, u32[]{:S(2)}, u32[]{:S(2)}) collective-permute-start(bf16[160,512]{1,0:T(8,128)(2,1)S(1)} %slice.18), channel_id=1, source_target_pairs={{8,0},{16,8},{24,16},{9,1},{17,9},{25,17},{10,2},{18,10},{26,18},{... | collective-permute-start | bytes 491528 | tf_op jit(solution)/shard_map/ppermute | solution.py:23
  3.6 3.8 %multiply_convert_fusion.2 = (bf16[1024,1,200]{0,2,1:T(8,128)(2,1)S(1)}, bf16[1024,1,200]{0,2,1:T(8,128)(2,1)S(1)}) fusion(s32[200]{0:T(256)S(1)} %iota_add_fusion, f32[1024]{0:T(1024)S(1)} %get-tuple-element.21, f32[1024]{0:T(1024)S(1)} %get-tuple-element.22), kind=kLoop, calls=%fused_computation.26 | loop fusion | flops 4096000 | bytes 828192 | tf_op jit(solution)/shard_map/convert
  7.4 2.6 %collective-permute-done = bf16[160,512]{1,0:T(8,128)(2,1)S(1)} collective-permute-done((bf16[160,512]{1,0:T(8,128)(2,1)S(1)}, bf16[160,512]{1,0:T(8,128)(2,1)S(1)}, u32[]{:S(2)}, u32[]{:S(2)}) %collective-permute-start) | collective-permute-done | bytes 163872 | tf_op jit(solution)/shard_map/ppermute | solution.py:23
  10.2 1.6 %fusion.5 = bf16[8,2,200,160]{2,3,0,1:T(8,128)(2,1)S(1)} fusion(bf16[160,8,512]{2,0,1:T(8,128)(2,1)S(1)} %bitcast.48, bf16[160,8,512]{2,0,1:T(8,128)(2,1)S(1)} %bitcast.47, f32[160]{0:T(256)S(1)} %convert_element_type.48, bf16[1024,1,200]{0,2,1:T(8,128)(2,1)S(1)} %get-tuple-element.20, bf16[1024,1,200]{0,2,1:T(8,128)(2,1)S(1)} %get-tuple-element.19), kind=kOutput, calls=%fused_computation.10 | convolution fusion | flops 1056481280 | bytes 4465280 | tf_op jit(solution)/shard_map/cwk,kpf->wpfc/dot_general | solution.py:197
  11.8 1.6 %copy.15 = bf16[8,2,200,160]{3,1,2,0:T(2,128)(2,1)S(1)} copy(bf16[8,2,200,160]{2,3,0,1:T(8,128)(2,1)S(1)} %fusion.5) | data formatting | bytes 2048000 | tf_op jit(solution)/shard_map/convert_element_type | solution.py:199
  13.4 1.3 %copy.16 = bf16[4,50,2,2,4,160]{5,4,3,2,1,0:T(4,128)(2,1)S(1)} copy(bf16[4,50,2,2,4,160]{5,2,1,0,4,3:T(2,128)(2,1)S(1)} %bitcast.43) | data formatting | bytes 2048000 | tf_op jit(solution)/shard_map/transpose | solution.py:205
  14.6 1.4 %reshape.193 = bf16[4,50,4,640]{3,2,1,0:T(4,128)(2,1)S(1)} reshape(bf16[4,50,2,2,4,160]{5,4,3,2,1,0:T(4,128)(2,1)S(1)} %copy.16) | data formatting | bytes 2048000 | tf_op jit(solution)/shard_map/reshape | solution.py:205
  16.1 1.1 %fusion.17 = (bf16[4,25,4,640]{3,2,1,0:T(4,128)(2,1)}, bf16[4,25,4,640]{3,2,1,0:T(4,128)(2,1)S(1)}) fusion(bf16[4,50,4,640]{3,2,1,0:T(4,128)(2,1)S(1)} %reshape.193), kind=kLoop, calls=%fused_computation.41 | loop fusion | bytes 2048000 | tf_op jit(solution)/shard_map/slice | solution.py:214
  17.2 9.4 %all_to_all.10 = bf16[4,25,4,640]{3,2,1,0:T(4,128)(2,1)S(1)} all-to-all(bf16[4,25,4,640]{3,2,1,0:T(4,128)(2,1)S(1)} %get-tuple-element.18), channel_id=1, replica_groups=mesh['seg'=4,'chan'=8] {'seg'}, dimensions={0} | all-to-all | bytes 1024000 | tf_op jit(solution)/shard_map/all_to_all | solution.py:214
  26.6 3.5 %all-to-all-start.1 = ((bf16[4,25,4,640]{3,2,1,0:T(4,128)(2,1)}), bf16[4,25,4,640]{3,2,1,0:T(4,128)(2,1)S(1)}, u32[]{:S(2)}, u32[]{:S(2)}) async-start(bf16[4,25,4,640]{3,2,1,0:T(4,128)(2,1)} %get-tuple-element.17), calls=%async_computation.1 | async-start | bytes 1024000 | tf_op jit(solution)/shard_map/all_to_all | solution.py:214
  30.3 0.9 reshape.194.own_ref
  31.2 3.2 %collective-permute-start.2 = (bf16[25,16,640]{2,1,0:T(8,128)(2,1)}, bf16[25,16,640]{2,1,0:T(8,128)(2,1)S(1)}, u32[]{:S(2)}, u32[]{:S(2)}) collective-permute-start(bf16[25,16,640]{2,1,0:T(8,128)(2,1)} %reshape.194.own_ref), channel_id=1, source_target_pairs={{0,2},{1,3},{2,4},{3,5},{4,6},{5,7},{8,10},{9,11},{10,12},{11,13},... | collective-permute-start | bytes 1536008 | tf_op jit(solution)/shard_map/ppermute | solution.py:23
  34.5 1.3 %collective-permute-start.1 = (bf16[25,16,640]{2,1,0:T(8,128)(2,1)}, bf16[25,16,640]{2,1,0:T(8,128)(2,1)S(1)}, u32[]{:S(2)}, u32[]{:S(2)}) collective-permute-start(bf16[25,16,640]{2,1,0:T(8,128)(2,1)} %reshape.194.own_ref), channel_id=1, source_target_pairs={{2,0},{3,1},{4,2},{5,3},{6,4},{7,5},{10,8},{11,9},{12,10},{13,11},... | collective-permute-start | bytes 1536008 | tf_op jit(solution)/shard_map/ppermute | solution.py:23
  35.9 0.9 reshape.195.own_ref
  36.9 4.0 %collective-permute-start.7 = (bf16[25,16,640]{2,1,0:T(8,128)(2,1)}, bf16[25,16,640]{2,1,0:T(8,128)(2,1)S(1)}, u32[]{:S(2)}, u32[]{:S(2)}) collective-permute-start(bf16[25,16,640]{2,1,0:T(8,128)(2,1)} %reshape.195.own_ref), channel_id=1, source_target_pairs={{0,2},{1,3},{2,4},{3,5},{4,6},{5,7},{8,10},{9,11},{10,12},{11,13},... | collective-permute-start | bytes 1536008 | tf_op jit(solution)/shard_map/ppermute | solution.py:23
  40.9 1.3 %collective-permute-start.6 = (bf16[25,16,640]{2,1,0:T(8,128)(2,1)}, bf16[25,16,640]{2,1,0:T(8,128)(2,1)S(1)}, u32[]{:S(2)}, u32[]{:S(2)}) collective-permute-start(bf16[25,16,640]{2,1,0:T(8,128)(2,1)} %reshape.195.own_ref), channel_id=1, source_target_pairs={{2,0},{3,1},{4,2},{5,3},{6,4},{7,5},{10,8},{11,9},{12,10},{13,11},... | collective-permute-start | bytes 1536008 | tf_op jit(solution)/shard_map/ppermute | solution.py:23
  42.2 4.0 %collective-permute-start.3 = (bf16[25,16,640]{2,1,0:T(8,128)(2,1)}, bf16[25,16,640]{2,1,0:T(8,128)(2,1)}, u32[]{:S(2)}, u32[]{:S(2)}) collective-permute-start(bf16[25,16,640]{2,1,0:T(8,128)(2,1)} %reshape.194.own_ref), channel_id=1, source_target_pairs={{0,1},{1,0},{2,3},{3,2},{4,5},{5,4},{6,7},{7,6},{8,9},{9,8},{10,11... | collective-permute-start | bytes 1536008 | tf_op jit(solution)/shard_map/ppermute | solution.py:170
  46.2 3.7 %shard_map.55.left_ref = bf16[25,160,128]{2,1,0:T(8,128)(2,1)S(1)} custom-call(bf16[25,16,640]{2,1,0:T(8,128)(2,1)} %reshape.194.own_ref), custom_call_target="tpu_custom_call" | custom-call | bytes 12288000 | tf_op jit(solution)/shard_map/pallas_call | solution.py:65
  49.9 3.8 %shard_map.56.left_ref = bf16[25,160,128]{2,1,0:T(8,128)(2,1)S(1)} custom-call(bf16[25,16,640]{2,1,0:T(8,128)(2,1)} %reshape.195.own_ref), custom_call_target="tpu_custom_call" | custom-call | bytes 12288000 | tf_op jit(solution)/shard_map/pallas_call | solution.py:65
  53.8 3.5 %collective-permute-done.6.refs_1_ = bf16[25,16,640]{2,1,0:T(8,128)(2,1)S(1)} collective-permute-done((bf16[25,16,640]{2,1,0:T(8,128)(2,1)}, bf16[25,16,640]{2,1,0:T(8,128)(2,1)S(1)}, u32[]{:S(2)}, u32[]{:S(2)}) %collective-permute-start.6) | collective-permute-done | bytes 512032 | tf_op jit(solution)/shard_map/ppermute | solution.py:23
  57.3 1.1 %pad_maximum_fusion.2 = bf16[2,25,16,640]{3,2,1,0:T(8,128)(2,1)} fusion(bf16[1,25,16,640]{3,2,1,0:T(8,128)(2,1)S(1)} %bitcast.38, bf16[1,25,16,640]{3,2,1,0:T(8,128)(2,1)S(1)} %bitcast.39), kind=kLoop, calls=%fused_computation.18 | loop fusion | flops 512000 | bytes 2048000 | tf_op jit(solution)/shard_map/stack | solution.py:175
  58.4 4.3 %collective-permute-start.9 = (bf16[2,25,16,640]{3,2,1,0:T(8,128)(2,1)}, bf16[2,25,16,640]{3,2,1,0:T(8,128)(2,1)}, u32[]{:S(2)}, u32[]{:S(2)}) collective-permute-start(bf16[2,25,16,640]{3,2,1,0:T(8,128)(2,1)} %pad_maximum_fusion.2), channel_id=1, source_target_pairs={{0,1},{1,0},{2,3},{3,2},{4,5},{5,4},{6,7},{7,6},{8,9},{9,8},{10,11... | collective-permute-start | bytes 3072008 | tf_op jit(solution)/shard_map/ppermute | solution.py:175
  62.7 1.1 %pad_maximum_fusion.1 = bf16[2,25,16,640]{3,2,1,0:T(8,128)(2,1)} fusion(bf16[1,25,16,640]{3,2,1,0:T(8,128)(2,1)S(1)} %bitcast.40, bf16[1,25,16,640]{3,2,1,0:T(8,128)(2,1)S(1)} %bitcast.41), kind=kLoop, calls=%fused_computation.17 | loop fusion | flops 512000 | bytes 2048000 | tf_op jit(solution)/shard_map/stack | solution.py:175
  63.8 0.9 broadcast_select_fusion.1
  64.7 3.5 %collective-permute-start.5 = (bf16[25,16,640]{2,1,0:T(8,128)(2,1)}, bf16[25,16,640]{2,1,0:T(8,128)(2,1)}, u32[]{:S(2)}, u32[]{:S(2)}) collective-permute-start(bf16[25,16,640]{2,1,0:T(8,128)(2,1)} %broadcast_select_fusion.1), channel_id=1, source_target_pairs={{1,2},{2,1},{3,4},{4,3},{5,6},{6,5},{9,10},{10,9},{11,12},{12,11},... | collective-permute-start | bytes 1536008 | tf_op jit(solution)/shard_map/ppermute | solution.py:174
  68.2 0.9 broadcast_select_fusion
  69.9 2.0 %collective-permute-start.10 = (bf16[25,16,640]{2,1,0:T(8,128)(2,1)}, bf16[25,16,640]{2,1,0:T(8,128)(2,1)}, u32[]{:S(2)}, u32[]{:S(2)}) collective-permute-start(bf16[25,16,640]{2,1,0:T(8,128)(2,1)} %broadcast_select_fusion), channel_id=1, source_target_pairs={{1,2},{2,1},{3,4},{4,3},{5,6},{6,5},{9,10},{10,9},{11,12},{12,11},... | collective-permute-start | bytes 1536008 | tf_op jit(solution)/shard_map/ppermute | solution.py:174
  72.6 8.2 %collective-permute-done.10.refs_4_ = bf16[25,16,640]{2,1,0:T(8,128)(2,1)} collective-permute-done((bf16[25,16,640]{2,1,0:T(8,128)(2,1)}, bf16[25,16,640]{2,1,0:T(8,128)(2,1)}, u32[]{:S(2)}, u32[]{:S(2)}) %collective-permute-start.10) | collective-permute-done | bytes 512032 | tf_op jit(solution)/shard_map/ppermute | solution.py:174
  80.8 1.0 %copy-done.3 = bf16[25,16,640]{2,1,0:T(8,128)(2,1)S(1)} copy-done((bf16[25,16,640]{2,1,0:T(8,128)(2,1)S(1)}, bf16[25,16,640]{2,1,0:T(8,128)(2,1)}, u32[]{:S(2)}) %copy-start.3) | copy-done | bytes 512024
  81.9 7.7 %shard_map.57.refs_5_ = bf16[2,50,400,128]{3,2,1,0:T(8,128)(2,1)} custom-call(s32[2]{0:T(128)S(1)} %gather_fusion, bf16[25,160,128]{2,1,0:T(8,128)(2,1)S(1)} %shard_map.56.left_ref, bf16[25,16,640]{2,1,0:T(8,128)(2,1)S(1)} %copy-done.3, bf16[25,16,640]{2,1,0:T(8,128)(2,1)S(1)} %collective-permute-done.6.refs_1_, ...), custom_call_target="tpu_custom_call" | custom-call | flops 655360000 | bytes 15360000 | tf_op jit(solution)/shard_map/pallas_call | solution.py:151
  89.6 8.2 %shard_map.58 = bf16[2,50,400,128]{3,2,1,0:T(8,128)(2,1)} custom-call(s32[2]{0:T(128)S(1)} %gather_fusion, bf16[25,160,128]{2,1,0:T(8,128)(2,1)S(1)} %copy-done.1, bf16[25,16,640]{2,1,0:T(8,128)(2,1)} %collective-permute-done.3.refs_0_, bf16[25,16,640]{2,1,0:T(8,128)(2,1)S(1)} %collective-permute-done.1.refs_1_, ...), custom_call_target="tpu_custom_call", output_to_operand_aliasing={{}: (7, {})} | custom-call | flops 655360000 | bytes 15360000 | tf_op jit(solution)/shard_map/pallas_call | solution.py:151
  (43 shorter events, 2.6 us)
Async XLA Ops:
  0.0 1.8 %copy-start.4 = (bf16[160,4096]{1,0:T(8,128)(2,1)S(1)}, bf16[160,4096]{1,0:T(8,128)(2,1)}, u32[]{:S(2)}) copy-start(bf16[160,4096]{1,0:T(8,128)(2,1)} %param.5) | copy-start | bytes 3932164
  1.8 1.7 %copy-start.5 = (s32[160]{0:T(256)S(1)}, s32[160]{0:T(256)}, u32[]{:S(2)}) copy-start(s32[160]{0:T(256)} %param.6) | copy-start | bytes 1924
  2.1 7.9 %collective-permute-start = (bf16[160,512]{1,0:T(8,128)(2,1)S(1)}, bf16[160,512]{1,0:T(8,128)(2,1)S(1)}, u32[]{:S(2)}, u32[]{:S(2)}) collective-permute-start(bf16[160,512]{1,0:T(8,128)(2,1)S(1)} %slice.18), channel_id=1, source_target_pairs={{8,0},{16,8},{24,16},{9,1},{17,9},{25,17},{10,2},{18,10},{26,18},{... | collective-permute-start | bytes 491528 | tf_op jit(solution)/shard_map/ppermute | solution.py:23
  26.6 9.1 %all-to-all-start.1 = ((bf16[4,25,4,640]{3,2,1,0:T(4,128)(2,1)}), bf16[4,25,4,640]{3,2,1,0:T(4,128)(2,1)S(1)}, u32[]{:S(2)}, u32[]{:S(2)}) async-start(bf16[4,25,4,640]{3,2,1,0:T(4,128)(2,1)} %get-tuple-element.17), calls=%async_computation.1 | async-start | bytes 1024000 | tf_op jit(solution)/shard_map/all_to_all | solution.py:214
  31.2 22.5 %collective-permute-start.2 = (bf16[25,16,640]{2,1,0:T(8,128)(2,1)}, bf16[25,16,640]{2,1,0:T(8,128)(2,1)S(1)}, u32[]{:S(2)}, u32[]{:S(2)}) collective-permute-start(bf16[25,16,640]{2,1,0:T(8,128)(2,1)} %reshape.194.own_ref), channel_id=1, source_target_pairs={{0,2},{1,3},{2,4},{3,5},{4,6},{5,7},{8,10},{9,11},{10,12},{11,13},... | collective-permute-start | bytes 1536008 | tf_op jit(solution)/shard_map/ppermute | solution.py:23
  34.5 19.4 %collective-permute-start.1 = (bf16[25,16,640]{2,1,0:T(8,128)(2,1)}, bf16[25,16,640]{2,1,0:T(8,128)(2,1)S(1)}, u32[]{:S(2)}, u32[]{:S(2)}) collective-permute-start(bf16[25,16,640]{2,1,0:T(8,128)(2,1)} %reshape.194.own_ref), channel_id=1, source_target_pairs={{2,0},{3,1},{4,2},{5,3},{6,4},{7,5},{10,8},{11,9},{12,10},{13,11},... | collective-permute-start | bytes 1536008 | tf_op jit(solution)/shard_map/ppermute | solution.py:23
  36.9 17.0 %collective-permute-start.7 = (bf16[25,16,640]{2,1,0:T(8,128)(2,1)}, bf16[25,16,640]{2,1,0:T(8,128)(2,1)S(1)}, u32[]{:S(2)}, u32[]{:S(2)}) collective-permute-start(bf16[25,16,640]{2,1,0:T(8,128)(2,1)} %reshape.195.own_ref), channel_id=1, source_target_pairs={{0,2},{1,3},{2,4},{3,5},{4,6},{5,7},{8,10},{9,11},{10,12},{11,13},... | collective-permute-start | bytes 1536008 | tf_op jit(solution)/shard_map/ppermute | solution.py:23
  40.9 16.5 %collective-permute-start.6 = (bf16[25,16,640]{2,1,0:T(8,128)(2,1)}, bf16[25,16,640]{2,1,0:T(8,128)(2,1)S(1)}, u32[]{:S(2)}, u32[]{:S(2)}) collective-permute-start(bf16[25,16,640]{2,1,0:T(8,128)(2,1)} %reshape.195.own_ref), channel_id=1, source_target_pairs={{2,0},{3,1},{4,2},{5,3},{6,4},{7,5},{10,8},{11,9},{12,10},{13,11},... | collective-permute-start | bytes 1536008 | tf_op jit(solution)/shard_map/ppermute | solution.py:23
  42.2 47.4 %collective-permute-start.3 = (bf16[25,16,640]{2,1,0:T(8,128)(2,1)}, bf16[25,16,640]{2,1,0:T(8,128)(2,1)}, u32[]{:S(2)}, u32[]{:S(2)}) collective-permute-start(bf16[25,16,640]{2,1,0:T(8,128)(2,1)} %reshape.194.own_ref), channel_id=1, source_target_pairs={{0,1},{1,0},{2,3},{3,2},{4,5},{5,4},{6,7},{7,6},{8,9},{9,8},{10,11... | collective-permute-start | bytes 1536008 | tf_op jit(solution)/shard_map/ppermute | solution.py:170
  49.9 8.5 %copy-start = (bf16[25,160,128]{2,1,0:T(8,128)(2,1)}, bf16[25,160,128]{2,1,0:T(8,128)(2,1)S(1)}, u32[]{:S(2)}) copy-start(bf16[25,160,128]{2,1,0:T(8,128)(2,1)S(1)} %shard_map.55.left_ref) | copy-start | bytes 3072004
  53.7 15.3 %collective-permute-start.8 = (bf16[25,16,640]{2,1,0:T(8,128)(2,1)}, bf16[25,16,640]{2,1,0:T(8,128)(2,1)S(1)}, u32[]{:S(2)}, u32[]{:S(2)}) collective-permute-start(bf16[25,16,640]{2,1,0:T(8,128)(2,1)} %reshape.195.own_ref), channel_id=1, source_target_pairs={{0,1},{1,0},{2,3},{3,2},{4,5},{5,4},{6,7},{7,6},{8,9},{9,8},{10,11... | collective-permute-start | bytes 1536008 | tf_op jit(solution)/shard_map/ppermute | solution.py:170
  58.4 22.4 %collective-permute-start.9 = (bf16[2,25,16,640]{3,2,1,0:T(8,128)(2,1)}, bf16[2,25,16,640]{3,2,1,0:T(8,128)(2,1)}, u32[]{:S(2)}, u32[]{:S(2)}) collective-permute-start(bf16[2,25,16,640]{3,2,1,0:T(8,128)(2,1)} %pad_maximum_fusion.2), channel_id=1, source_target_pairs={{0,1},{1,0},{2,3},{3,2},{4,5},{5,4},{6,7},{7,6},{8,9},{9,8},{10,11... | collective-permute-start | bytes 3072008 | tf_op jit(solution)/shard_map/ppermute | solution.py:175
  63.7 8.1 %copy-start.8 = (s32[2,1]{0,1:T(1,128)S(1)}, s32[2,1]{0,1:T(1,128)}, u32[]{:S(2)}) copy-start(s32[2,1]{0,1:T(1,128)} %param.7) | copy-start | bytes 28
  63.7 8.2 %copy-start.6 = (s32[7]{0:T(128)S(1)}, s32[7]{0:T(128)}, u32[]{:S(2)}) copy-start(s32[7]{0:T(128)} %constant.63.clone) | copy-start | bytes 88
  63.7 8.2 %copy-start.7 = (s32[7]{0:T(128)S(1)}, s32[7]{0:T(128)}, u32[]{:S(2)}) copy-start(s32[7]{0:T(128)} %constant.62.clone) | copy-start | bytes 88
  63.8 25.8 %collective-permute-start.4 = (bf16[2,25,16,640]{3,2,1,0:T(8,128)(2,1)}, bf16[2,25,16,640]{3,2,1,0:T(8,128)(2,1)}, u32[]{:S(2)}, u32[]{:S(2)}) collective-permute-start(bf16[2,25,16,640]{3,2,1,0:T(8,128)(2,1)} %pad_maximum_fusion.1), channel_id=1, source_target_pairs={{0,1},{1,0},{2,3},{3,2},{4,5},{5,4},{6,7},{7,6},{8,9},{9,8},{10,11... | collective-permute-start | bytes 3072008 | tf_op jit(solution)/shard_map/ppermute | solution.py:175
  64.7 24.9 %collective-permute-start.5 = (bf16[25,16,640]{2,1,0:T(8,128)(2,1)}, bf16[25,16,640]{2,1,0:T(8,128)(2,1)}, u32[]{:S(2)}, u32[]{:S(2)}) collective-permute-start(bf16[25,16,640]{2,1,0:T(8,128)(2,1)} %broadcast_select_fusion.1), channel_id=1, source_target_pairs={{1,2},{2,1},{3,4},{4,3},{5,6},{6,5},{9,10},{10,9},{11,12},{12,11},... | collective-permute-start | bytes 1536008 | tf_op jit(solution)/shard_map/ppermute | solution.py:174
  69.1 0.8 copy-start.2
  69.9 10.9 %collective-permute-start.10 = (bf16[25,16,640]{2,1,0:T(8,128)(2,1)}, bf16[25,16,640]{2,1,0:T(8,128)(2,1)}, u32[]{:S(2)}, u32[]{:S(2)}) collective-permute-start(bf16[25,16,640]{2,1,0:T(8,128)(2,1)} %broadcast_select_fusion), channel_id=1, source_target_pairs={{1,2},{2,1},{3,4},{4,3},{5,6},{6,5},{9,10},{10,9},{11,12},{12,11},... | collective-permute-start | bytes 1536008 | tf_op jit(solution)/shard_map/ppermute | solution.py:174
  72.6 17.0 %copy-start.1 = (bf16[25,160,128]{2,1,0:T(8,128)(2,1)S(1)}, bf16[25,160,128]{2,1,0:T(8,128)(2,1)}, u32[]{:S(2)}) copy-start(bf16[25,160,128]{2,1,0:T(8,128)(2,1)} %copy-done) | copy-start | bytes 3072004
  80.8 1.0 %copy-start.3 = (bf16[25,16,640]{2,1,0:T(8,128)(2,1)S(1)}, bf16[25,16,640]{2,1,0:T(8,128)(2,1)}, u32[]{:S(2)}) copy-start(bf16[25,16,640]{2,1,0:T(8,128)(2,1)} %copy-done.2) | copy-start | bytes 1536004

commit v6 on v4

--- a/solution.py
+++ b/solution.py
@@ -163,18 +163,20 @@
 def fetch_band(own, make_left):
     count = lax.axis_size("chan")
     swap = [(b, b ^ 1) for b in range(count)]
-    above = shifted(own, "chan", -2)
-    below = shifted(own, "chan", 2)
+    ahead = [1 - 2 * (b % 2) for b in range(count)]
+    moves = [[(b + k * ahead[b], b) for b in range(count)] for k in (2, -2, -1)]
+    near, far, along = [[(a, b) for a, b in move if 0 <= a < count] for move in moves]
+    second = lax.ppermute(own, "chan", near)
+    behind = lax.ppermute(own, "chan", far)
     twin = lax.ppermute(own, "chan", swap)
-    above, below, left = lax.optimization_barrier((above, below, make_left(own)))
-    on_down = lax.ppermute(above, "chan", [(b, b - 1) for b in range(2, count, 2)])
-    on_up = lax.ppermute(below, "chan", [(b, b + 1) for b in range(1, count - 1, 2)])
-    twin_above = lax.ppermute(above, "chan", swap)
-    twin_below = lax.ppermute(below, "chan", swap)
-    return left, [twin, above, below, twin_above, twin_below, on_down, on_up]
-
-
-PLACES = ((6, 2, 4, 0, 0, 1, 3), (4, 2, 0, 0, 3, 1, 5))
+    second, behind, left = lax.optimization_barrier((second, behind, make_left(own)))
+    passed = lax.ppermute(second, "chan", along)
+    twin_second = lax.ppermute(second, "chan", swap)
+    twin_behind = lax.ppermute(behind, "chan", swap)
+    return left, [twin, second, behind, twin_second, twin_behind, passed]
+
+
+PLACES = (5, 2, 3, 0, 0, 1, 4)
 
 
 def per_device(record, valid, pairs):
@@ -202,8 +204,10 @@
     split = spectra.reshape(half, batch, 2, segs, freqs, channels)
     packed = split.transpose(3, 4, 2, 0, 1, 5).reshape(segs, freqs, 2 * half, batch * channels)
     block = lax.axis_index("chan")
-    row = jnp.where(block % 2 == 1, jnp.array(PLACES[1]), jnp.array(PLACES[0]))
-    chosen = row[pairs[:, 0] - block + BAND].astype(jnp.int32)
+    offset = (pairs[:, 0] - block) * (1 - 2 * (block % 2))
+    chosen = jnp.zeros_like(offset)
+    for reach_k, place in zip(range(-BAND, BAND + 1), PLACES):
+        chosen = jnp.where(offset == reach_k, place, chosen)
     factor = 1.0 / math.sqrt(segs * windows)
     group = freq_group(freqs)
     cut = pl.cdiv(freqs // group, 2) * group

time: 91.3 us -> 87 us (0.953)
  starting transfers between devices: 40.9 us -> 27.5 us
  blocking collectives: 9.4 us -> 17.8 us
  local copies, waits for them, and re-layouts: 7.59 us -> 10.9 us
  waiting for transfers between devices: 4.92 us -> 2.62 us
    ppermute x5 -> x1, starting transfers between devices: 12 us -> 1.29 us  [shifted(): lax.ppermute(value, axis, [(source, source + steps) for source in range(i...]
    all_to_all x1 -> x2, blocking collectives: 9.4 us -> 17.8 us  [per_device(): lax.all_to_all(packed[:, first:last], 'seg', split_axis=0, concat_axis=0,...]
    unnamed x18, local copies, waits for them, and re-layouts: 0.73 us -> 5.48 us
    all_to_all x1 -> x0, starting transfers between devices: 3.47 us -> none  [per_device(): lax.all_to_all(packed[:, first:last], 'seg', split_axis=0, concat_axis=0,...]
    ppermute x8 -> x10, waiting for transfers between devices: 2.31 us -> 0.03 us  [the longest x2 0.01 us: fetch_band(): second = lax.ppermute(own, 'chan', near)]
    ppermute x2, starting transfers between devices: 4.14 us -> 5.36 us  [fetch_band(): twin = lax.ppermute(own, 'chan', swap)]
    ppermute x8 -> x10, starting transfers between devices: 21.2 us -> 20.8 us  [the longest x2 9.61 us: fetch_band(): second = lax.ppermute(own, 'chan', near)]
    ppermute x5 -> x1, waiting for transfers between devices: 2.6 us -> 2.59 us  [shifted(): lax.ppermute(value, axis, [(source, source + steps) for source in range(i...]
  transfers between devices with their start and end apart: 16 -> 13, of which waited for: 2 -> 1; matrix products, arithmetic and copies ran while one was open for 6% -> 5% of each run, Pallas kernels for 13% -> 13%
where the time goes in v6:
time: 87 us; the launch traced here: 86 us
  starting transfers between devices  27.5 us (32%)
  Pallas kernels  19.3 us (22%)
  blocking collectives  17.8 us (20%)
  local copies, waits for them, and re-layouts  10.9 us (13%)
  other arithmetic  6.01 us (7%)
  waiting for transfers between devices  2.62 us (3%)
  matrix products  1.58 us (2%)
    all_to_all x2, blocking collectives, per_device(): lax.all_to_all(packed[:, first:last], 'seg', split_axis=0, concat_axis=0,...  17.8 us
    pallas_call x2, Pallas kernels, cross_stacks(): pl.pallas_call(functools.partial(gram_kernel, factor, len(found), len(ext...  15.9 us
    ppermute x2, starting transfers between devices, fetch_band(): second = lax.ppermute(own, 'chan', near)  9.61 us
    ppermute x2, starting transfers between devices, fetch_band(): passed = lax.ppermute(second, 'chan', along)  8.18 us
    unnamed x18, local copies, waits for them, and re-layouts  5.48 us
    ppermute x2, starting transfers between devices, fetch_band(): twin = lax.ppermute(own, 'chan', swap)  5.36 us
    another operation x1, other arithmetic  3.78 us
    pallas_call x2, Pallas kernels, turned_own(): pl.pallas_call(functools.partial(turn_kernel, half), grid=(freqs // group...  3.43 us
  transfers between devices with their start and end apart: 13, of which 1 were waited for; matrix products, arithmetic and copies ran while one was open for 5% of the time, Pallas kernels for 13%

profile of v6, /device:TPU:1, one launch (start us, length us, event | category | flops | bytes accessed | tf_op | source)
XLA Modules:
  0.0 86.0 jit_solution(6873209955043078590)
XLA Ops:
  0.0 1.8 %fusion = f32[160]{0:T(256)S(1)} fusion(bf16[160,4096]{1,0:T(8,128)(2,1)} %param.3), kind=kLoop, calls=%fused_computation.2 | loop fusion | flops 1965920 | bytes 1311360 | tf_op jit(solution)/shard_map/reduce_sum | solution.py:186
  1.8 0.3 fusion.1
  2.1 1.3 %collective-permute-start = (bf16[160,512]{1,0:T(8,128)(2,1)S(1)}, bf16[160,512]{1,0:T(8,128)(2,1)S(1)}, u32[]{:S(2)}, u32[]{:S(2)}) collective-permute-start(bf16[160,512]{1,0:T(8,128)(2,1)S(1)} %slice.16), channel_id=1, source_target_pairs={{8,0},{16,8},{24,16},{9,1},{17,9},{25,17},{10,2},{18,10},{26,18},{... | collective-permute-start | bytes 491528 | tf_op jit(solution)/shard_map/ppermute | solution.py:23
  3.6 3.8 %multiply_convert_fusion.2 = (bf16[1024,1,200]{0,2,1:T(8,128)(2,1)S(1)}, bf16[1024,1,200]{0,2,1:T(8,128)(2,1)S(1)}) fusion(s32[200]{0:T(256)S(1)} %iota_add_fusion, f32[1024]{0:T(1024)S(1)} %get-tuple-element.21, f32[1024]{0:T(1024)S(1)} %get-tuple-element.22), kind=kLoop, calls=%fused_computation.23 | loop fusion | flops 4096000 | bytes 828192 | tf_op jit(solution)/shard_map/convert
  7.4 2.6 %collective-permute-done = bf16[160,512]{1,0:T(8,128)(2,1)S(1)} collective-permute-done((bf16[160,512]{1,0:T(8,128)(2,1)S(1)}, bf16[160,512]{1,0:T(8,128)(2,1)S(1)}, u32[]{:S(2)}, u32[]{:S(2)}) %collective-permute-start) | collective-permute-done | bytes 163872 | tf_op jit(solution)/shard_map/ppermute | solution.py:23
  10.2 1.6 %fusion.5 = bf16[8,2,200,160]{2,3,0,1:T(8,128)(2,1)S(1)} fusion(bf16[160,8,512]{2,0,1:T(8,128)(2,1)S(1)} %bitcast.40, bf16[160,8,512]{2,0,1:T(8,128)(2,1)S(1)} %bitcast.39, f32[160]{0:T(256)S(1)} %convert_element_type.48, bf16[1024,1,200]{0,2,1:T(8,128)(2,1)S(1)} %get-tuple-element.20, bf16[1024,1,200]{0,2,1:T(8,128)(2,1)S(1)} %get-tuple-element.19), kind=kOutput, calls=%fused_computation.9 | convolution fusion | flops 1056481280 | bytes 4465280 | tf_op jit(solution)/shard_map/cwk,kpf->wpfc/dot_general | solution.py:197
  11.8 1.6 %copy.13 = bf16[8,2,200,160]{3,1,2,0:T(2,128)(2,1)S(1)} copy(bf16[8,2,200,160]{2,3,0,1:T(8,128)(2,1)S(1)} %fusion.5) | data formatting | bytes 2048000 | tf_op jit(solution)/shard_map/convert_element_type | solution.py:199
  13.4 1.3 %copy.14 = bf16[4,50,2,2,4,160]{5,4,3,2,1,0:T(4,128)(2,1)S(1)} copy(bf16[4,50,2,2,4,160]{5,2,1,0,4,3:T(2,128)(2,1)S(1)} %bitcast.35) | data formatting | bytes 2048000 | tf_op jit(solution)/shard_map/transpose | solution.py:205
  14.6 1.4 %reshape.214 = bf16[4,50,4,640]{3,2,1,0:T(4,128)(2,1)S(1)} reshape(bf16[4,50,2,2,4,160]{5,4,3,2,1,0:T(4,128)(2,1)S(1)} %copy.14) | data formatting | bytes 2048000 | tf_op jit(solution)/shard_map/reshape | solution.py:205
  16.1 0.4 fusion.17
  16.4 9.4 %all_to_all.10 = bf16[4,25,4,640]{3,2,1,0:T(4,128)(2,1)S(1)} all-to-all(bf16[4,25,4,640]{3,2,1,0:T(4,128)(2,1)S(1)} %get-tuple-element.17), channel_id=1, replica_groups=mesh['seg'=4,'chan'=8] {'seg'}, dimensions={0} | all-to-all | bytes 1024000 | tf_op jit(solution)/shard_map/all_to_all | solution.py:216
  26.2 1.3 %collective-permute-start.8 = (bf16[25,16,640]{2,1,0:T(8,128)(2,1)S(1)}, bf16[25,16,640]{2,1,0:T(8,128)(2,1)}, u32[]{:S(2)}, u32[]{:S(2)}) collective-permute-start(bf16[25,16,640]{2,1,0:T(8,128)(2,1)S(1)} %reshape.216.own_ref), channel_id=1, source_target_pairs={{3,1},{0,2},{5,3},{2,4},{7,5},{4,6},{11,9},{8,10},{13,11},{10,12},... | collective-permute-start | bytes 1536008 | tf_op jit(solution)/shard_map/ppermute | solution.py:170
  27.5 4.8 %collective-permute-start.7 = (bf16[25,16,640]{2,1,0:T(8,128)(2,1)S(1)}, bf16[25,16,640]{2,1,0:T(8,128)(2,1)}, u32[]{:S(2)}, u32[]{:S(2)}) collective-permute-start(bf16[25,16,640]{2,1,0:T(8,128)(2,1)S(1)} %reshape.216.own_ref), channel_id=1, source_target_pairs={{2,0},{4,2},{1,3},{6,4},{3,5},{5,7},{10,8},{12,10},{9,11},{14,12},... | collective-permute-start | bytes 1536008 | tf_op jit(solution)/shard_map/ppermute | solution.py:169
  32.3 8.4 %all_to_all.11 = bf16[4,25,4,640]{3,2,1,0:T(4,128)(2,1)S(1)} all-to-all(bf16[4,25,4,640]{3,2,1,0:T(4,128)(2,1)S(1)} %get-tuple-element.18), channel_id=1, replica_groups=mesh['seg'=4,'chan'=8] {'seg'}, dimensions={0} | all-to-all | bytes 1024000 | tf_op jit(solution)/shard_map/all_to_all | solution.py:216
  40.6 0.2 copy.15
  41.0 1.3 %collective-permute-start.2 = (bf16[25,16,640]{2,1,0:T(8,128)(2,1)S(1)}, bf16[25,16,640]{2,1,0:T(8,128)(2,1)}, u32[]{:S(2)}, u32[]{:S(2)}) collective-permute-start(bf16[25,16,640]{2,1,0:T(8,128)(2,1)S(1)} %reshape.215.own_ref), channel_id=1, source_target_pairs={{3,1},{0,2},{5,3},{2,4},{7,5},{4,6},{11,9},{8,10},{13,11},{10,12},... | collective-permute-start | bytes 1536008 | tf_op jit(solution)/shard_map/ppermute | solution.py:170
  42.3 4.8 %collective-permute-start.1 = (bf16[25,16,640]{2,1,0:T(8,128)(2,1)S(1)}, bf16[25,16,640]{2,1,0:T(8,128)(2,1)}, u32[]{:S(2)}, u32[]{:S(2)}) collective-permute-start(bf16[25,16,640]{2,1,0:T(8,128)(2,1)S(1)} %reshape.215.own_ref), channel_id=1, source_target_pairs={{2,0},{4,2},{1,3},{6,4},{3,5},{5,7},{10,8},{12,10},{9,11},{14,12},... | collective-permute-start | bytes 1536008 | tf_op jit(solution)/shard_map/ppermute | solution.py:169
  47.1 4.2 %collective-permute-start.9 = (bf16[25,16,640]{2,1,0:T(8,128)(2,1)S(1)}, bf16[25,16,640]{2,1,0:T(8,128)(2,1)S(1)}, u32[]{:S(2)}, u32[]{:S(2)}) collective-permute-start(bf16[25,16,640]{2,1,0:T(8,128)(2,1)S(1)} %reshape.216.own_ref), channel_id=1, source_target_pairs={{0,1},{1,0},{2,3},{3,2},{4,5},{5,4},{6,7},{7,6},{8,9},{9,8},{10,11... | collective-permute-start | bytes 1536008 | tf_op jit(solution)/shard_map/ppermute | solution.py:171
  51.3 1.7 %shard_map.38.left_ref = bf16[25,160,128]{2,1,0:T(8,128)(2,1)S(1)} custom-call(bf16[25,16,640]{2,1,0:T(8,128)(2,1)S(1)} %reshape.216.own_ref), custom_call_target="tpu_custom_call" | custom-call | bytes 12288000 | tf_op jit(solution)/shard_map/pallas_call | solution.py:65
  53.1 4.6 %collective-permute-start.12 = (bf16[25,16,640]{2,1,0:T(8,128)(2,1)}, bf16[25,16,640]{2,1,0:T(8,128)(2,1)S(1)}, u32[]{:S(2)}, u32[]{:S(2)}) collective-permute-start(bf16[25,16,640]{2,1,0:T(8,128)(2,1)} %collective-permute-done.7.refs_1_), channel_id=1, source_target_pairs={{2,1},{1,2},{4,3},{3,4},{6,5},{5,6},{10,9},{9,10},{12,11},{11,12},... | collective-permute-start | bytes 1536008 | tf_op jit(solution)/shard_map/ppermute | solution.py:173
  57.8 0.3 collective-permute-start.10
  58.1 1.7 %shard_map.37.left_ref = bf16[25,160,128]{2,1,0:T(8,128)(2,1)S(1)} custom-call(bf16[25,16,640]{2,1,0:T(8,128)(2,1)S(1)} %reshape.215.own_ref), custom_call_target="tpu_custom_call" | custom-call | bytes 12288000 | tf_op jit(solution)/shard_map/pallas_call | solution.py:65
  59.9 1.1 %collective-permute-start.3 = (bf16[25,16,640]{2,1,0:T(8,128)(2,1)S(1)}, bf16[25,16,640]{2,1,0:T(8,128)(2,1)}, u32[]{:S(2)}, u32[]{:S(2)}) collective-permute-start(bf16[25,16,640]{2,1,0:T(8,128)(2,1)S(1)} %reshape.215.own_ref), channel_id=1, source_target_pairs={{0,1},{1,0},{2,3},{3,2},{4,5},{5,4},{6,7},{7,6},{8,9},{9,8},{10,11... | collective-permute-start | bytes 1536008 | tf_op jit(solution)/shard_map/ppermute | solution.py:171
  61.0 0.8 copy-done
  61.8 0.8 copy-done.2
  62.6 3.6 %collective-permute-start.6 = (bf16[25,16,640]{2,1,0:T(8,128)(2,1)}, bf16[25,16,640]{2,1,0:T(8,128)(2,1)}, u32[]{:S(2)}, u32[]{:S(2)}) collective-permute-start(bf16[25,16,640]{2,1,0:T(8,128)(2,1)} %collective-permute-done.1.refs_1_), channel_id=1, source_target_pairs={{2,1},{1,2},{4,3},{3,4},{6,5},{5,6},{10,9},{9,10},{12,11},{11,12},... | collective-permute-start | bytes 1536008 | tf_op jit(solution)/shard_map/ppermute | solution.py:173
  66.2 0.8 copy-done.4
  67.0 1.0 %copy-done.1 = bf16[25,16,640]{2,1,0:T(8,128)(2,1)S(1)} copy-done((bf16[25,16,640]{2,1,0:T(8,128)(2,1)S(1)}, bf16[25,16,640]{2,1,0:T(8,128)(2,1)}, u32[]{:S(2)}) %copy-start.1) | copy-done | bytes 512024
  68.0 1.0 %copy-done.3 = bf16[25,16,640]{2,1,0:T(8,128)(2,1)S(1)} copy-done((bf16[25,16,640]{2,1,0:T(8,128)(2,1)S(1)}, bf16[25,16,640]{2,1,0:T(8,128)(2,1)}, u32[]{:S(2)}) %copy-start.3) | copy-done | bytes 512024
  69.0 1.0 %copy-done.5 = bf16[25,16,640]{2,1,0:T(8,128)(2,1)S(1)} copy-done((bf16[25,16,640]{2,1,0:T(8,128)(2,1)S(1)}, bf16[25,16,640]{2,1,0:T(8,128)(2,1)}, u32[]{:S(2)}) %copy-start.5) | copy-done | bytes 512024
  70.1 7.7 %shard_map.39.refs_6_ = bf16[2,50,400,128]{3,2,1,0:T(8,128)(2,1)} custom-call(s32[2]{0:T(128)S(1)} %fusion.15.sel_ref, bf16[25,160,128]{2,1,0:T(8,128)(2,1)S(1)} %shard_map.38.left_ref, bf16[25,16,640]{2,1,0:T(8,128)(2,1)S(1)} %copy-done.1, bf16[25,16,640]{2,1,0:T(8,128)(2,1)} %collective-permute-done.7.refs_1_, ...), custom_call_target="tpu_custom_call" | custom-call | flops 655360000 | bytes 15360000 | tf_op jit(solution)/shard_map/pallas_call | solution.py:149
  77.8 8.2 %shard_map.40 = bf16[2,50,400,128]{3,2,1,0:T(8,128)(2,1)} custom-call(s32[2]{0:T(128)S(1)} %fusion.15.sel_ref, bf16[25,160,128]{2,1,0:T(8,128)(2,1)S(1)} %shard_map.37.left_ref, bf16[25,16,640]{2,1,0:T(8,128)(2,1)} %collective-permute-done.3.refs_0_, bf16[25,16,640]{2,1,0:T(8,128)(2,1)} %collective-permute-done.1.refs_1_, ...), custom_call_target="tpu_custom_call", output_to_operand_aliasing={{}: (8, {})} | custom-call | flops 655360000 | bytes 15360000 | tf_op jit(solution)/shard_map/pallas_call | solution.py:149
  (39 shorter events, 1.0 us)
Async XLA Ops:
  0.0 1.8 %copy-start.6 = (bf16[160,4096]{1,0:T(8,128)(2,1)S(1)}, bf16[160,4096]{1,0:T(8,128)(2,1)}, u32[]{:S(2)}) copy-start(bf16[160,4096]{1,0:T(8,128)(2,1)} %param.3) | copy-start | bytes 3932164
  1.8 1.7 %copy-start.7 = (s32[160]{0:T(256)S(1)}, s32[160]{0:T(256)}, u32[]{:S(2)}) copy-start(s32[160]{0:T(256)} %param.4) | copy-start | bytes 1924
  2.1 7.9 %collective-permute-start = (bf16[160,512]{1,0:T(8,128)(2,1)S(1)}, bf16[160,512]{1,0:T(8,128)(2,1)S(1)}, u32[]{:S(2)}, u32[]{:S(2)}) collective-permute-start(bf16[160,512]{1,0:T(8,128)(2,1)S(1)} %slice.16), channel_id=1, source_target_pairs={{8,0},{16,8},{24,16},{9,1},{17,9},{25,17},{10,2},{18,10},{26,18},{... | collective-permute-start | bytes 491528 | tf_op jit(solution)/shard_map/ppermute | solution.py:23
  26.2 26.9 %collective-permute-start.8 = (bf16[25,16,640]{2,1,0:T(8,128)(2,1)S(1)}, bf16[25,16,640]{2,1,0:T(8,128)(2,1)}, u32[]{:S(2)}, u32[]{:S(2)}) collective-permute-start(bf16[25,16,640]{2,1,0:T(8,128)(2,1)S(1)} %reshape.216.own_ref), channel_id=1, source_target_pairs={{3,1},{0,2},{5,3},{2,4},{7,5},{4,6},{11,9},{8,10},{13,11},{10,12},... | collective-permute-start | bytes 1536008 | tf_op jit(solution)/shard_map/ppermute | solution.py:170
  27.5 25.6 %collective-permute-start.7 = (bf16[25,16,640]{2,1,0:T(8,128)(2,1)S(1)}, bf16[25,16,640]{2,1,0:T(8,128)(2,1)}, u32[]{:S(2)}, u32[]{:S(2)}) collective-permute-start(bf16[25,16,640]{2,1,0:T(8,128)(2,1)S(1)} %reshape.216.own_ref), channel_id=1, source_target_pairs={{2,0},{4,2},{1,3},{6,4},{3,5},{5,7},{10,8},{12,10},{9,11},{14,12},... | collective-permute-start | bytes 1536008 | tf_op jit(solution)/shard_map/ppermute | solution.py:169
  41.0 26.0 %copy-start.8 = (s32[2,1]{0,1:T(1,128)S(1)}, s32[2,1]{0,1:T(1,128)}, u32[]{:S(2)}) copy-start(s32[2,1]{0,1:T(1,128)} %param.5) | copy-start | bytes 28
  41.0 16.8 %collective-permute-start.2 = (bf16[25,16,640]{2,1,0:T(8,128)(2,1)S(1)}, bf16[25,16,640]{2,1,0:T(8,128)(2,1)}, u32[]{:S(2)}, u32[]{:S(2)}) collective-permute-start(bf16[25,16,640]{2,1,0:T(8,128)(2,1)S(1)} %reshape.215.own_ref), channel_id=1, source_target_pairs={{3,1},{0,2},{5,3},{2,4},{7,5},{4,6},{11,9},{8,10},{13,11},{10,12},... | collective-permute-start | bytes 1536008 | tf_op jit(solution)/shard_map/ppermute | solution.py:170
  42.3 17.6 %collective-permute-start.1 = (bf16[25,16,640]{2,1,0:T(8,128)(2,1)S(1)}, bf16[25,16,640]{2,1,0:T(8,128)(2,1)}, u32[]{:S(2)}, u32[]{:S(2)}) collective-permute-start(bf16[25,16,640]{2,1,0:T(8,128)(2,1)S(1)} %reshape.215.own_ref), channel_id=1, source_target_pairs={{2,0},{4,2},{1,3},{6,4},{3,5},{5,7},{10,8},{12,10},{9,11},{14,12},... | collective-permute-start | bytes 1536008 | tf_op jit(solution)/shard_map/ppermute | solution.py:169
  47.1 13.9 %collective-permute-start.9 = (bf16[25,16,640]{2,1,0:T(8,128)(2,1)S(1)}, bf16[25,16,640]{2,1,0:T(8,128)(2,1)S(1)}, u32[]{:S(2)}, u32[]{:S(2)}) collective-permute-start(bf16[25,16,640]{2,1,0:T(8,128)(2,1)S(1)} %reshape.216.own_ref), channel_id=1, source_target_pairs={{0,1},{1,0},{2,3},{3,2},{4,5},{5,4},{6,7},{7,6},{8,9},{9,8},{10,11... | collective-permute-start | bytes 1536008 | tf_op jit(solution)/shard_map/ppermute | solution.py:171
  53.0 8.7 %collective-permute-start.11 = (bf16[25,16,640]{2,1,0:T(8,128)(2,1)}, bf16[25,16,640]{2,1,0:T(8,128)(2,1)S(1)}, u32[]{:S(2)}, u32[]{:S(2)}) collective-permute-start(bf16[25,16,640]{2,1,0:T(8,128)(2,1)} %collective-permute-done.8.refs_2_), channel_id=1, source_target_pairs={{0,1},{1,0},{2,3},{3,2},{4,5},{5,4},{6,7},{7,6},{8,9},{9,8},{10,11... | collective-permute-start | bytes 1536008 | tf_op jit(solution)/shard_map/ppermute | solution.py:175
  53.1 13.0 %collective-permute-start.12 = (bf16[25,16,640]{2,1,0:T(8,128)(2,1)}, bf16[25,16,640]{2,1,0:T(8,128)(2,1)S(1)}, u32[]{:S(2)}, u32[]{:S(2)}) collective-permute-start(bf16[25,16,640]{2,1,0:T(8,128)(2,1)} %collective-permute-done.7.refs_1_), channel_id=1, source_target_pairs={{2,1},{1,2},{4,3},{3,4},{6,5},{5,6},{10,9},{9,10},{12,11},{11,12},... | collective-permute-start | bytes 1536008 | tf_op jit(solution)/shard_map/ppermute | solution.py:173
  57.8 9.2 %collective-permute-start.10 = (bf16[25,16,640]{2,1,0:T(8,128)(2,1)}, bf16[25,16,640]{2,1,0:T(8,128)(2,1)}, u32[]{:S(2)}, u32[]{:S(2)}) collective-permute-start(bf16[25,16,640]{2,1,0:T(8,128)(2,1)} %collective-permute-done.7.refs_1_), channel_id=1, source_target_pairs={{0,1},{1,0},{2,3},{3,2},{4,5},{5,4},{6,7},{7,6},{8,9},{9,8},{10,11... | collective-permute-start | bytes 1536008 | tf_op jit(solution)/shard_map/ppermute | solution.py:174
  59.9 17.9 %collective-permute-start.3 = (bf16[25,16,640]{2,1,0:T(8,128)(2,1)S(1)}, bf16[25,16,640]{2,1,0:T(8,128)(2,1)}, u32[]{:S(2)}, u32[]{:S(2)}) collective-permute-start(bf16[25,16,640]{2,1,0:T(8,128)(2,1)S(1)} %reshape.215.own_ref), channel_id=1, source_target_pairs={{0,1},{1,0},{2,3},{3,2},{4,5},{5,4},{6,7},{7,6},{8,9},{9,8},{10,11... | collective-permute-start | bytes 1536008 | tf_op jit(solution)/shard_map/ppermute | solution.py:171
  61.0 0.8 copy-start
  61.8 16.0 %collective-permute-start.5 = (bf16[25,16,640]{2,1,0:T(8,128)(2,1)}, bf16[25,16,640]{2,1,0:T(8,128)(2,1)S(1)}, u32[]{:S(2)}, u32[]{:S(2)}) collective-permute-start(bf16[25,16,640]{2,1,0:T(8,128)(2,1)} %collective-permute-done.2.refs_2_), channel_id=1, source_target_pairs={{0,1},{1,0},{2,3},{3,2},{4,5},{5,4},{6,7},{7,6},{8,9},{9,8},{10,11... | collective-permute-start | bytes 1536008 | tf_op jit(solution)/shard_map/ppermute | solution.py:175
  61.8 0.8 copy-start.2
  62.6 15.2 %collective-permute-start.6 = (bf16[25,16,640]{2,1,0:T(8,128)(2,1)}, bf16[25,16,640]{2,1,0:T(8,128)(2,1)}, u32[]{:S(2)}, u32[]{:S(2)}) collective-permute-start(bf16[25,16,640]{2,1,0:T(8,128)(2,1)} %collective-permute-done.1.refs_1_), channel_id=1, source_target_pairs={{2,1},{1,2},{4,3},{3,4},{6,5},{5,6},{10,9},{9,10},{12,11},{11,12},... | collective-permute-start | bytes 1536008 | tf_op jit(solution)/shard_map/ppermute | solution.py:173
  66.1 0.8 copy-start.4
  66.9 10.9 %collective-permute-start.4 = (bf16[25,16,640]{2,1,0:T(8,128)(2,1)}, bf16[25,16,640]{2,1,0:T(8,128)(2,1)}, u32[]{:S(2)}, u32[]{:S(2)}) collective-permute-start(bf16[25,16,640]{2,1,0:T(8,128)(2,1)} %collective-permute-done.1.refs_1_), channel_id=1, source_target_pairs={{0,1},{1,0},{2,3},{3,2},{4,5},{5,4},{6,7},{7,6},{8,9},{9,8},{10,11... | collective-permute-start | bytes 1536008 | tf_op jit(solution)/shard_map/ppermute | solution.py:174
  67.0 1.0 %copy-start.1 = (bf16[25,16,640]{2,1,0:T(8,128)(2,1)S(1)}, bf16[25,16,640]{2,1,0:T(8,128)(2,1)}, u32[]{:S(2)}) copy-start(bf16[25,16,640]{2,1,0:T(8,128)(2,1)} %copy-done) | copy-start | bytes 1536004
  68.0 1.0 %copy-start.3 = (bf16[25,16,640]{2,1,0:T(8,128)(2,1)S(1)}, bf16[25,16,640]{2,1,0:T(8,128)(2,1)}, u32[]{:S(2)}) copy-start(bf16[25,16,640]{2,1,0:T(8,128)(2,1)} %copy-done.2) | copy-start | bytes 1536004
  69.0 1.0 %copy-start.5 = (bf16[25,16,640]{2,1,0:T(8,128)(2,1)S(1)}, bf16[25,16,640]{2,1,0:T(8,128)(2,1)}, u32[]{:S(2)}) copy-start(bf16[25,16,640]{2,1,0:T(8,128)(2,1)} %copy-done.4) | copy-start | bytes 1536004

commit v7 on v6

--- a/solution.py
+++ b/solution.py
@@ -151,7 +151,7 @@
         grid_spec=grid_spec,
         out_shape=jax.ShapeDtypeStruct((STEPS, total, lines, LANES), jnp.bfloat16),
         input_output_aliases={2 + len(found): 0} if extra else {},
-        compiler_params=pltpu.CompilerParams(vmem_limit_bytes=24 * 2**20),
+        compiler_params=pltpu.CompilerParams(vmem_limit_bytes=56 * 2**20),
         cost_estimate=pl.CostEstimate(
             flops=4 * STEPS * freqs * double * chans * chans,
             bytes_accessed=12 * STEPS * freqs * chans * chans,

time: 87 us -> 86.7 us (level)
  Pallas kernels: 19.3 us -> 22 us
  local copies, waits for them, and re-layouts: 10.9 us -> 8.97 us
  starting transfers between devices: 27.5 us -> 25.7 us
    pallas_call x2, Pallas kernels: 15.9 us -> 18.5 us  [cross_stacks(): pl.pallas_call(functools.partial(gram_kernel, factor, len(found), len(ext...]
    unnamed x18 -> x22, local copies, waits for them, and re-layouts: 5.48 us -> 3.53 us
  transfers between devices with their start and end apart: 13 -> 13, of which waited for: 1 -> 2; matrix products, arithmetic and copies ran while one was open for 5% -> 6% of each run, Pallas kernels for 13% -> 15%
where the time goes in v7:
time: 86.7 us; the launch traced here: 85.6 us
  starting transfers between devices  25.7 us (30%)
  Pallas kernels  22 us (25%)
  blocking collectives  17.8 us (21%)
  local copies, waits for them, and re-layouts  8.97 us (10%)
  other arithmetic  6.49 us (7%)
  waiting for transfers between devices  2.8 us (3%)
  matrix products  1.58 us (2%)
    pallas_call x2, Pallas kernels, cross_stacks(): pl.pallas_call(functools.partial(gram_kernel, factor, len(found), len(ext...  18.5 us
    all_to_all x2, blocking collectives, per_device(): lax.all_to_all(packed[:, first:last], 'seg', split_axis=0, concat_axis=0,...  17.8 us
    ppermute x2, starting transfers between devices, fetch_band(): second = lax.ppermute(own, 'chan', near)  8.8 us
    ppermute x2, starting transfers between devices, fetch_band(): passed = lax.ppermute(second, 'chan', along)  7.97 us
    ppermute x2, starting transfers between devices, fetch_band(): twin = lax.ppermute(own, 'chan', swap)  4.78 us
    another operation x1, other arithmetic  3.78 us
    unnamed x22, local copies, waits for them, and re-layouts  3.53 us
    pallas_call x2, Pallas kernels, turned_own(): pl.pallas_call(functools.partial(turn_kernel, half), grid=(freqs // group...  3.45 us
  transfers between devices with their start and end apart: 13, of which 2 were waited for; matrix products, arithmetic and copies ran while one was open for 6% of the time, Pallas kernels for 15%

profile of v7, /device:TPU:1, one launch (start us, length us, event | category | flops | bytes accessed | tf_op | source)
XLA Modules:
  0.0 85.6 jit_solution(18022690808658345145)
XLA Ops:
  0.0 1.8 %fusion = f32[160]{0:T(256)S(1)} fusion(bf16[160,4096]{1,0:T(8,128)(2,1)} %param.3), kind=kLoop, calls=%fused_computation.2 | loop fusion | flops 1965920 | bytes 1311360 | tf_op jit(solution)/shard_map/reduce_sum | solution.py:186
  1.8 0.3 fusion.1
  2.1 1.3 %collective-permute-start = (bf16[160,512]{1,0:T(8,128)(2,1)S(1)}, bf16[160,512]{1,0:T(8,128)(2,1)S(1)}, u32[]{:S(2)}, u32[]{:S(2)}) collective-permute-start(bf16[160,512]{1,0:T(8,128)(2,1)S(1)} %slice.16), channel_id=1, source_target_pairs={{8,0},{16,8},{24,16},{9,1},{17,9},{25,17},{10,2},{18,10},{26,18},{... | collective-permute-start | bytes 491528 | tf_op jit(solution)/shard_map/ppermute | solution.py:23
  3.6 3.8 %multiply_convert_fusion.2 = (bf16[1024,1,200]{0,2,1:T(8,128)(2,1)S(1)}, bf16[1024,1,200]{0,2,1:T(8,128)(2,1)S(1)}) fusion(s32[200]{0:T(256)S(1)} %iota_add_fusion, f32[1024]{0:T(1024)S(1)} %get-tuple-element.21, f32[1024]{0:T(1024)S(1)} %get-tuple-element.22), kind=kLoop, calls=%fused_computation.23 | loop fusion | flops 4096000 | bytes 828192 | tf_op jit(solution)/shard_map/convert
  7.4 2.6 %collective-permute-done = bf16[160,512]{1,0:T(8,128)(2,1)S(1)} collective-permute-done((bf16[160,512]{1,0:T(8,128)(2,1)S(1)}, bf16[160,512]{1,0:T(8,128)(2,1)S(1)}, u32[]{:S(2)}, u32[]{:S(2)}) %collective-permute-start) | collective-permute-done | bytes 163872 | tf_op jit(solution)/shard_map/ppermute | solution.py:23
  10.2 1.6 %fusion.5 = bf16[8,2,200,160]{2,3,0,1:T(8,128)(2,1)S(1)} fusion(bf16[160,8,512]{2,0,1:T(8,128)(2,1)S(1)} %bitcast.40, bf16[160,8,512]{2,0,1:T(8,128)(2,1)S(1)} %bitcast.39, f32[160]{0:T(256)S(1)} %convert_element_type.48, bf16[1024,1,200]{0,2,1:T(8,128)(2,1)S(1)} %get-tuple-element.20, bf16[1024,1,200]{0,2,1:T(8,128)(2,1)S(1)} %get-tuple-element.19), kind=kOutput, calls=%fused_computation.9 | convolution fusion | flops 1056481280 | bytes 4465280 | tf_op jit(solution)/shard_map/cwk,kpf->wpfc/dot_general | solution.py:197
  11.8 1.6 %copy.13 = bf16[8,2,200,160]{3,1,2,0:T(2,128)(2,1)S(1)} copy(bf16[8,2,200,160]{2,3,0,1:T(8,128)(2,1)S(1)} %fusion.5) | data formatting | bytes 2048000 | tf_op jit(solution)/shard_map/convert_element_type | solution.py:199
  13.4 1.3 %copy.14 = bf16[4,50,2,2,4,160]{5,4,3,2,1,0:T(4,128)(2,1)S(1)} copy(bf16[4,50,2,2,4,160]{5,2,1,0,4,3:T(2,128)(2,1)S(1)} %bitcast.35) | data formatting | bytes 2048000 | tf_op jit(solution)/shard_map/transpose | solution.py:205
  14.6 1.4 %reshape.214 = bf16[4,50,4,640]{3,2,1,0:T(4,128)(2,1)S(1)} reshape(bf16[4,50,2,2,4,160]{5,4,3,2,1,0:T(4,128)(2,1)S(1)} %copy.14) | data formatting | bytes 2048000 | tf_op jit(solution)/shard_map/reshape | solution.py:205
  16.1 0.4 fusion.17
  16.4 9.4 %all_to_all.10 = bf16[4,25,4,640]{3,2,1,0:T(4,128)(2,1)S(1)} all-to-all(bf16[4,25,4,640]{3,2,1,0:T(4,128)(2,1)S(1)} %get-tuple-element.17), channel_id=1, replica_groups=mesh['seg'=4,'chan'=8] {'seg'}, dimensions={0} | all-to-all | bytes 1024000 | tf_op jit(solution)/shard_map/all_to_all | solution.py:216
  25.9 0.2 copy.16
  26.2 1.3 %collective-permute-start.8 = (bf16[25,16,640]{2,1,0:T(8,128)(2,1)S(1)}, bf16[25,16,640]{2,1,0:T(8,128)(2,1)S(1)}, u32[]{:S(2)}, u32[]{:S(2)}) collective-permute-start(bf16[25,16,640]{2,1,0:T(8,128)(2,1)S(1)} %reshape.216.own_ref), channel_id=1, source_target_pairs={{3,1},{0,2},{5,3},{2,4},{7,5},{4,6},{11,9},{8,10},{13,11},{10,12},... | collective-permute-start | bytes 1536008 | tf_op jit(solution)/shard_map/ppermute | solution.py:170
  27.5 4.0 %collective-permute-start.7 = (bf16[25,16,640]{2,1,0:T(8,128)(2,1)S(1)}, bf16[25,16,640]{2,1,0:T(8,128)(2,1)S(1)}, u32[]{:S(2)}, u32[]{:S(2)}) collective-permute-start(bf16[25,16,640]{2,1,0:T(8,128)(2,1)S(1)} %reshape.216.own_ref), channel_id=1, source_target_pairs={{2,0},{4,2},{1,3},{6,4},{3,5},{5,7},{10,8},{12,10},{9,11},{14,12},... | collective-permute-start | bytes 1536008 | tf_op jit(solution)/shard_map/ppermute | solution.py:169
  31.5 8.4 %all_to_all.11 = bf16[4,25,4,640]{3,2,1,0:T(4,128)(2,1)S(1)} all-to-all(bf16[4,25,4,640]{3,2,1,0:T(4,128)(2,1)S(1)} %get-tuple-element.18), channel_id=1, replica_groups=mesh['seg'=4,'chan'=8] {'seg'}, dimensions={0} | all-to-all | bytes 1024000 | tf_op jit(solution)/shard_map/all_to_all | solution.py:216
  39.9 0.2 copy.15
  40.2 1.3 %collective-permute-start.2 = (bf16[25,16,640]{2,1,0:T(8,128)(2,1)S(1)}, bf16[25,16,640]{2,1,0:T(8,128)(2,1)}, u32[]{:S(2)}, u32[]{:S(2)}) collective-permute-start(bf16[25,16,640]{2,1,0:T(8,128)(2,1)S(1)} %reshape.215.own_ref), channel_id=1, source_target_pairs={{3,1},{0,2},{5,3},{2,4},{7,5},{4,6},{11,9},{8,10},{13,11},{10,12},... | collective-permute-start | bytes 1536008 | tf_op jit(solution)/shard_map/ppermute | solution.py:170
  41.5 4.8 %collective-permute-start.1 = (bf16[25,16,640]{2,1,0:T(8,128)(2,1)S(1)}, bf16[25,16,640]{2,1,0:T(8,128)(2,1)}, u32[]{:S(2)}, u32[]{:S(2)}) collective-permute-start(bf16[25,16,640]{2,1,0:T(8,128)(2,1)S(1)} %reshape.215.own_ref), channel_id=1, source_target_pairs={{2,0},{4,2},{1,3},{6,4},{3,5},{5,7},{10,8},{12,10},{9,11},{14,12},... | collective-permute-start | bytes 1536008 | tf_op jit(solution)/shard_map/ppermute | solution.py:169
  46.3 4.3 %collective-permute-start.9 = (bf16[25,16,640]{2,1,0:T(8,128)(2,1)S(1)}, bf16[25,16,640]{2,1,0:T(8,128)(2,1)S(1)}, u32[]{:S(2)}, u32[]{:S(2)}) collective-permute-start(bf16[25,16,640]{2,1,0:T(8,128)(2,1)S(1)} %reshape.216.own_ref), channel_id=1, source_target_pairs={{0,1},{1,0},{2,3},{3,2},{4,5},{5,4},{6,7},{7,6},{8,9},{9,8},{10,11... | collective-permute-start | bytes 1536008 | tf_op jit(solution)/shard_map/ppermute | solution.py:171
  50.6 1.7 %shard_map.38.left_ref = bf16[25,160,128]{2,1,0:T(8,128)(2,1)S(1)} custom-call(bf16[25,16,640]{2,1,0:T(8,128)(2,1)S(1)} %reshape.216.own_ref), custom_call_target="tpu_custom_call" | custom-call | bytes 12288000 | tf_op jit(solution)/shard_map/pallas_call | solution.py:65
  52.3 1.0 %copy-done = bf16[25,160,128]{2,1,0:T(8,128)(2,1)} copy-done((bf16[25,160,128]{2,1,0:T(8,128)(2,1)}, bf16[25,160,128]{2,1,0:T(8,128)(2,1)S(1)}, u32[]{:S(2)}) %copy-start) | copy-done | bytes 1024024
  53.4 4.6 %collective-permute-start.12 = (bf16[25,16,640]{2,1,0:T(8,128)(2,1)S(1)}, bf16[25,16,640]{2,1,0:T(8,128)(2,1)S(1)}, u32[]{:S(2)}, u32[]{:S(2)}) collective-permute-start(bf16[25,16,640]{2,1,0:T(8,128)(2,1)S(1)} %collective-permute-done.7.refs_1_), channel_id=1, source_target_pairs={{2,1},{1,2},{4,3},{3,4},{6,5},{5,6},{10,9},{9,10},{12,11},{11,12},... | collective-permute-start | bytes 1536008 | tf_op jit(solution)/shard_map/ppermute | solution.py:173
  58.1 1.7 %shard_map.37.left_ref = bf16[25,160,128]{2,1,0:T(8,128)(2,1)S(1)} custom-call(bf16[25,16,640]{2,1,0:T(8,128)(2,1)S(1)} %reshape.215.own_ref), custom_call_target="tpu_custom_call" | custom-call | bytes 12288000 | tf_op jit(solution)/shard_map/pallas_call | solution.py:65
  59.8 1.0 %copy-done.1 = bf16[25,160,128]{2,1,0:T(8,128)(2,1)} copy-done((bf16[25,160,128]{2,1,0:T(8,128)(2,1)}, bf16[25,160,128]{2,1,0:T(8,128)(2,1)S(1)}, u32[]{:S(2)}) %copy-start.1) | copy-done | bytes 1024024
  60.8 0.5 collective-permute-start.3
  61.4 3.3 %collective-permute-start.6 = (bf16[25,16,640]{2,1,0:T(8,128)(2,1)}, bf16[25,16,640]{2,1,0:T(8,128)(2,1)}, u32[]{:S(2)}, u32[]{:S(2)}) collective-permute-start(bf16[25,16,640]{2,1,0:T(8,128)(2,1)} %collective-permute-done.1.refs_1_), channel_id=1, source_target_pairs={{2,1},{1,2},{4,3},{3,4},{6,5},{5,6},{10,9},{9,10},{12,11},{11,12},... | collective-permute-start | bytes 1536008 | tf_op jit(solution)/shard_map/ppermute | solution.py:173
  64.8 0.2 collective-permute-done.12.refs_5_
  64.9 0.8 copy-done.7
  65.7 0.5 fusion.15.sel_ref
  66.3 9.2 %shard_map.39.refs_6_ = bf16[2,50,400,128]{3,2,1,0:T(8,128)(2,1)} custom-call(s32[2]{0:T(128)} %fusion.15.sel_ref, bf16[25,160,128]{2,1,0:T(8,128)(2,1)} %copy-done, bf16[25,16,640]{2,1,0:T(8,128)(2,1)} %copy-done.5, bf16[25,16,640]{2,1,0:T(8,128)(2,1)} %copy-done.4, bf16[25,16,640]{2,1,0:T(8,128)(2,1)} %copy-done.3, ...), custom_call_target="tpu_custom_call" | custom-call | flops 655360000 | bytes 15360000 | tf_op jit(solution)/shard_map/pallas_call | solution.py:149
  75.6 0.8 copy-done.8
  76.3 9.3 %shard_map.40 = bf16[2,50,400,128]{3,2,1,0:T(8,128)(2,1)} custom-call(s32[2]{0:T(128)} %fusion.15.sel_ref, bf16[25,160,128]{2,1,0:T(8,128)(2,1)} %copy-done.1, bf16[25,16,640]{2,1,0:T(8,128)(2,1)} %collective-permute-done.3.refs_0_, bf16[25,16,640]{2,1,0:T(8,128)(2,1)} %collective-permute-done.1.refs_1_, ...), custom_call_target="tpu_custom_call", output_to_operand_aliasing={{}: (8, {})} | custom-call | flops 655360000 | bytes 15360000 | tf_op jit(solution)/shard_map/pallas_call | solution.py:149
  (43 shorter events, 0.9 us)
Async XLA Ops:
  0.0 1.8 %copy-start.2 = (bf16[160,4096]{1,0:T(8,128)(2,1)S(1)}, bf16[160,4096]{1,0:T(8,128)(2,1)}, u32[]{:S(2)}) copy-start(bf16[160,4096]{1,0:T(8,128)(2,1)} %param.3) | copy-start | bytes 3932164
  1.8 1.7 %copy-start.9 = (s32[160]{0:T(256)S(1)}, s32[160]{0:T(256)}, u32[]{:S(2)}) copy-start(s32[160]{0:T(256)} %param.4) | copy-start | bytes 1924
  2.1 7.9 %collective-permute-start = (bf16[160,512]{1,0:T(8,128)(2,1)S(1)}, bf16[160,512]{1,0:T(8,128)(2,1)S(1)}, u32[]{:S(2)}, u32[]{:S(2)}) collective-permute-start(bf16[160,512]{1,0:T(8,128)(2,1)S(1)} %slice.16), channel_id=1, source_target_pairs={{8,0},{16,8},{24,16},{9,1},{17,9},{25,17},{10,2},{18,10},{26,18},{... | collective-permute-start | bytes 491528 | tf_op jit(solution)/shard_map/ppermute | solution.py:23
  26.2 27.1 %collective-permute-start.8 = (bf16[25,16,640]{2,1,0:T(8,128)(2,1)S(1)}, bf16[25,16,640]{2,1,0:T(8,128)(2,1)S(1)}, u32[]{:S(2)}, u32[]{:S(2)}) collective-permute-start(bf16[25,16,640]{2,1,0:T(8,128)(2,1)S(1)} %reshape.216.own_ref), channel_id=1, source_target_pairs={{3,1},{0,2},{5,3},{2,4},{7,5},{4,6},{11,9},{8,10},{13,11},{10,12},... | collective-permute-start | bytes 1536008 | tf_op jit(solution)/shard_map/ppermute | solution.py:170
  27.5 25.8 %collective-permute-start.7 = (bf16[25,16,640]{2,1,0:T(8,128)(2,1)S(1)}, bf16[25,16,640]{2,1,0:T(8,128)(2,1)S(1)}, u32[]{:S(2)}, u32[]{:S(2)}) collective-permute-start(bf16[25,16,640]{2,1,0:T(8,128)(2,1)S(1)} %reshape.216.own_ref), channel_id=1, source_target_pairs={{2,0},{4,2},{1,3},{6,4},{3,5},{5,7},{10,8},{12,10},{9,11},{14,12},... | collective-permute-start | bytes 1536008 | tf_op jit(solution)/shard_map/ppermute | solution.py:169
  40.2 25.6 %copy-start.10 = (s32[2,1]{0,1:T(1,128)S(1)}, s32[2,1]{0,1:T(1,128)}, u32[]{:S(2)}) copy-start(s32[2,1]{0,1:T(1,128)} %param.5) | copy-start | bytes 28
  40.2 17.8 %collective-permute-start.2 = (bf16[25,16,640]{2,1,0:T(8,128)(2,1)S(1)}, bf16[25,16,640]{2,1,0:T(8,128)(2,1)}, u32[]{:S(2)}, u32[]{:S(2)}) collective-permute-start(bf16[25,16,640]{2,1,0:T(8,128)(2,1)S(1)} %reshape.215.own_ref), channel_id=1, source_target_pairs={{3,1},{0,2},{5,3},{2,4},{7,5},{4,6},{11,9},{8,10},{13,11},{10,12},... | collective-permute-start | bytes 1536008 | tf_op jit(solution)/shard_map/ppermute | solution.py:170
  41.5 19.3 %collective-permute-start.1 = (bf16[25,16,640]{2,1,0:T(8,128)(2,1)S(1)}, bf16[25,16,640]{2,1,0:T(8,128)(2,1)}, u32[]{:S(2)}, u32[]{:S(2)}) collective-permute-start(bf16[25,16,640]{2,1,0:T(8,128)(2,1)S(1)} %reshape.215.own_ref), channel_id=1, source_target_pairs={{2,0},{4,2},{1,3},{6,4},{3,5},{5,7},{10,8},{12,10},{9,11},{14,12},... | collective-permute-start | bytes 1536008 | tf_op jit(solution)/shard_map/ppermute | solution.py:169
  46.3 15.0 %collective-permute-start.9 = (bf16[25,16,640]{2,1,0:T(8,128)(2,1)S(1)}, bf16[25,16,640]{2,1,0:T(8,128)(2,1)S(1)}, u32[]{:S(2)}, u32[]{:S(2)}) collective-permute-start(bf16[25,16,640]{2,1,0:T(8,128)(2,1)S(1)} %reshape.216.own_ref), channel_id=1, source_target_pairs={{0,1},{1,0},{2,3},{3,2},{4,5},{5,4},{6,7},{7,6},{8,9},{9,8},{10,11... | collective-permute-start | bytes 1536008 | tf_op jit(solution)/shard_map/ppermute | solution.py:171
  52.3 1.0 %copy-start = (bf16[25,160,128]{2,1,0:T(8,128)(2,1)}, bf16[25,160,128]{2,1,0:T(8,128)(2,1)S(1)}, u32[]{:S(2)}) copy-start(bf16[25,160,128]{2,1,0:T(8,128)(2,1)S(1)} %shard_map.38.left_ref) | copy-start | bytes 3072004
  53.3 13.0 %copy-start.3 = (bf16[25,16,640]{2,1,0:T(8,128)(2,1)}, bf16[25,16,640]{2,1,0:T(8,128)(2,1)S(1)}, u32[]{:S(2)}) copy-start(bf16[25,16,640]{2,1,0:T(8,128)(2,1)S(1)} %collective-permute-done.8.refs_2_) | copy-start | bytes 1536004
  53.3 13.0 %copy-start.4 = (bf16[25,16,640]{2,1,0:T(8,128)(2,1)}, bf16[25,16,640]{2,1,0:T(8,128)(2,1)S(1)}, u32[]{:S(2)}) copy-start(bf16[25,16,640]{2,1,0:T(8,128)(2,1)S(1)} %collective-permute-done.7.refs_1_) | copy-start | bytes 1536004
  53.3 8.1 %collective-permute-start.11 = (bf16[25,16,640]{2,1,0:T(8,128)(2,1)S(1)}, bf16[25,16,640]{2,1,0:T(8,128)(2,1)S(1)}, u32[]{:S(2)}, u32[]{:S(2)}) collective-permute-start(bf16[25,16,640]{2,1,0:T(8,128)(2,1)S(1)} %collective-permute-done.8.refs_2_), channel_id=1, source_target_pairs={{0,1},{1,0},{2,3},{3,2},{4,5},{5,4},{6,7},{7,6},{8,9},{9,8},{10,11... | collective-permute-start | bytes 1536008 | tf_op jit(solution)/shard_map/ppermute | solution.py:175
  53.4 11.6 %collective-permute-start.12 = (bf16[25,16,640]{2,1,0:T(8,128)(2,1)S(1)}, bf16[25,16,640]{2,1,0:T(8,128)(2,1)S(1)}, u32[]{:S(2)}, u32[]{:S(2)}) collective-permute-start(bf16[25,16,640]{2,1,0:T(8,128)(2,1)S(1)} %collective-permute-done.7.refs_1_), channel_id=1, source_target_pairs={{2,1},{1,2},{4,3},{3,4},{6,5},{5,6},{10,9},{9,10},{12,11},{11,12},... | collective-permute-start | bytes 1536008 | tf_op jit(solution)/shard_map/ppermute | solution.py:173
  58.0 8.2 %collective-permute-start.10 = (bf16[25,16,640]{2,1,0:T(8,128)(2,1)S(1)}, bf16[25,16,640]{2,1,0:T(8,128)(2,1)}, u32[]{:S(2)}, u32[]{:S(2)}) collective-permute-start(bf16[25,16,640]{2,1,0:T(8,128)(2,1)S(1)} %collective-permute-done.7.refs_1_), channel_id=1, source_target_pairs={{0,1},{1,0},{2,3},{3,2},{4,5},{5,4},{6,7},{7,6},{8,9},{9,8},{10,11... | collective-permute-start | bytes 1536008 | tf_op jit(solution)/shard_map/ppermute | solution.py:174
  59.8 1.0 %copy-start.1 = (bf16[25,160,128]{2,1,0:T(8,128)(2,1)}, bf16[25,160,128]{2,1,0:T(8,128)(2,1)S(1)}, u32[]{:S(2)}) copy-start(bf16[25,160,128]{2,1,0:T(8,128)(2,1)S(1)} %shard_map.37.left_ref) | copy-start | bytes 3072004
  60.8 14.7 %collective-permute-start.3 = (bf16[25,16,640]{2,1,0:T(8,128)(2,1)S(1)}, bf16[25,16,640]{2,1,0:T(8,128)(2,1)}, u32[]{:S(2)}, u32[]{:S(2)}) collective-permute-start(bf16[25,16,640]{2,1,0:T(8,128)(2,1)S(1)} %reshape.215.own_ref), channel_id=1, source_target_pairs={{0,1},{1,0},{2,3},{3,2},{4,5},{5,4},{6,7},{7,6},{8,9},{9,8},{10,11... | collective-permute-start | bytes 1536008 | tf_op jit(solution)/shard_map/ppermute | solution.py:171
  61.3 4.9 %copy-start.5 = (bf16[25,16,640]{2,1,0:T(8,128)(2,1)}, bf16[25,16,640]{2,1,0:T(8,128)(2,1)S(1)}, u32[]{:S(2)}) copy-start(bf16[25,16,640]{2,1,0:T(8,128)(2,1)S(1)} %collective-permute-done.9.refs_0_) | copy-start | bytes 1536004
  61.3 14.2 %collective-permute-start.5 = (bf16[25,16,640]{2,1,0:T(8,128)(2,1)}, bf16[25,16,640]{2,1,0:T(8,128)(2,1)S(1)}, u32[]{:S(2)}, u32[]{:S(2)}) collective-permute-start(bf16[25,16,640]{2,1,0:T(8,128)(2,1)} %collective-permute-done.2.refs_2_), channel_id=1, source_target_pairs={{0,1},{1,0},{2,3},{3,2},{4,5},{5,4},{6,7},{7,6},{8,9},{9,8},{10,11... | collective-permute-start | bytes 1536008 | tf_op jit(solution)/shard_map/ppermute | solution.py:175
  61.4 4.9 %copy-start.6 = (bf16[25,16,640]{2,1,0:T(8,128)(2,1)}, bf16[25,16,640]{2,1,0:T(8,128)(2,1)S(1)}, u32[]{:S(2)}) copy-start(bf16[25,16,640]{2,1,0:T(8,128)(2,1)S(1)} %collective-permute-done.11.refs_4_) | copy-start | bytes 1536004
  61.4 14.1 %collective-permute-start.6 = (bf16[25,16,640]{2,1,0:T(8,128)(2,1)}, bf16[25,16,640]{2,1,0:T(8,128)(2,1)}, u32[]{:S(2)}, u32[]{:S(2)}) collective-permute-start(bf16[25,16,640]{2,1,0:T(8,128)(2,1)} %collective-permute-done.1.refs_1_), channel_id=1, source_target_pairs={{2,1},{1,2},{4,3},{3,4},{6,5},{5,6},{10,9},{9,10},{12,11},{11,12},... | collective-permute-start | bytes 1536008 | tf_op jit(solution)/shard_map/ppermute | solution.py:173
  64.9 0.8 copy-start.7
  65.7 9.8 %collective-permute-start.4 = (bf16[25,16,640]{2,1,0:T(8,128)(2,1)}, bf16[25,16,640]{2,1,0:T(8,128)(2,1)}, u32[]{:S(2)}, u32[]{:S(2)}) collective-permute-start(bf16[25,16,640]{2,1,0:T(8,128)(2,1)} %collective-permute-done.1.refs_1_), channel_id=1, source_target_pairs={{0,1},{1,0},{2,3},{3,2},{4,5},{5,4},{6,7},{7,6},{8,9},{9,8},{10,11... | collective-permute-start | bytes 1536008 | tf_op jit(solution)/shard_map/ppermute | solution.py:174
  75.5 0.8 copy-start.8

commit v8 on v7

--- a/solution.py
+++ b/solution.py
@@ -210,7 +210,7 @@
         chosen = jnp.where(offset == reach_k, place, chosen)
     factor = 1.0 / math.sqrt(segs * windows)
     group = freq_group(freqs)
-    cut = pl.cdiv(freqs // group, 2) * group
+    cut = max(1, 2 * (freqs // group) // 5) * group
     chunks = []
     for first, last in ((0, cut), (cut, freqs)):
         got = lax.all_to_all(packed[:, first:last], "seg", split_axis=0, concat_axis=0, tiled=True)

time: 86.7 us -> 88 us (1.015)
  blocking collectives: 17.8 us -> 0 us
  starting transfers between devices: 25.7 us -> 35.2 us
  waiting for transfers between devices: 2.8 us -> 10 us
  local copies, waits for them, and re-layouts: 8.97 us -> 11.5 us
    all_to_all x2 -> x0, blocking collectives: 17.8 us -> none  [per_device(): lax.all_to_all(packed[:, first:last], 'seg', split_axis=0, concat_axis=0,...]
    all_to_all x0 -> x2, starting transfers between devices: none -> 7.02 us  [per_device(): lax.all_to_all(packed[:, first:last], 'seg', split_axis=0, concat_axis=0,...]
    all_to_all x0 -> x2, waiting for transfers between devices: none -> 5.87 us  [per_device(): lax.all_to_all(packed[:, first:last], 'seg', split_axis=0, concat_axis=0,...]
    ppermute x2, starting transfers between devices: 0.17 us -> 3.97 us  [fetch_band(): twin_behind = lax.ppermute(behind, 'chan', swap)]
    ppermute x2, starting transfers between devices: 7.97 us -> 5.56 us  [fetch_band(): passed = lax.ppermute(second, 'chan', along)]
    slice x1 -> x2, local copies, waits for them, and re-layouts: 0.35 us -> 1.95 us  [per_device(): packed[:, first:last]]
    ppermute x2, waiting for transfers between devices: 0.01 us -> 1.52 us  [fetch_band(): twin_second = lax.ppermute(second, 'chan', swap)]
    unnamed x22 -> x24, local copies, waits for them, and re-layouts: 3.53 us -> 4.44 us
  transfers between devices with their start and end apart: 13 -> 15, of which waited for: 2 -> 4; matrix products, arithmetic and copies ran while one was open for 6% -> 7% of each run, Pallas kernels for 15% -> 13%
where the time goes in v8:
time: 88 us; the launch traced here: 87.2 us
  starting transfers between devices  35.2 us (40%)
  Pallas kernels  22 us (25%)
  local copies, waits for them, and re-layouts  11.5 us (13%)
  waiting for transfers between devices  10 us (11%)
  other arithmetic  6.59 us (7%)
  matrix products  1.58 us (2%)
    pallas_call x2, Pallas kernels, cross_stacks(): pl.pallas_call(functools.partial(gram_kernel, factor, len(found), len(ext...  18.5 us
    ppermute x2, starting transfers between devices, fetch_band(): second = lax.ppermute(own, 'chan', near)  8.78 us
    all_to_all x2, starting transfers between devices, per_device(): lax.all_to_all(packed[:, first:last], 'seg', split_axis=0, concat_axis=0,...  7.02 us
    all_to_all x2, waiting for transfers between devices, per_device(): lax.all_to_all(packed[:, first:last], 'seg', split_axis=0, concat_axis=0,...  5.87 us
    ppermute x2, starting transfers between devices, fetch_band(): passed = lax.ppermute(second, 'chan', along)  5.56 us
    ppermute x2, starting transfers between devices, fetch_band(): twin = lax.ppermute(own, 'chan', swap)  5.47 us
    unnamed x24, local copies, waits for them, and re-layouts  4.44 us
    ppermute x2, starting transfers between devices, fetch_band(): twin_behind = lax.ppermute(behind, 'chan', swap)  3.97 us
  transfers between devices with their start and end apart: 15, of which 4 were waited for; matrix products, arithmetic and copies ran while one was open for 7% of the time, Pallas kernels for 13%

profile of v8, /device:TPU:1, one launch (start us, length us, event | category | flops | bytes accessed | tf_op | source)
XLA Modules:
  0.0 87.2 jit_solution(7718740946759136486)
XLA Ops:
  0.0 1.8 %fusion = f32[160]{0:T(256)S(1)} fusion(bf16[160,4096]{1,0:T(8,128)(2,1)} %param.3), kind=kLoop, calls=%fused_computation.2 | loop fusion | flops 1965920 | bytes 1311360 | tf_op jit(solution)/shard_map/reduce_sum | solution.py:186
  2.1 1.3 %collective-permute-start = (bf16[160,512]{1,0:T(8,128)(2,1)S(1)}, bf16[160,512]{1,0:T(8,128)(2,1)S(1)}, u32[]{:S(2)}, u32[]{:S(2)}) collective-permute-start(bf16[160,512]{1,0:T(8,128)(2,1)S(1)} %slice.16), channel_id=1, source_target_pairs={{8,0},{16,8},{24,16},{9,1},{17,9},{25,17},{10,2},{18,10},{26,18},{... | collective-permute-start | bytes 491528 | tf_op jit(solution)/shard_map/ppermute | solution.py:23
  3.6 3.8 %multiply_convert_fusion.2 = (bf16[1024,1,200]{0,2,1:T(8,128)(2,1)S(1)}, bf16[1024,1,200]{0,2,1:T(8,128)(2,1)S(1)}) fusion(s32[200]{0:T(256)S(1)} %iota_add_fusion, f32[1024]{0:T(1024)S(1)} %get-tuple-element.19, f32[1024]{0:T(1024)S(1)} %get-tuple-element.20), kind=kLoop, calls=%fused_computation.23 | loop fusion | flops 4096000 | bytes 828192 | tf_op jit(solution)/shard_map/convert
  7.4 2.6 %collective-permute-done = bf16[160,512]{1,0:T(8,128)(2,1)S(1)} collective-permute-done((bf16[160,512]{1,0:T(8,128)(2,1)S(1)}, bf16[160,512]{1,0:T(8,128)(2,1)S(1)}, u32[]{:S(2)}, u32[]{:S(2)}) %collective-permute-start) | collective-permute-done | bytes 163872 | tf_op jit(solution)/shard_map/ppermute | solution.py:23
  10.2 1.6 %fusion.5 = bf16[8,2,200,160]{2,3,0,1:T(8,128)(2,1)S(1)} fusion(bf16[160,8,512]{2,0,1:T(8,128)(2,1)S(1)} %bitcast.40, bf16[160,8,512]{2,0,1:T(8,128)(2,1)S(1)} %bitcast.39, f32[160]{0:T(256)S(1)} %convert_element_type.48, bf16[1024,1,200]{0,2,1:T(8,128)(2,1)S(1)} %get-tuple-element.18, bf16[1024,1,200]{0,2,1:T(8,128)(2,1)S(1)} %get-tuple-element.17), kind=kOutput, calls=%fused_computation.9 | convolution fusion | flops 1056481280 | bytes 4465280 | tf_op jit(solution)/shard_map/cwk,kpf->wpfc/dot_general | solution.py:197
  11.8 1.6 %copy.13 = bf16[8,2,200,160]{3,1,2,0:T(2,128)(2,1)S(1)} copy(bf16[8,2,200,160]{2,3,0,1:T(8,128)(2,1)S(1)} %fusion.5) | data formatting | bytes 2048000 | tf_op jit(solution)/shard_map/convert_element_type | solution.py:199
  13.4 1.3 %copy.14 = bf16[4,50,2,2,4,160]{5,4,3,2,1,0:T(4,128)(2,1)S(1)} copy(bf16[4,50,2,2,4,160]{5,2,1,0,4,3:T(2,128)(2,1)S(1)} %bitcast.35) | data formatting | bytes 2048000 | tf_op jit(solution)/shard_map/transpose | solution.py:205
  14.6 1.4 %reshape.214 = bf16[4,50,4,640]{3,2,1,0:T(4,128)(2,1)S(1)} reshape(bf16[4,50,2,2,4,160]{5,4,3,2,1,0:T(4,128)(2,1)S(1)} %copy.14) | data formatting | bytes 2048000 | tf_op jit(solution)/shard_map/reshape | solution.py:205
  16.1 0.9 %slice.18 = bf16[4,20,4,640]{3,2,1,0:T(4,128)(2,1)} slice(bf16[4,50,4,640]{3,2,1,0:T(4,128)(2,1)S(1)} %reshape.214), slice={[0:4], [0:20], [0:4], [0:640]} | slice | bytes 819200 | tf_op jit(solution)/shard_map/slice | solution.py:216
  17.0 3.5 %all-to-all-start.1 = ((bf16[4,20,4,640]{3,2,1,0:T(4,128)(2,1)}), bf16[4,20,4,640]{3,2,1,0:T(4,128)(2,1)S(1)}, u32[]{:S(2)}, u32[]{:S(2)}) async-start(bf16[4,20,4,640]{3,2,1,0:T(4,128)(2,1)} %slice.18), calls=%async_computation.1 | async-start | bytes 819200 | tf_op jit(solution)/shard_map/all_to_all | solution.py:216
  20.5 1.0 %slice.17 = bf16[4,30,4,640]{3,2,1,0:T(4,128)(2,1)} slice(bf16[4,50,4,640]{3,2,1,0:T(4,128)(2,1)S(1)} %reshape.214), slice={[0:4], [20:50], [0:4], [0:640]} | slice | bytes 1228800 | tf_op jit(solution)/shard_map/slice | solution.py:216
  21.5 5.0 %all-to-all-done.1 = bf16[4,20,4,640]{3,2,1,0:T(4,128)(2,1)S(1)} async-done(((bf16[4,20,4,640]{3,2,1,0:T(4,128)(2,1)}), bf16[4,20,4,640]{3,2,1,0:T(4,128)(2,1)S(1)}, u32[]{:S(2)}, u32[]{:S(2)}) %all-to-all-start.1) | async-done | bytes 409632 | tf_op jit(solution)/shard_map/all_to_all | solution.py:216
  26.5 3.6 %all-to-all-start = ((bf16[4,30,4,640]{3,2,1,0:T(4,128)(2,1)}), bf16[4,30,4,640]{3,2,1,0:T(4,128)(2,1)S(1)}, u32[]{:S(2)}, u32[]{:S(2)}) async-start(bf16[4,30,4,640]{3,2,1,0:T(4,128)(2,1)} %slice.17), calls=%async_computation | async-start | bytes 1228800 | tf_op jit(solution)/shard_map/all_to_all | solution.py:216
  30.3 1.3 %collective-permute-start.8 = (bf16[20,16,640]{2,1,0:T(8,128)(2,1)S(1)}, bf16[20,16,640]{2,1,0:T(8,128)(2,1)}, u32[]{:S(2)}, u32[]{:S(2)}) collective-permute-start(bf16[20,16,640]{2,1,0:T(8,128)(2,1)S(1)} %reshape.216.own_ref), channel_id=1, source_target_pairs={{3,1},{0,2},{5,3},{2,4},{7,5},{4,6},{11,9},{8,10},{13,11},{10,12},... | collective-permute-start | bytes 1228808 | tf_op jit(solution)/shard_map/ppermute | solution.py:170
  31.6 4.8 %collective-permute-start.7 = (bf16[20,16,640]{2,1,0:T(8,128)(2,1)S(1)}, bf16[20,16,640]{2,1,0:T(8,128)(2,1)}, u32[]{:S(2)}, u32[]{:S(2)}) collective-permute-start(bf16[20,16,640]{2,1,0:T(8,128)(2,1)S(1)} %reshape.216.own_ref), channel_id=1, source_target_pairs={{2,0},{4,2},{1,3},{6,4},{3,5},{5,7},{10,8},{12,10},{9,11},{14,12},... | collective-permute-start | bytes 1228808 | tf_op jit(solution)/shard_map/ppermute | solution.py:169
  36.4 0.9 all-to-all-done
  37.6 1.3 %collective-permute-start.2 = (bf16[30,16,640]{2,1,0:T(8,128)(2,1)S(1)}, bf16[30,16,640]{2,1,0:T(8,128)(2,1)S(1)}, u32[]{:S(2)}, u32[]{:S(2)}) collective-permute-start(bf16[30,16,640]{2,1,0:T(8,128)(2,1)S(1)} %reshape.215.own_ref), channel_id=1, source_target_pairs={{3,1},{0,2},{5,3},{2,4},{7,5},{4,6},{11,9},{8,10},{13,11},{10,12},... | collective-permute-start | bytes 1843208 | tf_op jit(solution)/shard_map/ppermute | solution.py:170
  38.9 4.0 %collective-permute-start.1 = (bf16[30,16,640]{2,1,0:T(8,128)(2,1)S(1)}, bf16[30,16,640]{2,1,0:T(8,128)(2,1)S(1)}, u32[]{:S(2)}, u32[]{:S(2)}) collective-permute-start(bf16[30,16,640]{2,1,0:T(8,128)(2,1)S(1)} %reshape.215.own_ref), channel_id=1, source_target_pairs={{2,0},{4,2},{1,3},{6,4},{3,5},{5,7},{10,8},{12,10},{9,11},{14,12},... | collective-permute-start | bytes 1843208 | tf_op jit(solution)/shard_map/ppermute | solution.py:169
  42.9 2.3 %collective-permute-start.9 = (bf16[20,16,640]{2,1,0:T(8,128)(2,1)S(1)}, bf16[20,16,640]{2,1,0:T(8,128)(2,1)S(1)}, u32[]{:S(2)}, u32[]{:S(2)}) collective-permute-start(bf16[20,16,640]{2,1,0:T(8,128)(2,1)S(1)} %reshape.216.own_ref), channel_id=1, source_target_pairs={{0,1},{1,0},{2,3},{3,2},{4,5},{5,4},{6,7},{7,6},{8,9},{9,8},{10,11... | collective-permute-start | bytes 1228808 | tf_op jit(solution)/shard_map/ppermute | solution.py:171
  45.3 1.4 %shard_map.38.left_ref = bf16[20,160,128]{2,1,0:T(8,128)(2,1)S(1)} custom-call(bf16[20,16,640]{2,1,0:T(8,128)(2,1)S(1)} %reshape.216.own_ref), custom_call_target="tpu_custom_call" | custom-call | bytes 9830400 | tf_op jit(solution)/shard_map/pallas_call | solution.py:65
  46.7 0.9 %copy-done.1 = bf16[20,160,128]{2,1,0:T(8,128)(2,1)} copy-done((bf16[20,160,128]{2,1,0:T(8,128)(2,1)}, bf16[20,160,128]{2,1,0:T(8,128)(2,1)S(1)}, u32[]{:S(2)}) %copy-start.1) | copy-done | bytes 819224
  47.6 3.1 %collective-permute-start.11 = (bf16[20,16,640]{2,1,0:T(8,128)(2,1)}, bf16[20,16,640]{2,1,0:T(8,128)(2,1)S(1)}, u32[]{:S(2)}, u32[]{:S(2)}) collective-permute-start(bf16[20,16,640]{2,1,0:T(8,128)(2,1)} %collective-permute-done.8.refs_2_), channel_id=1, source_target_pairs={{0,1},{1,0},{2,3},{3,2},{4,5},{5,4},{6,7},{7,6},{8,9},{9,8},{10,11... | collective-permute-start | bytes 1228808 | tf_op jit(solution)/shard_map/ppermute | solution.py:175
  50.7 1.9 %collective-permute-start.12 = (bf16[20,16,640]{2,1,0:T(8,128)(2,1)}, bf16[20,16,640]{2,1,0:T(8,128)(2,1)}, u32[]{:S(2)}, u32[]{:S(2)}) collective-permute-start(bf16[20,16,640]{2,1,0:T(8,128)(2,1)} %collective-permute-done.7.refs_1_), channel_id=1, source_target_pairs={{2,1},{1,2},{4,3},{3,4},{6,5},{5,6},{10,9},{9,10},{12,11},{11,12},... | collective-permute-start | bytes 1228808 | tf_op jit(solution)/shard_map/ppermute | solution.py:173
  52.6 2.1 %shard_map.37.left_ref = bf16[30,160,128]{2,1,0:T(8,128)(2,1)S(1)} custom-call(bf16[30,16,640]{2,1,0:T(8,128)(2,1)S(1)} %reshape.215.own_ref), custom_call_target="tpu_custom_call" | custom-call | bytes 14745600 | tf_op jit(solution)/shard_map/pallas_call | solution.py:65
  54.7 1.0 %copy-done = bf16[30,160,128]{2,1,0:T(8,128)(2,1)} copy-done((bf16[30,160,128]{2,1,0:T(8,128)(2,1)}, bf16[30,160,128]{2,1,0:T(8,128)(2,1)S(1)}, u32[]{:S(2)}) %copy-start) | copy-done | bytes 1228824
  55.7 3.1 %collective-permute-start.3 = (bf16[30,16,640]{2,1,0:T(8,128)(2,1)S(1)}, bf16[30,16,640]{2,1,0:T(8,128)(2,1)S(1)}, u32[]{:S(2)}, u32[]{:S(2)}) collective-permute-start(bf16[30,16,640]{2,1,0:T(8,128)(2,1)S(1)} %reshape.215.own_ref), channel_id=1, source_target_pairs={{0,1},{1,0},{2,3},{3,2},{4,5},{5,4},{6,7},{7,6},{8,9},{9,8},{10,11... | collective-permute-start | bytes 1843208 | tf_op jit(solution)/shard_map/ppermute | solution.py:171
  58.9 0.8 collective-permute-start.5
  59.7 3.6 %collective-permute-start.6 = (bf16[30,16,640]{2,1,0:T(8,128)(2,1)S(1)}, bf16[30,16,640]{2,1,0:T(8,128)(2,1)}, u32[]{:S(2)}, u32[]{:S(2)}) collective-permute-start(bf16[30,16,640]{2,1,0:T(8,128)(2,1)S(1)} %collective-permute-done.1.refs_1_), channel_id=1, source_target_pairs={{2,1},{1,2},{4,3},{3,4},{6,5},{5,6},{10,9},{9,10},{12,11},{11,12},... | collective-permute-start | bytes 1843208 | tf_op jit(solution)/shard_map/ppermute | solution.py:173
  65.3 1.5 %collective-permute-done.10.refs_3_ = bf16[20,16,640]{2,1,0:T(8,128)(2,1)S(1)} collective-permute-done((bf16[20,16,640]{2,1,0:T(8,128)(2,1)}, bf16[20,16,640]{2,1,0:T(8,128)(2,1)S(1)}, u32[]{:S(2)}, u32[]{:S(2)}) %collective-permute-start.10) | collective-permute-done | bytes 409632 | tf_op jit(solution)/shard_map/ppermute | solution.py:174
  67.5 8.1 %shard_map.39.refs_6_ = bf16[2,50,400,128]{3,2,1,0:T(8,128)(2,1)} custom-call(s32[2]{0:T(128)} %fusion.15.sel_ref, bf16[20,160,128]{2,1,0:T(8,128)(2,1)} %copy-done.1, bf16[20,16,640]{2,1,0:T(8,128)(2,1)} %copy-done.7, bf16[20,16,640]{2,1,0:T(8,128)(2,1)} %collective-permute-done.7.refs_1_, bf16[20,16,640]{2,1,0:T(8,128)(2,1)} %collective-permute-done.8.refs_2_, ...), custom_call_target="tpu_custom_call" | custom-call | flops 524288000 | bytes 12288000 | tf_op jit(solution)/shard_map/pallas_call | solution.py:149
  75.7 0.8 copy-done.5
  76.7 10.5 %shard_map.40 = bf16[2,50,400,128]{3,2,1,0:T(8,128)(2,1)} custom-call(s32[2]{0:T(128)} %fusion.15.sel_ref, bf16[30,160,128]{2,1,0:T(8,128)(2,1)} %copy-done, bf16[30,16,640]{2,1,0:T(8,128)(2,1)} %copy-done.5, bf16[30,16,640]{2,1,0:T(8,128)(2,1)} %copy-done.4, bf16[30,16,640]{2,1,0:T(8,128)(2,1)} %copy-done.3, ...), custom_call_target="tpu_custom_call", output_to_operand_aliasing={{}: (8, {})} | custom-call | flops 786432000 | bytes 18432000 | tf_op jit(solution)/shard_map/pallas_call | solution.py:149
  (48 shorter events, 4.2 us)
Async XLA Ops:
  0.0 1.8 %copy-start.2 = (bf16[160,4096]{1,0:T(8,128)(2,1)S(1)}, bf16[160,4096]{1,0:T(8,128)(2,1)}, u32[]{:S(2)}) copy-start(bf16[160,4096]{1,0:T(8,128)(2,1)} %param.3) | copy-start | bytes 3932164
  1.8 1.7 %copy-start.10 = (s32[160]{0:T(256)S(1)}, s32[160]{0:T(256)}, u32[]{:S(2)}) copy-start(s32[160]{0:T(256)} %param.4) | copy-start | bytes 1924
  2.1 7.9 %collective-permute-start = (bf16[160,512]{1,0:T(8,128)(2,1)S(1)}, bf16[160,512]{1,0:T(8,128)(2,1)S(1)}, u32[]{:S(2)}, u32[]{:S(2)}) collective-permute-start(bf16[160,512]{1,0:T(8,128)(2,1)S(1)} %slice.16), channel_id=1, source_target_pairs={{8,0},{16,8},{24,16},{9,1},{17,9},{25,17},{10,2},{18,10},{26,18},{... | collective-permute-start | bytes 491528 | tf_op jit(solution)/shard_map/ppermute | solution.py:23
  17.0 9.5 %all-to-all-start.1 = ((bf16[4,20,4,640]{3,2,1,0:T(4,128)(2,1)}), bf16[4,20,4,640]{3,2,1,0:T(4,128)(2,1)S(1)}, u32[]{:S(2)}, u32[]{:S(2)}) async-start(bf16[4,20,4,640]{3,2,1,0:T(4,128)(2,1)} %slice.18), calls=%async_computation.1 | async-start | bytes 819200 | tf_op jit(solution)/shard_map/all_to_all | solution.py:216
  26.5 10.7 %all-to-all-start = ((bf16[4,30,4,640]{3,2,1,0:T(4,128)(2,1)}), bf16[4,30,4,640]{3,2,1,0:T(4,128)(2,1)S(1)}, u32[]{:S(2)}, u32[]{:S(2)}) async-start(bf16[4,30,4,640]{3,2,1,0:T(4,128)(2,1)} %slice.17), calls=%async_computation | async-start | bytes 1228800 | tf_op jit(solution)/shard_map/all_to_all | solution.py:216
  30.3 17.2 %collective-permute-start.8 = (bf16[20,16,640]{2,1,0:T(8,128)(2,1)S(1)}, bf16[20,16,640]{2,1,0:T(8,128)(2,1)}, u32[]{:S(2)}, u32[]{:S(2)}) collective-permute-start(bf16[20,16,640]{2,1,0:T(8,128)(2,1)S(1)} %reshape.216.own_ref), channel_id=1, source_target_pairs={{3,1},{0,2},{5,3},{2,4},{7,5},{4,6},{11,9},{8,10},{13,11},{10,12},... | collective-permute-start | bytes 1228808 | tf_op jit(solution)/shard_map/ppermute | solution.py:170
  31.6 15.9 %collective-permute-start.7 = (bf16[20,16,640]{2,1,0:T(8,128)(2,1)S(1)}, bf16[20,16,640]{2,1,0:T(8,128)(2,1)}, u32[]{:S(2)}, u32[]{:S(2)}) collective-permute-start(bf16[20,16,640]{2,1,0:T(8,128)(2,1)S(1)} %reshape.216.own_ref), channel_id=1, source_target_pairs={{2,0},{4,2},{1,3},{6,4},{3,5},{5,7},{10,8},{12,10},{9,11},{14,12},... | collective-permute-start | bytes 1228808 | tf_op jit(solution)/shard_map/ppermute | solution.py:169
  37.6 27.1 %copy-start.11 = (s32[2,1]{0,1:T(1,128)S(1)}, s32[2,1]{0,1:T(1,128)}, u32[]{:S(2)}) copy-start(s32[2,1]{0,1:T(1,128)} %param.5) | copy-start | bytes 28
  37.6 18.1 %collective-permute-start.2 = (bf16[30,16,640]{2,1,0:T(8,128)(2,1)S(1)}, bf16[30,16,640]{2,1,0:T(8,128)(2,1)S(1)}, u32[]{:S(2)}, u32[]{:S(2)}) collective-permute-start(bf16[30,16,640]{2,1,0:T(8,128)(2,1)S(1)} %reshape.215.own_ref), channel_id=1, source_target_pairs={{3,1},{0,2},{5,3},{2,4},{7,5},{4,6},{11,9},{8,10},{13,11},{10,12},... | collective-permute-start | bytes 1843208 | tf_op jit(solution)/shard_map/ppermute | solution.py:170
  38.9 20.0 %collective-permute-start.1 = (bf16[30,16,640]{2,1,0:T(8,128)(2,1)S(1)}, bf16[30,16,640]{2,1,0:T(8,128)(2,1)S(1)}, u32[]{:S(2)}, u32[]{:S(2)}) collective-permute-start(bf16[30,16,640]{2,1,0:T(8,128)(2,1)S(1)} %reshape.215.own_ref), channel_id=1, source_target_pairs={{2,0},{4,2},{1,3},{6,4},{3,5},{5,7},{10,8},{12,10},{9,11},{14,12},... | collective-permute-start | bytes 1843208 | tf_op jit(solution)/shard_map/ppermute | solution.py:169
  42.9 16.8 %collective-permute-start.9 = (bf16[20,16,640]{2,1,0:T(8,128)(2,1)S(1)}, bf16[20,16,640]{2,1,0:T(8,128)(2,1)S(1)}, u32[]{:S(2)}, u32[]{:S(2)}) collective-permute-start(bf16[20,16,640]{2,1,0:T(8,128)(2,1)S(1)} %reshape.216.own_ref), channel_id=1, source_target_pairs={{0,1},{1,0},{2,3},{3,2},{4,5},{5,4},{6,7},{7,6},{8,9},{9,8},{10,11... | collective-permute-start | bytes 1228808 | tf_op jit(solution)/shard_map/ppermute | solution.py:171
  46.7 0.9 %copy-start.1 = (bf16[20,160,128]{2,1,0:T(8,128)(2,1)}, bf16[20,160,128]{2,1,0:T(8,128)(2,1)S(1)}, u32[]{:S(2)}) copy-start(bf16[20,160,128]{2,1,0:T(8,128)(2,1)S(1)} %shard_map.38.left_ref) | copy-start | bytes 2457604
  47.6 15.8 %collective-permute-start.11 = (bf16[20,16,640]{2,1,0:T(8,128)(2,1)}, bf16[20,16,640]{2,1,0:T(8,128)(2,1)S(1)}, u32[]{:S(2)}, u32[]{:S(2)}) collective-permute-start(bf16[20,16,640]{2,1,0:T(8,128)(2,1)} %collective-permute-done.8.refs_2_), channel_id=1, source_target_pairs={{0,1},{1,0},{2,3},{3,2},{4,5},{5,4},{6,7},{7,6},{8,9},{9,8},{10,11... | collective-permute-start | bytes 1228808 | tf_op jit(solution)/shard_map/ppermute | solution.py:175
  50.7 13.5 %collective-permute-start.12 = (bf16[20,16,640]{2,1,0:T(8,128)(2,1)}, bf16[20,16,640]{2,1,0:T(8,128)(2,1)}, u32[]{:S(2)}, u32[]{:S(2)}) collective-permute-start(bf16[20,16,640]{2,1,0:T(8,128)(2,1)} %collective-permute-done.7.refs_1_), channel_id=1, source_target_pairs={{2,1},{1,2},{4,3},{3,4},{6,5},{5,6},{10,9},{9,10},{12,11},{11,12},... | collective-permute-start | bytes 1228808 | tf_op jit(solution)/shard_map/ppermute | solution.py:173
  54.7 1.0 %copy-start = (bf16[30,160,128]{2,1,0:T(8,128)(2,1)}, bf16[30,160,128]{2,1,0:T(8,128)(2,1)S(1)}, u32[]{:S(2)}) copy-start(bf16[30,160,128]{2,1,0:T(8,128)(2,1)S(1)} %shard_map.37.left_ref) | copy-start | bytes 3686404
  55.7 19.9 %copy-start.3 = (bf16[30,16,640]{2,1,0:T(8,128)(2,1)}, bf16[30,16,640]{2,1,0:T(8,128)(2,1)S(1)}, u32[]{:S(2)}) copy-start(bf16[30,16,640]{2,1,0:T(8,128)(2,1)S(1)} %collective-permute-done.2.refs_2_) | copy-start | bytes 1843204
  55.7 19.9 %collective-permute-start.3 = (bf16[30,16,640]{2,1,0:T(8,128)(2,1)S(1)}, bf16[30,16,640]{2,1,0:T(8,128)(2,1)S(1)}, u32[]{:S(2)}, u32[]{:S(2)}) collective-permute-start(bf16[30,16,640]{2,1,0:T(8,128)(2,1)S(1)} %reshape.215.own_ref), channel_id=1, source_target_pairs={{0,1},{1,0},{2,3},{3,2},{4,5},{5,4},{6,7},{7,6},{8,9},{9,8},{10,11... | collective-permute-start | bytes 1843208 | tf_op jit(solution)/shard_map/ppermute | solution.py:171
  58.9 16.7 %copy-start.4 = (bf16[30,16,640]{2,1,0:T(8,128)(2,1)}, bf16[30,16,640]{2,1,0:T(8,128)(2,1)S(1)}, u32[]{:S(2)}) copy-start(bf16[30,16,640]{2,1,0:T(8,128)(2,1)S(1)} %collective-permute-done.1.refs_1_) | copy-start | bytes 1843204
  58.9 16.8 %collective-permute-start.5 = (bf16[30,16,640]{2,1,0:T(8,128)(2,1)S(1)}, bf16[30,16,640]{2,1,0:T(8,128)(2,1)S(1)}, u32[]{:S(2)}, u32[]{:S(2)}) collective-permute-start(bf16[30,16,640]{2,1,0:T(8,128)(2,1)S(1)} %collective-permute-done.2.refs_2_), channel_id=1, source_target_pairs={{0,1},{1,0},{2,3},{3,2},{4,5},{5,4},{6,7},{7,6},{8,9},{9,8},{10,11... | collective-permute-start | bytes 1843208 | tf_op jit(solution)/shard_map/ppermute | solution.py:175
  59.7 3.7 %copy-start.7 = (bf16[20,16,640]{2,1,0:T(8,128)(2,1)}, bf16[20,16,640]{2,1,0:T(8,128)(2,1)S(1)}, u32[]{:S(2)}) copy-start(bf16[20,16,640]{2,1,0:T(8,128)(2,1)S(1)} %collective-permute-done.9.refs_0_) | copy-start | bytes 1228804
  59.7 15.9 %collective-permute-start.6 = (bf16[30,16,640]{2,1,0:T(8,128)(2,1)S(1)}, bf16[30,16,640]{2,1,0:T(8,128)(2,1)}, u32[]{:S(2)}, u32[]{:S(2)}) collective-permute-start(bf16[30,16,640]{2,1,0:T(8,128)(2,1)S(1)} %collective-permute-done.1.refs_1_), channel_id=1, source_target_pairs={{2,1},{1,2},{4,3},{3,4},{6,5},{5,6},{10,9},{9,10},{12,11},{11,12},... | collective-permute-start | bytes 1843208 | tf_op jit(solution)/shard_map/ppermute | solution.py:173
  63.4 0.8 copy-start.8
  64.2 11.5 %collective-permute-start.4 = (bf16[30,16,640]{2,1,0:T(8,128)(2,1)S(1)}, bf16[30,16,640]{2,1,0:T(8,128)(2,1)}, u32[]{:S(2)}, u32[]{:S(2)}) collective-permute-start(bf16[30,16,640]{2,1,0:T(8,128)(2,1)S(1)} %collective-permute-done.1.refs_1_), channel_id=1, source_target_pairs={{0,1},{1,0},{2,3},{3,2},{4,5},{5,4},{6,7},{7,6},{8,9},{9,8},{10,11... | collective-permute-start | bytes 1843208 | tf_op jit(solution)/shard_map/ppermute | solution.py:174
  64.2 2.6 %collective-permute-start.10 = (bf16[20,16,640]{2,1,0:T(8,128)(2,1)}, bf16[20,16,640]{2,1,0:T(8,128)(2,1)S(1)}, u32[]{:S(2)}, u32[]{:S(2)}) collective-permute-start(bf16[20,16,640]{2,1,0:T(8,128)(2,1)} %collective-permute-done.7.refs_1_), channel_id=1, source_target_pairs={{0,1},{1,0},{2,3},{3,2},{4,5},{5,4},{6,7},{7,6},{8,9},{9,8},{10,11... | collective-permute-start | bytes 1228808 | tf_op jit(solution)/shard_map/ppermute | solution.py:174
  66.8 0.8 copy-start.9
  75.6 0.8 copy-start.5
  75.6 1.0 %copy-start.6 = (bf16[30,16,640]{2,1,0:T(8,128)(2,1)}, bf16[30,16,640]{2,1,0:T(8,128)(2,1)S(1)}, u32[]{:S(2)}) copy-start(bf16[30,16,640]{2,1,0:T(8,128)(2,1)S(1)} %collective-permute-done.5.refs_4_) | copy-start | bytes 1843204
